TPU v7x, 256 devices: a whole 4x4x8 slice. The times are simulated.
256 devices in a mesh: src: 4 (over z_hi, core), tile: 64 (over x, z_lo, y).
Axes of the slice: x: 4, y: 4, z: 8 (z_hi: 2, z_lo: 4; z = z_hi * 4 + z_lo), core: 2. Of those that a mesh axis runs over, the one named last changes fastest.
Arguments:
- mask_logits: float32 [32768, 512], P('tile'), may hold values from -10 to 10
- target: int32 [32768, 512], P('tile'), may hold values 0 or 1
- weights: float32 [64], P('src'), may hold values from 0.0078125 to 0.03125
- shifts: int32 [64, 2], P('src'), may hold values from -11 to 11
Outputs:
- mask_grad: float32 [32768, 512], P('tile')
- weight_grad: float32 [64], P('src')
- loss: float32 [], replicated
All inputs are finite; a program needn't handle non-finite values. No bound on the sum of `target` on one device may be relied on, other than what follows from the above.
Results may differ from a plain program's by a relative error of at most 0.0008.
The roundings to bfloat16 on the way count: a program that leaves them out, or rounds other values in their place, can miss the bound.
Values may be sent and summed in bfloat16 or wider, within the bound.
No kernel may reach another device: no remote copies, remote signals or barrier semaphores. Data moves between devices by JAX's collectives and lax.ppermute only.
A program may use at most 64 MiB of HBM per device.

v0:
```python
import jax
import jax.numpy as jnp
from jax import lax
from jax.sharding import PartitionSpec as P

FREQS = 64
RADIUS = 20
MARGIN = 64


STEEPNESS = 12.0
THRESHOLD = 0.2
HIGHEST = lax.Precision.HIGHEST


def extended(x, sides, width):
    for axis, dim in sides:
        peers, length = (lax.axis_size(axis), x.shape[dim])
        up = [(i, (i + 1) % peers) for i in range(peers - 1)]
        down = [(j, i) for i, j in up]
        last = lax.slice_in_dim(x, length - width, length, axis=dim)
        first = lax.slice_in_dim(x, 0, width, axis=dim)
        before = lax.ppermute(last, axis, up)
        after = lax.ppermute(first, axis, down)
        x = jnp.concatenate([before, x, after], axis=dim)
    return x


def sent_to_all(x, axis):
    peers = lax.axis_size(axis)
    return lax.all_to_all(jnp.broadcast_to(x[None], (peers, *x.shape)), axis, 0, 0, tiled=True)


def taken_together(x, axis):
    return sent_to_all(x, axis).sum(axis=0)


def in_one(arrays, axis):
    ends = [0]
    for a in arrays:
        ends.append(ends[-1] + a.size)
    total = taken_together(jnp.concatenate([a.ravel() for a in arrays]), axis)
    return tuple((total[b:e].reshape(a.shape) for a, b, e in zip(arrays, ends, ends[1:])))


def angles(length_used, offset, period):
    position = jnp.arange(length_used, dtype=jnp.int32)[:, None] + offset
    frequency = jnp.arange(FREQS, dtype=jnp.int32)[None, :] - FREQS // 2
    cycles = jnp.mod(position * frequency, period).astype(jnp.float32)
    angle_value = cycles * jnp.float32(2.0 * 3.141592653589793 / period)
    return (jnp.cos(angle_value), jnp.sin(angle_value))


def make_tables(tile_rows, frame_rows, col_count):
    column_cosine, column_sine = angles(col_count, 0, col_count)
    column_forward = jnp.concatenate([column_cosine, -column_sine], 1).astype(jnp.bfloat16)
    frame_cosine, frame_sine = angles(frame_rows, 0, frame_rows)
    row_forward = jnp.concatenate([frame_cosine.T, -frame_sine.T], 0).astype(jnp.bfloat16)
    owned_cosine, owned_sine = angles(tile_rows, MARGIN, frame_rows)
    row_inverse = (jnp.concatenate([owned_cosine, owned_sine], 1) / frame_rows).astype(jnp.bfloat16)
    cosine_scaled = column_cosine.T / col_count
    sine_scaled = column_sine.T / col_count
    upper_block = jnp.concatenate([cosine_scaled, sine_scaled], 1)
    lower_block = jnp.concatenate([-sine_scaled, cosine_scaled], 1)
    column_inverse = jnp.concatenate([upper_block, lower_block], 0).astype(jnp.bfloat16)
    return (column_forward, row_forward, row_inverse, column_inverse)


def pupil_masks(shifts):
    frequency = jnp.arange(FREQS, dtype=jnp.int32) - FREQS // 2
    offset_across = frequency[None, :, None] - shifts[:, 0][:, None, None]
    offset_along = frequency[None, None, :] - shifts[:, 1][:, None, None]
    inside = offset_across * offset_across + offset_along * offset_along <= RADIUS * RADIUS
    return inside.astype(jnp.float32)


def spectrum(framed, column_forward, row_forward):
    column_part = jnp.dot(framed, column_forward, preferred_element_type=jnp.float32).astype(
        jnp.bfloat16
    )
    product = jnp.dot(row_forward, column_part, preferred_element_type=jnp.float32)
    spectrum_real = (product[:FREQS, :FREQS] - product[FREQS:, FREQS:]).astype(jnp.bfloat16)
    spectrum_imag = (product[:FREQS, FREQS:] + product[FREQS:, :FREQS]).astype(jnp.bfloat16)
    return (spectrum_real, spectrum_imag)


def pupil_blocks(pupils, spectrum_real, spectrum_imag):
    pass_real = pupils * spectrum_real.astype(jnp.float32)
    pass_imag = pupils * spectrum_imag.astype(jnp.float32)
    upper_block = jnp.concatenate([pass_real, pass_imag], 2)
    lower_block = jnp.concatenate([-pass_imag, pass_real], 2)
    return jnp.concatenate([upper_block, lower_block], 1).astype(jnp.bfloat16)


def images(blocks, row_inverse, column_inverse):
    row_field = jnp.einsum(
        "pk,skj->spj", row_inverse, blocks, preferred_element_type=jnp.float32
    ).astype(jnp.bfloat16)
    source_count, tile_rows, doubled_freqs = row_field.shape
    fields = jnp.dot(
        row_field.reshape(source_count * tile_rows, doubled_freqs),
        column_inverse,
        preferred_element_type=jnp.float32,
    )
    return fields.reshape(source_count, tile_rows, -1)


def field_powers(fields):
    col_count = fields.shape[2] // 2
    return (
        fields[:, :, :col_count] * fields[:, :, :col_count]
        + fields[:, :, col_count:] * fields[:, :, col_count:]
    )


def apply_resist(intensity, target_rows):
    printed = jax.nn.sigmoid(STEEPNESS * (intensity - THRESHOLD))
    error_value = printed - target_rows.astype(jnp.float32)
    cotangent = 2.0 * STEEPNESS * error_value * printed * (1.0 - printed)
    return (cotangent, jnp.sum(error_value * error_value))


def frame_gradient(grad_real, grad_imag, column_forward, row_forward):
    upper_block = jnp.concatenate([grad_real, grad_imag], 1)
    lower_block = jnp.concatenate([grad_imag, -grad_real], 1)
    product_grad = jnp.concatenate([upper_block, lower_block], 0)
    column_grad = jnp.dot(row_forward.astype(jnp.float32).T, product_grad, precision=HIGHEST)
    return jnp.dot(column_grad, column_forward.astype(jnp.float32).T, precision=HIGHEST)


def on_device(mask_logits, target, weights, shifts):
    tile_rows, col_count = mask_logits.shape
    frame_rows = tile_rows + 2 * MARGIN
    column_forward, row_forward, row_inverse, column_inverse = make_tables(
        tile_rows, frame_rows, col_count
    )
    opening = jax.nn.sigmoid(mask_logits)
    framed = extended(opening.astype(jnp.bfloat16), (("tile", 0),), MARGIN)
    spectrum_real, spectrum_imag = spectrum(framed, column_forward, row_forward)
    pupils = pupil_masks(shifts)
    source_count = weights.shape[0]
    pupil_pairs = pupils.reshape(source_count // 2, 2, FREQS, FREQS)
    weight_pairs = weights.reshape(source_count // 2, 2)

    def forward_step(running, pair_item):
        pupil_pair, weight_pair = pair_item
        fields = images(
            pupil_blocks(pupil_pair, spectrum_real, spectrum_imag), row_inverse, column_inverse
        )
        return (running + jnp.sum(weight_pair[:, None, None] * field_powers(fields), 0), None)

    partial_image, unused = lax.scan(
        forward_step, jnp.zeros((tile_rows, col_count), jnp.float32), (pupil_pairs, weight_pairs)
    )
    intensity = lax.psum(partial_image, "src")
    cotangent, error_sum = apply_resist(intensity, target)
    doubled = jnp.concatenate([cotangent, cotangent], 1)

    def backward_step(running, pair_item):
        pupil_pair, weight_pair = pair_item
        fields = images(
            pupil_blocks(pupil_pair, spectrum_real, spectrum_imag), row_inverse, column_inverse
        )
        source_terms = jnp.sum(cotangent[None] * field_powers(fields), axis=(1, 2))
        scaling = (2.0 * weight_pair)[:, None, None] * doubled[None]
        field_grad = (scaling * fields).astype(jnp.bfloat16)
        row_grad = lax.dot_general(
            field_grad.reshape(-1, 2 * col_count),
            column_inverse,
            (((1,), (1,)), ((), ())),
            preferred_element_type=jnp.float32,
        )
        row_grad = row_grad.astype(jnp.bfloat16).reshape(2, tile_rows, -1)
        block_grad = jnp.einsum(
            "pk,spj->skj", row_inverse, row_grad, preferred_element_type=jnp.float32
        )
        grad_real = jnp.sum(
            pupil_pair * (block_grad[:, :FREQS, :FREQS] + block_grad[:, FREQS:, FREQS:]), 0
        )
        grad_imag = jnp.sum(
            pupil_pair * (block_grad[:, :FREQS, FREQS:] - block_grad[:, FREQS:, :FREQS]), 0
        )
        return ((running[0] + grad_real, running[1] + grad_imag), source_terms)

    zero_spectrum = jnp.zeros((FREQS, FREQS), jnp.float32)
    grads, pair_terms = lax.scan(
        backward_step, (zero_spectrum, zero_spectrum), (pupil_pairs, weight_pairs)
    )
    source_terms = pair_terms.reshape(source_count)
    grad_real, grad_imag = in_one((grads[0], grads[1]), "src")
    frame_grad = frame_gradient(grad_real, grad_imag, column_forward, row_forward)
    margin_grads = jnp.concatenate([frame_grad[:MARGIN], frame_grad[MARGIN + tile_rows :]], 0)
    beside_all = extended(margin_grads.astype(jnp.bfloat16), (("tile", 0),), MARGIN).astype(
        margin_grads.dtype
    )
    owned_grads = frame_grad[MARGIN : MARGIN + tile_rows]
    owned_grads = owned_grads.at[:MARGIN].add(beside_all[:MARGIN])
    owned_grads = owned_grads.at[tile_rows - MARGIN :].add(beside_all[3 * MARGIN :])
    mask_grad = owned_grads * opening * (1.0 - opening)
    pixel_total = tile_rows * col_count * lax.axis_size("tile")
    weight_sum, error_total = in_one((source_terms, error_sum), "tile")
    return (mask_grad, weight_sum / pixel_total, error_total / pixel_total)


def solution(mesh):
    placed = (P("tile", None), P("tile", None), P("src"), P("src", None))
    return jax.shard_map(
        on_device,
        mesh=mesh,
        in_specs=placed,
        out_specs=(P("tile", None), P("src"), P()),
        check_vma=False,
    )
```

profile of v0, /device:TPU:2, one launch (start us, length us, event | category | flops | bytes accessed | tf_op | source)
XLA Modules:
  0.0 319.9 jit_solution(2772433926593908255)
XLA Ops:
  8.8 3.5 %collective-permute-start = (bf16[64,512]{1,0:T(8,128)(2,1)S(1)}, bf16[64,512]{1,0:T(8,128)(2,1)S(1)}, u32[]{:S(2)}, u32[]{:S(2)}) collective-permute-start(bf16[64,512]{1,0:T(8,128)(2,1)S(1)} %get-tuple-element.421), channel_id=1, source_target_pairs={{0,1},{1,2},{2,3},{3,4},{4,5},{5,6},{6,7},{7,8},{8,9},{9,10},{10,1... | collective-permute-start | bytes 196616 | tf_op jit(solution)/shard_map/ppermute | solution.py:23
  12.2 7.4 %collective-permute-start.1 = (bf16[64,512]{1,0:T(8,128)(2,1)S(1)}, bf16[64,512]{1,0:T(8,128)(2,1)S(1)}, u32[]{:S(2)}, u32[]{:S(2)}) collective-permute-start(bf16[64,512]{1,0:T(8,128)(2,1)S(1)} %get-tuple-element.422), channel_id=1, source_target_pairs={{1,0},{2,1},{3,2},{4,3},{5,4},{6,5},{7,6},{8,7},{9,8},{10,9},{11,1... | collective-permute-start | bytes 196616 | tf_op jit(solution)/shard_map/ppermute | solution.py:24
  23.9 50.4 %while.28 = (s32[]{:T(128)}, f32[512,512]{1,0:T(8,128)S(1)}, f32[8,2]{1,0:T(8,128)S(1)}, f32[8,2,64,64]{2,3,1,0:T(8,128)S(1)}, bf16[64,64]{0,1:T(8,128)(2,1)S(1)...) while((s32[]{:T(128)}, f32[512,512]{1,0:T(8,128)S(1)}, ...), condition=%wide.region_2.3_spmd.clone, body=%wide.region_0.2_spmd.clone.sunk | while | flops 305324032 | bytes 13189263 | solution.py:152
  26.9 2.9 fusion.146
  33.2 2.9 fusion.146
  39.5 2.9 fusion.146
  45.8 2.9 fusion.146
  52.1 2.9 fusion.146
  58.4 2.9 fusion.146
  75.3 71.9 %all-reduce.2.cloned.1.call-done = f32[512,512]{1,0:T(8,128)} async-done(((f32[512,512]{1,0:T(8,128)}), f32[512,512]{1,0:T(8,128)}) %all-reduce.2.cloned.1.call-update) | async-done | bytes 1048592 | tf_op jit(solution)/shard_map/psum | solution.py:155
  151.5 107.0 %while.29 = (s32[]{:T(128)}, f32[64,64]{0,1:T(8,128)}, f32[64,64]{0,1:T(8,128)}, f32[8,2]{1,0:T(8,128)}, f32[8,2,64,64]{2,3,1,0:T(8,128)S(1)}, /*index=5*/f32[8,...) while((s32[]{:T(128)}, f32[64,64]{0,1:T(8,128)}, ...), condition=%wide.region_8.9_spmd.clone, body=%wide.region_4.8_spmd.clone.sunk | while | flops 610385920 | bytes 19841912 | solution.py:186
  152.8 4.6 %multiply_convert_fusion.3 = (bf16[2,512,1024]{2,1,0:T(8,128)(2,1)S(1)}, f32[2,512,1024]{2,1,0:T(8,128)}) fusion(f32[512,1024]{1,0:T(8,128)} %get-tuple-element.650, f32[2]{0:T(128)} %multiply_bitcast_fusion.2, bf16[128,1024]{1,0:T(8,128)(2,1)S(1)} %get-tuple-element.654, bf16[512,128]{1,0:T(8,128)(2,1)S(1)} %get-tuple-element.653, ...), kind=kOutput, calls=%fused_computation.25.clone.1 | convolution fusion | flops 305528832 | bytes 8830984 | tf_op jit(solution)/shard_map/while/body/eval_jaxpr/dot_general | solution.py:100
  165.5 4.6 %multiply_convert_fusion.3 = (bf16[2,512,1024]{2,1,0:T(8,128)(2,1)S(1)}, f32[2,512,1024]{2,1,0:T(8,128)}) fusion(f32[512,1024]{1,0:T(8,128)} %get-tuple-element.650, f32[2]{0:T(128)} %multiply_bitcast_fusion.2, bf16[128,1024]{1,0:T(8,128)(2,1)S(1)} %get-tuple-element.654, bf16[512,128]{1,0:T(8,128)(2,1)S(1)} %get-tuple-element.653, ...), kind=kOutput, calls=%fused_computation.25.clone.1 | convolution fusion | flops 305528832 | bytes 8830984 | tf_op jit(solution)/shard_map/while/body/eval_jaxpr/dot_general | solution.py:100
  179.0 4.6 %multiply_convert_fusion.3 = (bf16[2,512,1024]{2,1,0:T(8,128)(2,1)S(1)}, f32[2,512,1024]{2,1,0:T(8,128)}) fusion(f32[512,1024]{1,0:T(8,128)} %get-tuple-element.650, f32[2]{0:T(128)} %multiply_bitcast_fusion.2, bf16[128,1024]{1,0:T(8,128)(2,1)S(1)} %get-tuple-element.654, bf16[512,128]{1,0:T(8,128)(2,1)S(1)} %get-tuple-element.653, ...), kind=kOutput, calls=%fused_computation.25.clone.1 | convolution fusion | flops 305528832 | bytes 8830984 | tf_op jit(solution)/shard_map/while/body/eval_jaxpr/dot_general | solution.py:100
  192.5 4.6 %multiply_convert_fusion.3 = (bf16[2,512,1024]{2,1,0:T(8,128)(2,1)S(1)}, f32[2,512,1024]{2,1,0:T(8,128)}) fusion(f32[512,1024]{1,0:T(8,128)} %get-tuple-element.650, f32[2]{0:T(128)} %multiply_bitcast_fusion.2, bf16[128,1024]{1,0:T(8,128)(2,1)S(1)} %get-tuple-element.654, bf16[512,128]{1,0:T(8,128)(2,1)S(1)} %get-tuple-element.653, ...), kind=kOutput, calls=%fused_computation.25.clone.1 | convolution fusion | flops 305528832 | bytes 8830984 | tf_op jit(solution)/shard_map/while/body/eval_jaxpr/dot_general | solution.py:100
  205.9 4.6 %multiply_convert_fusion.3 = (bf16[2,512,1024]{2,1,0:T(8,128)(2,1)S(1)}, f32[2,512,1024]{2,1,0:T(8,128)}) fusion(f32[512,1024]{1,0:T(8,128)} %get-tuple-element.650, f32[2]{0:T(128)} %multiply_bitcast_fusion.2, bf16[128,1024]{1,0:T(8,128)(2,1)S(1)} %get-tuple-element.654, bf16[512,128]{1,0:T(8,128)(2,1)S(1)} %get-tuple-element.653, ...), kind=kOutput, calls=%fused_computation.25.clone.1 | convolution fusion | flops 305528832 | bytes 8830984 | tf_op jit(solution)/shard_map/while/body/eval_jaxpr/dot_general | solution.py:100
  219.4 4.6 %multiply_convert_fusion.3 = (bf16[2,512,1024]{2,1,0:T(8,128)(2,1)S(1)}, f32[2,512,1024]{2,1,0:T(8,128)}) fusion(f32[512,1024]{1,0:T(8,128)} %get-tuple-element.650, f32[2]{0:T(128)} %multiply_bitcast_fusion.2, bf16[128,1024]{1,0:T(8,128)(2,1)S(1)} %get-tuple-element.654, bf16[512,128]{1,0:T(8,128)(2,1)S(1)} %get-tuple-element.653, ...), kind=kOutput, calls=%fused_computation.25.clone.1 | convolution fusion | flops 305528832 | bytes 8830984 | tf_op jit(solution)/shard_map/while/body/eval_jaxpr/dot_general | solution.py:100
  232.9 4.6 %multiply_convert_fusion.3 = (bf16[2,512,1024]{2,1,0:T(8,128)(2,1)S(1)}, f32[2,512,1024]{2,1,0:T(8,128)}) fusion(f32[512,1024]{1,0:T(8,128)} %get-tuple-element.650, f32[2]{0:T(128)} %multiply_bitcast_fusion.2, bf16[128,1024]{1,0:T(8,128)(2,1)S(1)} %get-tuple-element.654, bf16[512,128]{1,0:T(8,128)(2,1)S(1)} %get-tuple-element.653, ...), kind=kOutput, calls=%fused_computation.25.clone.1 | convolution fusion | flops 305528832 | bytes 8830984 | tf_op jit(solution)/shard_map/while/body/eval_jaxpr/dot_general | solution.py:100
  246.4 4.6 %multiply_convert_fusion.3 = (bf16[2,512,1024]{2,1,0:T(8,128)(2,1)S(1)}, f32[2,512,1024]{2,1,0:T(8,128)}) fusion(f32[512,1024]{1,0:T(8,128)} %get-tuple-element.650, f32[2]{0:T(128)} %multiply_bitcast_fusion.2, bf16[128,1024]{1,0:T(8,128)(2,1)S(1)} %get-tuple-element.654, bf16[512,128]{1,0:T(8,128)(2,1)S(1)} %get-tuple-element.653, ...), kind=kOutput, calls=%fused_computation.25.clone.1 | convolution fusion | flops 305528832 | bytes 8830984 | tf_op jit(solution)/shard_map/while/body/eval_jaxpr/dot_general | solution.py:100
  262.4 8.5 %all-to-all-start.1 = ((f32[64,1,17]{2,1,0:T(1,128)}), f32[64,1,17]{2,1,0:T(1,128)S(1)}, u32[]{:S(2)}, u32[]{:S(2)}) async-start(f32[64,1,17]{2,1,0:T(1,128)} %broadcast_in_dim.17), calls=%async_computation.1 | async-start | bytes 65536 | tf_op jit(solution)/shard_map/all_to_all | solution.py:31
  270.9 9.1 %all-to-all-done.1 = f32[64,1,17]{2,1,0:T(1,128)S(1)} async-done(((f32[64,1,17]{2,1,0:T(1,128)}), f32[64,1,17]{2,1,0:T(1,128)S(1)}, u32[]{:S(2)}, u32[]{:S(2)}) %all-to-all-start.1) | async-done | bytes 4384 | tf_op jit(solution)/shard_map/all_to_all | solution.py:31
  280.7 5.5 %all-to-all-start = ((f32[4,1,8192]{2,1,0:T(1,128)}), f32[4,1,8192]{2,1,0:T(1,128)S(1)}, u32[]{:S(2)}, u32[]{:S(2)}) async-start(f32[4,1,8192]{2,1,0:T(1,128)} %broadcast_in_dim.16), calls=%async_computation | async-start | bytes 262144 | tf_op jit(solution)/shard_map/all_to_all | solution.py:31
  286.3 8.4 %all-to-all-done = f32[4,1,8192]{2,1,0:T(1,128)S(1)} async-done(((f32[4,1,8192]{2,1,0:T(1,128)}), f32[4,1,8192]{2,1,0:T(1,128)S(1)}, u32[]{:S(2)}, u32[]{:S(2)}) %all-to-all-start) | async-done | bytes 131104 | tf_op jit(solution)/shard_map/all_to_all | solution.py:31
  300.6 8.2 %collective-permute-start.3 = (bf16[64,512]{1,0:T(8,128)(2,1)S(1)}, bf16[64,512]{1,0:T(8,128)(2,1)S(1)}, u32[]{:S(2)}, u32[]{:S(2)}) collective-permute-start(bf16[64,512]{1,0:T(8,128)(2,1)S(1)} %get-tuple-element.420), channel_id=1, source_target_pairs={{1,0},{2,1},{3,2},{4,3},{5,4},{6,5},{7,6},{8,7},{9,8},{10,9},{11,1... | collective-permute-start | bytes 196616 | tf_op jit(solution)/shard_map/ppermute | solution.py:24
  (299 shorter events, 125.8 us)
Async XLA Ops:
  7.2 15.2 %copy-start.12 = (s32[16,2]{0,1:T(2,128)S(1)}, s32[16,2]{0,1:T(2,128)}, u32[]{:S(2)}) copy-start(s32[16,2]{0,1:T(2,128)} %param.15) | copy-start | bytes 388
  7.2 15.4 %copy-start.13 = (f32[16]{0:T(128)S(1)}, f32[16]{0:T(128)}, u32[]{:S(2)}) copy-start(f32[16]{0:T(128)} %param.14) | copy-start | bytes 196
  7.2 140.1 %all-reduce.2.cloned.1.call-start = ((), (), s32[]{:S(2)}) async-start(), calls=%async_computation.2 | async-start | bytes 2097152 | tf_op jit(solution)/shard_map/psum | solution.py:155
  8.8 14.2 %collective-permute-start = (bf16[64,512]{1,0:T(8,128)(2,1)S(1)}, bf16[64,512]{1,0:T(8,128)(2,1)S(1)}, u32[]{:S(2)}, u32[]{:S(2)}) collective-permute-start(bf16[64,512]{1,0:T(8,128)(2,1)S(1)} %get-tuple-element.421), channel_id=1, source_target_pairs={{0,1},{1,2},{2,3},{3,4},{4,5},{5,6},{6,7},{7,8},{8,9},{9,10},{10,1... | collective-permute-start | bytes 196616 | tf_op jit(solution)/shard_map/ppermute | solution.py:23
  12.2 10.8 %collective-permute-start.1 = (bf16[64,512]{1,0:T(8,128)(2,1)S(1)}, bf16[64,512]{1,0:T(8,128)(2,1)S(1)}, u32[]{:S(2)}, u32[]{:S(2)}) collective-permute-start(bf16[64,512]{1,0:T(8,128)(2,1)S(1)} %get-tuple-element.422), channel_id=1, source_target_pairs={{1,0},{2,1},{3,2},{4,3},{5,4},{6,5},{7,6},{8,7},{9,8},{10,9},{11,1... | collective-permute-start | bytes 196616 | tf_op jit(solution)/shard_map/ppermute | solution.py:24
  160.0 4.1 %copy-start.5 = (bf16[64,64]{0,1:T(8,128)(2,1)S(1)}, bf16[64,64]{0,1:T(8,128)(2,1)}, u32[]{:S(2)}) copy-start(bf16[64,64]{0,1:T(8,128)(2,1)} %copy-done.4) | copy-start | bytes 24580 | tf_op jit(solution)/shard_map/while
  160.0 4.1 %copy-start.11 = (f32[8,2]{1,0:T(8,128)S(1)}, f32[8,2]{1,0:T(8,128)}, u32[]{:S(2)}) copy-start(f32[8,2]{1,0:T(8,128)} %copy-done.10) | copy-start | bytes 196 | tf_op jit(solution)/shard_map/while
  173.5 4.1 %copy-start.5 = (bf16[64,64]{0,1:T(8,128)(2,1)S(1)}, bf16[64,64]{0,1:T(8,128)(2,1)}, u32[]{:S(2)}) copy-start(bf16[64,64]{0,1:T(8,128)(2,1)} %copy-done.4) | copy-start | bytes 24580 | tf_op jit(solution)/shard_map/while
  173.5 4.1 %copy-start.11 = (f32[8,2]{1,0:T(8,128)S(1)}, f32[8,2]{1,0:T(8,128)}, u32[]{:S(2)}) copy-start(f32[8,2]{1,0:T(8,128)} %copy-done.10) | copy-start | bytes 196 | tf_op jit(solution)/shard_map/while
  186.9 4.1 %copy-start.5 = (bf16[64,64]{0,1:T(8,128)(2,1)S(1)}, bf16[64,64]{0,1:T(8,128)(2,1)}, u32[]{:S(2)}) copy-start(bf16[64,64]{0,1:T(8,128)(2,1)} %copy-done.4) | copy-start | bytes 24580 | tf_op jit(solution)/shard_map/while
  187.0 4.1 %copy-start.11 = (f32[8,2]{1,0:T(8,128)S(1)}, f32[8,2]{1,0:T(8,128)}, u32[]{:S(2)}) copy-start(f32[8,2]{1,0:T(8,128)} %copy-done.10) | copy-start | bytes 196 | tf_op jit(solution)/shard_map/while
  200.4 4.1 %copy-start.5 = (bf16[64,64]{0,1:T(8,128)(2,1)S(1)}, bf16[64,64]{0,1:T(8,128)(2,1)}, u32[]{:S(2)}) copy-start(bf16[64,64]{0,1:T(8,128)(2,1)} %copy-done.4) | copy-start | bytes 24580 | tf_op jit(solution)/shard_map/while
  200.4 4.1 %copy-start.11 = (f32[8,2]{1,0:T(8,128)S(1)}, f32[8,2]{1,0:T(8,128)}, u32[]{:S(2)}) copy-start(f32[8,2]{1,0:T(8,128)} %copy-done.10) | copy-start | bytes 196 | tf_op jit(solution)/shard_map/while
  213.9 4.1 %copy-start.5 = (bf16[64,64]{0,1:T(8,128)(2,1)S(1)}, bf16[64,64]{0,1:T(8,128)(2,1)}, u32[]{:S(2)}) copy-start(bf16[64,64]{0,1:T(8,128)(2,1)} %copy-done.4) | copy-start | bytes 24580 | tf_op jit(solution)/shard_map/while
  213.9 4.1 %copy-start.11 = (f32[8,2]{1,0:T(8,128)S(1)}, f32[8,2]{1,0:T(8,128)}, u32[]{:S(2)}) copy-start(f32[8,2]{1,0:T(8,128)} %copy-done.10) | copy-start | bytes 196 | tf_op jit(solution)/shard_map/while
  227.4 4.1 %copy-start.5 = (bf16[64,64]{0,1:T(8,128)(2,1)S(1)}, bf16[64,64]{0,1:T(8,128)(2,1)}, u32[]{:S(2)}) copy-start(bf16[64,64]{0,1:T(8,128)(2,1)} %copy-done.4) | copy-start | bytes 24580 | tf_op jit(solution)/shard_map/while
  227.4 4.1 %copy-start.11 = (f32[8,2]{1,0:T(8,128)S(1)}, f32[8,2]{1,0:T(8,128)}, u32[]{:S(2)}) copy-start(f32[8,2]{1,0:T(8,128)} %copy-done.10) | copy-start | bytes 196 | tf_op jit(solution)/shard_map/while
  240.9 4.1 %copy-start.11 = (f32[8,2]{1,0:T(8,128)S(1)}, f32[8,2]{1,0:T(8,128)}, u32[]{:S(2)}) copy-start(f32[8,2]{1,0:T(8,128)} %copy-done.10) | copy-start | bytes 196 | tf_op jit(solution)/shard_map/while
  254.4 4.1 %copy-start.11 = (f32[8,2]{1,0:T(8,128)S(1)}, f32[8,2]{1,0:T(8,128)}, u32[]{:S(2)}) copy-start(f32[8,2]{1,0:T(8,128)} %copy-done.10) | copy-start | bytes 196 | tf_op jit(solution)/shard_map/while
  262.4 17.6 %all-to-all-start.1 = ((f32[64,1,17]{2,1,0:T(1,128)}), f32[64,1,17]{2,1,0:T(1,128)S(1)}, u32[]{:S(2)}, u32[]{:S(2)}) async-start(f32[64,1,17]{2,1,0:T(1,128)} %broadcast_in_dim.17), calls=%async_computation.1 | async-start | bytes 65536 | tf_op jit(solution)/shard_map/all_to_all | solution.py:31
  280.7 14.0 %all-to-all-start = ((f32[4,1,8192]{2,1,0:T(1,128)}), f32[4,1,8192]{2,1,0:T(1,128)S(1)}, u32[]{:S(2)}, u32[]{:S(2)}) async-start(f32[4,1,8192]{2,1,0:T(1,128)} %broadcast_in_dim.16), calls=%async_computation | async-start | bytes 262144 | tf_op jit(solution)/shard_map/all_to_all | solution.py:31
  297.9 12.8 %copy-start.3 = (f32[512,512]{1,0:T(8,128)S(1)}, f32[512,512]{1,0:T(8,128)}, u32[]{:S(2)}) copy-start(f32[512,512]{1,0:T(8,128)} %param.12) | copy-start | bytes 3145732
  297.9 12.6 %collective-permute-start.2 = (bf16[64,512]{1,0:T(8,128)(2,1)S(1)}, bf16[64,512]{1,0:T(8,128)(2,1)S(1)}, u32[]{:S(2)}, u32[]{:S(2)}) collective-permute-start(bf16[64,512]{1,0:T(8,128)(2,1)S(1)} %get-tuple-element.419), channel_id=1, source_target_pairs={{0,1},{1,2},{2,3},{3,4},{4,5},{5,6},{6,7},{7,8},{8,9},{9,10},{10,1... | collective-permute-start | bytes 196616 | tf_op jit(solution)/shard_map/ppermute | solution.py:23
  300.6 10.1 %collective-permute-start.3 = (bf16[64,512]{1,0:T(8,128)(2,1)S(1)}, bf16[64,512]{1,0:T(8,128)(2,1)S(1)}, u32[]{:S(2)}, u32[]{:S(2)}) collective-permute-start(bf16[64,512]{1,0:T(8,128)(2,1)S(1)} %get-tuple-element.420), channel_id=1, source_target_pairs={{1,0},{2,1},{3,2},{4,3},{5,4},{6,5},{7,6},{8,7},{9,8},{10,9},{11,1... | collective-permute-start | bytes 196616 | tf_op jit(solution)/shard_map/ppermute | solution.py:24
  (39 other events, 83.9 us)
Sparse Core Ops, SparseCore 0:
  75.4 71.7 all-reduce.1
where the time goes:
time: 322 us; the launch traced here: 320 us
  waiting for transfers between devices  89.5 us (28%)
  other arithmetic  89.4 us (28%)
  matrix products  71.2 us (22%)
  starting transfers between devices  35.7 us (11%)
  local copies, waits for them, and re-layouts  16.9 us (5%)
  between operations  16.2 us (5%)
    psum x1, waiting for transfers between devices, on_device(): intensity = lax.psum(partial_image, 'src')  71.9 us
    dot_general x16, matrix products, images(): jnp.dot(row_field.reshape(source_count * tile_rows, doubled_freqs), colum...  60.1 us
    reduce_sum x8, other arithmetic, forward_step(): jnp.sum(weight_pair[:, None, None] * field_powers(fields), 0)  23.5 us
    reduce_sum x8, other arithmetic, backward_step(): source_terms = jnp.sum(cotangent[None] * field_powers(fields), axis=(1, 2))  22.5 us
    all_to_all x2, waiting for transfers between devices, sent_to_all(): lax.all_to_all(jnp.broadcast_to(x[None], (peers, *x.shape)), axis, 0, 0,...  17.5 us
    ppermute x2, starting transfers between devices, extended(): after = lax.ppermute(first, axis, down)  15.6 us
    all_to_all x2, starting transfers between devices, sent_to_all(): lax.all_to_all(jnp.broadcast_to(x[None], (peers, *x.shape)), axis, 0, 0,...  14 us
    add x8, other arithmetic, backward_step(): return ((running[0] + grad_real, running[1] + grad_imag), source_terms)  10.6 us
  transfers between devices with their start and end apart: 7, of which 3 were waited for; matrix products, arithmetic and copies ran while one was open for 1% of the time, Pallas kernels for 0%

commit v1 on v0

v1 whole, which is shorter than its diff:
```python
import numpy as np
import jax
import jax.numpy as jnp
from jax import lax
from jax.experimental import pallas as pl
from jax.experimental.pallas import tpu as pltpu
from jax.sharding import PartitionSpec as P

FREQS = 64
RADIUS = 20
MARGIN = 64
COLS = 512
TILE_ROWS = 512
FRAME = 640
SOURCES = 64
GROUPS = 4
PER_GROUP = SOURCES // GROUPS
ROWS = TILE_ROWS // GROUPS
STEEPNESS = 12.0
THRESHOLD = 0.2
STEP = 4
F32 = jnp.float32
BF16 = jnp.bfloat16


def angles(length_used, offset, period):
    position = np.arange(length_used, dtype=np.int32)[:, None] + offset
    frequency = np.arange(FREQS, dtype=np.int32)[None, :] - FREQS // 2
    cycles = np.mod(position * frequency, period).astype(np.float32)
    angle_value = (cycles * np.float32(2.0 * 3.141592653589793 / period)).astype(np.float64)
    return np.cos(angle_value).astype(np.float32), np.sin(angle_value).astype(np.float32)


def make_tables():
    column_cosine, column_sine = angles(COLS, 0, COLS)
    column_forward = np.concatenate([column_cosine, -column_sine], 1)
    frame_cosine, frame_sine = angles(FRAME, 0, FRAME)
    row_forward = np.concatenate([frame_cosine.T, -frame_sine.T], 0)
    owned_cosine, owned_sine = angles(TILE_ROWS, MARGIN, FRAME)
    row_inverse = np.concatenate([owned_cosine, owned_sine], 1) / np.float32(FRAME)
    cosine_scaled = column_cosine.T / np.float32(COLS)
    sine_scaled = column_sine.T / np.float32(COLS)
    upper_block = np.concatenate([cosine_scaled, sine_scaled], 1)
    lower_block = np.concatenate([-sine_scaled, cosine_scaled], 1)
    column_inverse = np.concatenate([upper_block, lower_block], 0)
    chunked = column_inverse.reshape(2 * FREQS, 2, COLS // 128, 128).transpose(0, 2, 1, 3)
    chunked = chunked.reshape(2 * FREQS, 2 * COLS)
    rounded = lambda a: np.ascontiguousarray(a).astype(BF16)
    return [rounded(a) for a in (column_forward, row_forward, row_inverse, chunked)]


COLUMN_FORWARD, ROW_FORWARD, ROW_INVERSE, COLUMN_INVERSE = make_tables()


def dot(a, b):
    return jnp.dot(a, b, preferred_element_type=F32)


def halves_sign(rows, left, right):
    lane = lax.broadcasted_iota(jnp.int32, (rows, 128), 1)
    return jnp.where(lane < FREQS, F32(left), F32(right))


def column_kernel(logits_ref, table_ref, out_ref, first_ref, last_ref):
    opening = jax.nn.sigmoid(logits_ref[...]).astype(BF16)
    out = dot(opening, table_ref[...]).astype(BF16)
    out_ref[...] = out
    first_ref[...] = out[:MARGIN]
    last_ref[...] = out[TILE_ROWS - MARGIN:]


def column_spectrum(mask_logits):
    shapes = [(TILE_ROWS, 128), (MARGIN, 128), (MARGIN, 128)]
    return pl.pallas_call(
        column_kernel,
        out_shape=[jax.ShapeDtypeStruct(s, BF16) for s in shapes],
        name="column_spectrum",
    )(mask_logits, jnp.asarray(COLUMN_FORWARD))


def pupil(scalars_ref, s):
    group, i = s // PER_GROUP, s % PER_GROUP
    across = scalars_ref[group, PER_GROUP + i]
    along = scalars_ref[group, 2 * PER_GROUP + i]
    row = lax.broadcasted_iota(jnp.int32, (FREQS, 128), 0) - FREQS // 2
    lane = jnp.bitwise_and(lax.broadcasted_iota(jnp.int32, (FREQS, 128), 1), FREQS - 1) - FREQS // 2
    row, lane = row.astype(F32) - across, lane.astype(F32) - along
    return row * row + lane * lane <= F32(RADIUS * RADIUS)


def image_kernel(group_ref, scalars_ref, own_ref, before_ref, after_ref, target_ref, row_forward_ref,
                 row_inverse_ref, row_inverse_t_ref, inverse_ref, inverse_t_ref, out_ref,
                 fields_ref, row_field_ref, intensity_ref, cotangent_ref, spectra_ref, terms_ref, grad_ref):
    frame = jnp.concatenate([before_ref[...], own_ref[...], after_ref[...]], 0)
    product = dot(row_forward_ref[...], frame)
    swapped = pltpu.roll(product[FREQS:], FREQS, 1)
    spectrum = (product[:FREQS] + halves_sign(FREQS, -1.0, 1.0) * swapped).astype(BF16).astype(F32)
    spectra_ref[:FREQS] = spectrum
    spectra_ref[FREQS:] = pltpu.roll(spectrum, FREQS, 1) * halves_sign(FREQS, -1.0, 1.0)
    intensity_ref[...] = jnp.zeros_like(intensity_ref)
    spectra = spectra_ref[...]

    @pl.loop(0, SOURCES // STEP)
    def _(step):
        blocks = []
        for j in range(STEP):
            inside = pupil(scalars_ref, step * STEP + j)
            inside = jnp.concatenate([inside, inside], 0)
            blocks.append(jnp.where(inside, spectra, F32(0)).astype(BF16))
        row_field = dot(row_inverse_ref[...], jnp.concatenate(blocks, 1)).astype(BF16)
        for j in range(STEP):
            start = pl.multiple_of((step * STEP + j) * ROWS, ROWS)
            row_field_ref[pl.ds(start, ROWS), :] = row_field[:, 128 * j:128 * (j + 1)]

    def weight(s):
        return scalars_ref[s // PER_GROUP, s % PER_GROUP]

    @pl.loop(0, SOURCES // STEP)
    def _(step):
        start = pl.multiple_of(step * (STEP * ROWS), STEP * ROWS)
        row_field = row_field_ref[pl.ds(start, STEP * ROWS), :]
        for n in range(4):
            fields = dot(row_field, inverse_ref[:, 256 * n:256 * (n + 1)])
            fields_ref[pl.ds(start, STEP * ROWS), 256 * n:256 * (n + 1)] = fields
            power = fields[:, :128] * fields[:, :128] + fields[:, 128:] * fields[:, 128:]
            total = weight(step * STEP) * power[:ROWS]
            for j in range(1, STEP):
                total = total + weight(step * STEP + j) * power[j * ROWS:(j + 1) * ROWS]
            intensity_ref[:, 128 * n:128 * (n + 1)] += total

    printed = jax.nn.sigmoid(F32(STEEPNESS) * (intensity_ref[...] - F32(THRESHOLD)))
    error_value = printed - target_ref[...].astype(F32)
    cotangent_ref[...] = F32(2.0 * STEEPNESS) * error_value * printed * (F32(1.0) - printed)
    error_rows = jnp.sum(error_value * error_value, 0, keepdims=True)
    error_lanes = (error_rows[:, :128] + error_rows[:, 128:256]) + (error_rows[:, 256:384] + error_rows[:, 384:])
    error_sum = jnp.sum(error_lanes, 1, keepdims=True)
    grad_ref[...] = jnp.zeros_like(grad_ref)

    @pl.loop(0, SOURCES // STEP)
    def _(step):
        start = pl.multiple_of(step * (STEP * ROWS), STEP * ROWS)
        row_grad = None
        for n in range(4):
            cot = cotangent_ref[:, 128 * n:128 * (n + 1)]
            parts = []
            for j in range(STEP):
                scaling = (F32(2.0) * weight(step * STEP + j)) * cot
                at = pl.multiple_of(start + j * ROWS, ROWS)
                fields = fields_ref[pl.ds(at, ROWS), 256 * n:256 * (n + 1)]
                parts.append((jnp.concatenate([scaling, scaling], 1) * fields).astype(BF16))
            part = dot(jnp.concatenate(parts, 0), inverse_t_ref[256 * n:256 * (n + 1), :])
            row_grad = part if row_grad is None else row_grad + part
        row_field = row_field_ref[pl.ds(start, STEP * ROWS), :].astype(F32)
        terms = row_grad * row_field
        rounded = row_grad.astype(BF16)
        for j in range(STEP):
            terms_ref[pl.ds(step * STEP + j, 1), :] = jnp.sum(terms[j * ROWS:(j + 1) * ROWS], 0, keepdims=True)
        block_grad = dot(row_inverse_t_ref[...],
                         jnp.concatenate([rounded[j * ROWS:(j + 1) * ROWS] for j in range(STEP)], 1))
        total = jnp.zeros((2 * FREQS, 128), F32)
        for j in range(STEP):
            inside = pupil(scalars_ref, step * STEP + j)
            inside = jnp.concatenate([inside, inside], 0)
            total = total + jnp.where(inside, block_grad[:, 128 * j:128 * (j + 1)], F32(0))
        grad_ref[...] += total

    grads = grad_ref[...]
    out_ref[:FREQS] = grads[:FREQS] + halves_sign(FREQS, 1.0, -1.0) * pltpu.roll(grads[FREQS:], FREQS, 1)
    term = jnp.sum(terms_ref[...], 1, keepdims=True)
    row = lax.broadcasted_iota(jnp.int32, (SOURCES, 128), 0)
    lane = lax.broadcasted_iota(jnp.int32, (SOURCES, 128), 1)
    term_row = jnp.sum(jnp.where(row == lane, term, F32(0)), 0, keepdims=True)
    lane_row = lax.broadcasted_iota(jnp.int32, (1, 128), 1)
    out_ref[FREQS:] = jnp.broadcast_to(jnp.where(lane_row == SOURCES, error_sum, term_row), (8, 128))


def image(group, scalars, own, before, after, target):
    fixed = lambda i, g: (0, 0)
    whole = lambda shape: pl.BlockSpec(shape, fixed)
    return pl.pallas_call(
        image_kernel,
        grid_spec=pltpu.PrefetchScalarGridSpec(
            num_scalar_prefetch=1,
            grid=(1,),
            in_specs=[
                pl.BlockSpec(memory_space=pltpu.SMEM),
                whole((TILE_ROWS, 128)), whole((MARGIN, 128)), whole((MARGIN, 128)),
                pl.BlockSpec((ROWS, COLS), lambda i, g: (g[0], 0)),
                whole((128, FRAME)),
                pl.BlockSpec((ROWS, 128), lambda i, g: (g[0], 0)),
                pl.BlockSpec((128, ROWS), lambda i, g: (0, g[0])),
                whole((128, 2 * COLS)), whole((2 * COLS, 128)),
            ],
            out_specs=whole((FREQS + 8, 128)),
            scratch_shapes=[
                pltpu.VMEM((SOURCES * ROWS, 2 * COLS), F32),
                pltpu.VMEM((SOURCES * ROWS, 128), BF16),
                pltpu.VMEM((ROWS, COLS), F32),
                pltpu.VMEM((ROWS, COLS), F32),
                pltpu.VMEM((128, 128), F32),
                pltpu.VMEM((SOURCES, 128), F32),
                pltpu.VMEM((128, 128), F32),
            ],
        ),
        out_shape=jax.ShapeDtypeStruct((FREQS + 8, 128), F32),
        compiler_params=pltpu.CompilerParams(vmem_limit_bytes=58 * 1024 * 1024),
        name="image",
    )(group, scalars, own, before, after, target, jnp.asarray(ROW_FORWARD), jnp.asarray(ROW_INVERSE),
      jnp.asarray(np.ascontiguousarray(ROW_INVERSE.T)), jnp.asarray(COLUMN_INVERSE),
      jnp.asarray(np.ascontiguousarray(COLUMN_INVERSE.T)))


def split_dot(table, x):
    high = x.astype(BF16)
    low = (x - high.astype(F32)).astype(BF16)
    return dot(jnp.concatenate([table, table], 1), jnp.concatenate([high, low], 0))


def dot_split(x, table):
    high = x.astype(BF16)
    low = (x - high.astype(F32)).astype(BF16)
    return dot(jnp.concatenate([high, low], 1), jnp.concatenate([table, table], 0))


def product_gradient(spectrum_grad):
    lower = pltpu.roll(spectrum_grad, FREQS, 1) * halves_sign(FREQS, 1.0, -1.0)
    return jnp.concatenate([spectrum_grad, lower], 0)


def owned_kernel(grad_ref, logits_ref, row_ref, column_ref, out_ref):
    column_grad = split_dot(row_ref[...], product_gradient(grad_ref[...]))
    opening = jax.nn.sigmoid(logits_ref[...])
    out_ref[...] = dot_split(column_grad, column_ref[...]) * opening * (F32(1.0) - opening)


def owned_gradient(spectrum_grad, mask_logits):
    return pl.pallas_call(
        owned_kernel,
        out_shape=jax.ShapeDtypeStruct((TILE_ROWS, COLS), F32),
        name="owned_gradient",
    )(spectrum_grad, mask_logits,
      jnp.asarray(np.ascontiguousarray(ROW_FORWARD.T[MARGIN:MARGIN + TILE_ROWS])),
      jnp.asarray(np.ascontiguousarray(COLUMN_FORWARD.T)))


def margin_kernel(before_ref, after_ref, logits_ref, row_ref, column_ref, grad_ref, out_ref):
    first = pl.program_id(0) == 0
    spectrum_grad = jnp.where(first, before_ref[...], after_ref[...])
    column_grad = split_dot(row_ref[...], product_gradient(spectrum_grad))
    opening = jax.nn.sigmoid(logits_ref[...])
    added = dot_split(column_grad, column_ref[...]) * opening * (F32(1.0) - opening)
    out_ref[...] = grad_ref[...] + added


def margin_gradient(before, after, mask_logits, grad):
    edge = lambda i: (i * (TILE_ROWS // MARGIN - 1), 0)
    fixed = lambda i: (0, 0)
    rows = np.concatenate([ROW_FORWARD.T[MARGIN + TILE_ROWS:], ROW_FORWARD.T[:MARGIN]], 0)
    return pl.pallas_call(
        margin_kernel,
        grid=(2,),
        in_specs=[
            pl.BlockSpec((FREQS, 128), fixed), pl.BlockSpec((FREQS, 128), fixed),
            pl.BlockSpec((MARGIN, COLS), edge),
            pl.BlockSpec((MARGIN, 128), lambda i: (i, 0)),
            pl.BlockSpec((128, COLS), fixed),
            pl.BlockSpec((MARGIN, COLS), edge),
        ],
        out_specs=pl.BlockSpec((MARGIN, COLS), edge),
        out_shape=jax.ShapeDtypeStruct((TILE_ROWS, COLS), F32),
        input_output_aliases={5: 0},
        name="margin_gradient",
    )(before, after, mask_logits, jnp.asarray(np.ascontiguousarray(rows)),
      jnp.asarray(np.ascontiguousarray(COLUMN_FORWARD.T)), grad)


def from_tiles_beside(last, first):
    peers = lax.axis_size("tile")
    up = [(i, i + 1) for i in range(peers - 1)]
    down = [(j, i) for i, j in up]
    return lax.ppermute(last, "tile", up), lax.ppermute(first, "tile", down)


def from_groups(x):
    return [x] + [lax.ppermute(x, "src", [(i, i ^ d) for i in range(GROUPS)]) for d in range(1, GROUPS)]


def on_device(mask_logits, target, weights, shifts):
    group = lax.axis_index("src").astype(jnp.int32).reshape(1)
    own_scalars = jnp.concatenate([weights, shifts[:, 0].astype(F32), shifts[:, 1].astype(F32)])
    scalars = jnp.stack(from_groups(own_scalars))
    own, first, last = column_spectrum(mask_logits)
    before, after = from_tiles_beside(last, first)
    partial = image(group, scalars, own, before, after, target)
    parts = from_groups(partial)
    spectrum_grad = (parts[0][:FREQS] + parts[1][:FREQS]) + (parts[2][:FREQS] + parts[3][:FREQS])
    grad_before, grad_after = from_tiles_beside(spectrum_grad, spectrum_grad)
    grad = owned_gradient(spectrum_grad, mask_logits)
    mask_grad = margin_gradient(grad_before, grad_after, mask_logits, grad)
    rows = [p[FREQS] for p in parts]
    own_terms = sum(rows[d][d * PER_GROUP:(d + 1) * PER_GROUP] for d in range(GROUPS))
    error = (rows[0][SOURCES] + rows[1][SOURCES]) + (rows[2][SOURCES] + rows[3][SOURCES])
    sums = jnp.concatenate([own_terms, error[None]])
    peers = lax.axis_size("tile")
    everyone = lax.all_to_all(jnp.broadcast_to(sums[None], (peers, PER_GROUP + 1)), "tile", 0, 0, tiled=True)
    total = everyone.sum(axis=0)
    pixels = TILE_ROWS * COLS * peers
    return mask_grad, total[:PER_GROUP] / (2.0 * weights) / pixels, total[PER_GROUP] / pixels


def solution(mesh):
    placed = (P("tile", None), P("tile", None), P("src"), P("src", None))
    return jax.shard_map(
        on_device,
        mesh=mesh,
        in_specs=placed,
        out_specs=(P("tile", None), P("src"), P()),
        check_vma=False,
    )
```

time: 322 us -> 99.8 us (0.31)
  other arithmetic: 89.4 us -> 2.87 us
  waiting for transfers between devices: 89.5 us -> 9.72 us
  matrix products: 71.2 us -> 0 us
  Pallas kernels: 0 us -> 30.6 us
  between operations: 16.2 us -> 5.16 us
  local copies, waits for them, and re-layouts: 16.9 us -> 6.09 us
  starting transfers between devices: 35.7 us -> 44.4 us
    psum x1 -> x0, waiting for transfers between devices: 71.9 us -> none  [on_device(): intensity = lax.psum(partial_image, 'src')]
    dot_general x35 -> x0, matrix products: 71.2 us -> none  [the longest x16 60.1 us: images(): jnp.dot(row_field.reshape(source_count * tile_rows, doubled_freqs), colum...]
    reduce_sum x27 -> x1, other arithmetic: 56.4 us -> 0.08 us  [on_device(): total = everyone.sum(axis=0)]
    pallas_call x0 -> x4, Pallas kernels: none -> 30.6 us  [the longest x1 23.1 us: image(): pl.pallas_call(image_kernel, grid_spec=pltpu.PrefetchScalarGridSpec(num_s...]
    all_to_all x2 -> x1, waiting for transfers between devices: 17.5 us -> 0.01 us  [on_device(): lax.all_to_all(jnp.broadcast_to(sums[None], (peers, PER_GROUP + 1)), 'til...]
    add x17 -> x2, other arithmetic: 13.4 us -> 0.77 us  [the longest x1 0.75 us: on_device(): sum((rows[d][d * PER_GROUP:(d + 1) * PER_GROUP] for d in range(GROUPS)))]
    ppermute x4 -> x10, starting transfers between devices: 21.7 us -> 32.9 us  [the longest x4 19.8 us: from_tiles_beside(): return (lax.ppermute(last, 'tile', up), lax.ppermute(first, 'tile', down))]
    dynamic_update_slice x8 -> x0, local copies, waits for them, and re-layouts: 10.3 us -> none  [on_device(): lax.scan(backward_step, (zero_spectrum, zero_spectrum), (pupil_pairs, wei...]
  transfers between devices with their start and end apart: 7 -> 11, of which waited for: 3 -> 4; matrix products, arithmetic and copies ran while one was open for 1% -> 4% of each run, Pallas kernels for 0% -> 5%
where the time goes in v1:
time: 99.8 us; the launch traced here: 98.9 us
  starting transfers between devices  44.4 us (44%)
  Pallas kernels  30.6 us (31%)
  waiting for transfers between devices  9.72 us (10%)
  local copies, waits for them, and re-layouts  6.09 us (6%)
  between operations  5.16 us (5%)
  other arithmetic  2.87 us (3%)
    pallas_call x1, Pallas kernels, image(): pl.pallas_call(image_kernel, grid_spec=pltpu.PrefetchScalarGridSpec(num_s...  23.1 us
    ppermute x4, starting transfers between devices, from_tiles_beside(): return (lax.ppermute(last, 'tile', up), lax.ppermute(first, 'tile', down))  19.8 us
    ppermute x6, starting transfers between devices, from_groups(): lax.ppermute(x, 'src', [(i, i ^ d) for i in range(GROUPS)])  13.1 us
    all_to_all x1, starting transfers between devices, on_device(): lax.all_to_all(jnp.broadcast_to(sums[None], (peers, PER_GROUP + 1)), 'til...  11.5 us
    ppermute x4, waiting for transfers between devices, from_tiles_beside(): return (lax.ppermute(last, 'tile', up), lax.ppermute(first, 'tile', down))  5.01 us
    ppermute x6, waiting for transfers between devices, from_groups(): lax.ppermute(x, 'src', [(i, i ^ d) for i in range(GROUPS)])  4.71 us
    pallas_call x1, Pallas kernels, owned_gradient(): pl.pallas_call(owned_kernel, out_shape=jax.ShapeDtypeStruct((TILE_ROWS, C...  2.81 us
    pallas_call x1, Pallas kernels, margin_gradient(): pl.pallas_call(margin_kernel, grid=(2,), in_specs=[pl.BlockSpec((FREQS, 1...  2.47 us
  transfers between devices with their start and end apart: 11, of which 4 were waited for; matrix products, arithmetic and copies ran while one was open for 4% of the time, Pallas kernels for 5%

profile of v1, /device:TPU:2, one launch (start us, length us, event | category | flops | bytes accessed | tf_op | source)
XLA Modules:
  0.0 98.9 jit_solution(12211782886453946292)
XLA Ops:
  0.6 0.8 convert_bitcast_fusion.1
  1.4 0.7 copy-done.6
  2.1 6.7 %collective-permute-start.2 = (f32[48]{0:T(128)S(1)}, f32[48]{0:T(128)S(1)}, u32[]{:S(2)}, u32[]{:S(2)}) collective-permute-start(f32[48]{0:T(128)S(1)} %pad_maximum_fusion.1), channel_id=1, source_target_pairs={{0,192},{64,128},{128,64},{192,0},{1,193},{65,129},{129,65},{193,1... | collective-permute-start | bytes 584 | tf_op jit(solution)/shard_map/ppermute | solution.py:285
  8.8 0.7 collective-permute-start.1
  9.5 2.2 %column_spectrum.1 = (bf16[512,128]{1,0:T(8,128)(2,1)}, bf16[64,128]{1,0:T(8,128)(2,1)}, bf16[64,128]{1,0:T(8,128)(2,1)}) custom-call(f32[512,512]{1,0:T(8,128)} %logits_ref.5, bf16[512,128]{1,0:T(8,128)(2,1)} %constant.35.clone.table_ref), custom_call_target="tpu_custom_call" | custom-call | tf_op jit(solution)/shard_map/column_spectrum/pallas_call | solution.py:74
  11.7 3.5 %collective-permute-start.3 = (bf16[64,128]{1,0:T(8,128)(2,1)}, bf16[64,128]{1,0:T(8,128)(2,1)S(1)}, u32[]{:S(2)}, u32[]{:S(2)}) collective-permute-start(bf16[64,128]{1,0:T(8,128)(2,1)} %get-tuple-element.7), channel_id=1, source_target_pairs={{0,1},{1,2},{2,3},{3,4},{4,5},{5,6},{6,7},{7,8},{8,9},{9,10},{10,1... | collective-permute-start | bytes 49160 | tf_op jit(solution)/shard_map/ppermute | solution.py:281
  15.1 7.2 %collective-permute-start.4 = (bf16[64,128]{1,0:T(8,128)(2,1)}, bf16[64,128]{1,0:T(8,128)(2,1)S(1)}, u32[]{:S(2)}, u32[]{:S(2)}) collective-permute-start(bf16[64,128]{1,0:T(8,128)(2,1)} %get-tuple-element.8), channel_id=1, source_target_pairs={{1,0},{2,1},{3,2},{4,3},{5,4},{6,5},{7,6},{8,7},{9,8},{10,9},{11,1... | collective-permute-start | bytes 49160 | tf_op jit(solution)/shard_map/ppermute | solution.py:281
  22.3 0.6 pad_maximum_fusion.scalars_ref
  22.9 1.0 %collective-permute-done.4.after_ref = bf16[64,128]{1,0:T(8,128)(2,1)S(1)} collective-permute-done((bf16[64,128]{1,0:T(8,128)(2,1)}, bf16[64,128]{1,0:T(8,128)(2,1)S(1)}, u32[]{:S(2)}, u32[]{:S(2)}) %collective-permute-start.4) | collective-permute-done | bytes 16416 | tf_op jit(solution)/shard_map/ppermute | solution.py:281
  23.9 0.6 copy-done.5
  24.5 23.1 %image.1 = f32[72,128]{1,0:T(8,128)} custom-call(s32[1]{0:T(128)} %bitcast.group_ref, f32[4,48]{1,0:T(4,128)} %pad_maximum_fusion.scalars_ref, bf16[512,128]{1,0:T(8,128)(2,1)} %get-tuple-element.6.own_ref, bf16[64,128]{1,0:T(8,128)(2,1)} %copy-done.4, bf16[64,128]{1,0:T(8,128)(2,1)} %copy-done.5, s32[512,512]{1,0:T(8,128)} %target_ref.1, ...), custom_call_target="tpu_custom_call" | custom-call | tf_op jit(solution)/shard_map/image/pallas_call | solution.py:180
  47.6 4.2 %collective-permute-start.7 = (f32[72,128]{1,0:T(8,128)}, f32[72,128]{1,0:T(8,128)S(1)}, u32[]{:S(2)}, u32[]{:S(2)}) collective-permute-start(f32[72,128]{1,0:T(8,128)} %image.1), channel_id=1, source_target_pairs={{0,192},{64,128},{128,64},{192,0},{1,193},{65,129},{129,65},{193,1... | collective-permute-start | bytes 110600 | tf_op jit(solution)/shard_map/ppermute | solution.py:285
  51.9 1.4 %collective-permute-start.6 = (f32[72,128]{1,0:T(8,128)}, f32[72,128]{1,0:T(8,128)S(1)}, u32[]{:S(2)}, u32[]{:S(2)}) collective-permute-start(f32[72,128]{1,0:T(8,128)} %image.1), channel_id=1, source_target_pairs={{0,128},{64,192},{128,0},{192,64},{1,129},{65,193},{129,1},{193,65... | collective-permute-start | bytes 110600 | tf_op jit(solution)/shard_map/ppermute | solution.py:285
  53.4 1.3 %slice.92 = f32[1,1]{1,0:T(1,128)} slice(f32[72,128]{1,0:T(8,128)} %image.1), slice={[64:65], [64:65]} | slice | bytes 8 | tf_op jit(solution)/shard_map/slice | solution.py:302
  55.8 4.1 %collective-permute-done.6 = f32[72,128]{1,0:T(8,128)S(1)} collective-permute-done((f32[72,128]{1,0:T(8,128)}, f32[72,128]{1,0:T(8,128)S(1)}, u32[]{:S(2)}, u32[]{:S(2)}) %collective-permute-start.6) | collective-permute-done | bytes 36896 | tf_op jit(solution)/shard_map/ppermute | solution.py:285
  63.7 0.8 fusion.1
  64.6 0.6 broadcast_in_dim.10
  65.2 11.5 %all-to-all-start = ((f32[64,1,17]{2,1,0:T(1,128)}), f32[64,1,17]{2,1,0:T(1,128)S(1)}, u32[]{:S(2)}, u32[]{:S(2)}) async-start(f32[64,1,17]{2,1,0:T(1,128)} %broadcast_in_dim.10), calls=%async_computation | async-start | bytes 65536 | tf_op jit(solution)/shard_map/all_to_all | solution.py:305
  76.7 7.3 %collective-permute-start.9 = (f32[64,128]{1,0:T(8,128)S(1)}, f32[64,128]{1,0:T(8,128)S(1)}, u32[]{:S(2)}, u32[]{:S(2)}) collective-permute-start(f32[64,128]{1,0:T(8,128)S(1)} %fusion.grad_ref), channel_id=1, source_target_pairs={{1,0},{2,1},{3,2},{4,3},{5,4},{6,5},{7,6},{8,7},{9,8},{10,9},{11,1... | collective-permute-start | bytes 98312 | tf_op jit(solution)/shard_map/ppermute | solution.py:281
  84.0 1.9 %collective-permute-start.8 = (f32[64,128]{1,0:T(8,128)S(1)}, f32[64,128]{1,0:T(8,128)S(1)}, u32[]{:S(2)}, u32[]{:S(2)}) collective-permute-start(f32[64,128]{1,0:T(8,128)S(1)} %fusion.grad_ref), channel_id=1, source_target_pairs={{0,1},{1,2},{2,3},{3,4},{4,5},{5,6},{6,7},{7,8},{8,9},{9,10},{10,1... | collective-permute-start | bytes 98312 | tf_op jit(solution)/shard_map/ppermute | solution.py:281
  86.0 2.8 %owned_gradient.1.grad_ref = f32[512,512]{1,0:T(8,128)} custom-call(f32[64,128]{1,0:T(8,128)} %copy-done.1, f32[512,512]{1,0:T(8,128)} %logits_ref.5, bf16[512,128]{1,0:T(8,128)(2,1)} %constant.41.clone.row_ref, bf16[128,512]{1,0:T(8,128)(2,1)} %constant.42.clone.column_ref), custom_call_target="tpu_custom_call" | custom-call | tf_op jit(solution)/shard_map/owned_gradient/pallas_call | solution.py:237
  90.6 4.0 %collective-permute-done.8.before_ref = f32[64,128]{1,0:T(8,128)S(1)} collective-permute-done((f32[64,128]{1,0:T(8,128)S(1)}, f32[64,128]{1,0:T(8,128)S(1)}, u32[]{:S(2)}, u32[]{:S(2)}) %collective-permute-start.8) | collective-permute-done | bytes 32800 | tf_op jit(solution)/shard_map/ppermute | solution.py:281
  94.7 0.6 copy-done.3
  95.3 2.5 %margin_gradient.1 = f32[512,512]{1,0:T(8,128)} custom-call(f32[64,128]{1,0:T(8,128)} %copy-done.3, f32[64,128]{1,0:T(8,128)} %copy-done.2, f32[512,512]{1,0:T(8,128)} %logits_ref.5, bf16[128,128]{1,0:T(8,128)(2,1)} %constant.43.clone.row_ref, bf16[128,512]{1,0:T(8,128)(2,1)} %constant.42.clone.column_ref, ...), custom_call_target="tpu_custom_call", output_to_operand_aliasing={{}: (5, {})} | custom-call | tf_op jit(solution)/shard_map/margin_gradient/pallas_call | solution.py:259
  (30 shorter events, 3.8 us)
Async XLA Ops:
  1.4 0.7 copy-start.6
  2.1 20.2 %collective-permute-start.2 = (f32[48]{0:T(128)S(1)}, f32[48]{0:T(128)S(1)}, u32[]{:S(2)}, u32[]{:S(2)}) collective-permute-start(f32[48]{0:T(128)S(1)} %pad_maximum_fusion.1), channel_id=1, source_target_pairs={{0,192},{64,128},{128,64},{192,0},{1,193},{65,129},{129,65},{193,1... | collective-permute-start | bytes 584 | tf_op jit(solution)/shard_map/ppermute | solution.py:285
  8.8 13.6 %collective-permute-start.1 = (f32[48]{0:T(128)S(1)}, f32[48]{0:T(128)S(1)}, u32[]{:S(2)}, u32[]{:S(2)}) collective-permute-start(f32[48]{0:T(128)S(1)} %pad_maximum_fusion.1), channel_id=1, source_target_pairs={{0,128},{64,192},{128,0},{192,64},{1,129},{65,193},{129,1},{193,65... | collective-permute-start | bytes 584 | tf_op jit(solution)/shard_map/ppermute | solution.py:285
  9.4 12.9 %collective-permute-start = (f32[48]{0:T(128)S(1)}, f32[48]{0:T(128)S(1)}, u32[]{:S(2)}, u32[]{:S(2)}) collective-permute-start(f32[48]{0:T(128)S(1)} %pad_maximum_fusion.1), channel_id=1, source_target_pairs={{0,64},{64,0},{128,192},{192,128},{1,65},{65,1},{129,193},{193,129... | collective-permute-start | bytes 584 | tf_op jit(solution)/shard_map/ppermute | solution.py:285
  11.7 11.3 %collective-permute-start.3 = (bf16[64,128]{1,0:T(8,128)(2,1)}, bf16[64,128]{1,0:T(8,128)(2,1)S(1)}, u32[]{:S(2)}, u32[]{:S(2)}) collective-permute-start(bf16[64,128]{1,0:T(8,128)(2,1)} %get-tuple-element.7), channel_id=1, source_target_pairs={{0,1},{1,2},{2,3},{3,4},{4,5},{5,6},{6,7},{7,8},{8,9},{9,10},{10,1... | collective-permute-start | bytes 49160 | tf_op jit(solution)/shard_map/ppermute | solution.py:281
  15.1 8.8 %collective-permute-start.4 = (bf16[64,128]{1,0:T(8,128)(2,1)}, bf16[64,128]{1,0:T(8,128)(2,1)S(1)}, u32[]{:S(2)}, u32[]{:S(2)}) collective-permute-start(bf16[64,128]{1,0:T(8,128)(2,1)} %get-tuple-element.8), channel_id=1, source_target_pairs={{1,0},{2,1},{3,2},{4,3},{5,4},{6,5},{7,6},{8,7},{9,8},{10,9},{11,1... | collective-permute-start | bytes 49160 | tf_op jit(solution)/shard_map/ppermute | solution.py:281
  22.9 1.0 %copy-start.4 = (bf16[64,128]{1,0:T(8,128)(2,1)}, bf16[64,128]{1,0:T(8,128)(2,1)S(1)}, u32[]{:S(2)}) copy-start(bf16[64,128]{1,0:T(8,128)(2,1)S(1)} %collective-permute-done.3.before_ref) | copy-start | bytes 49156
  23.9 0.6 copy-start.5
  47.6 7.6 %collective-permute-start.7 = (f32[72,128]{1,0:T(8,128)}, f32[72,128]{1,0:T(8,128)S(1)}, u32[]{:S(2)}, u32[]{:S(2)}) collective-permute-start(f32[72,128]{1,0:T(8,128)} %image.1), channel_id=1, source_target_pairs={{0,192},{64,128},{128,64},{192,0},{1,193},{65,129},{129,65},{193,1... | collective-permute-start | bytes 110600 | tf_op jit(solution)/shard_map/ppermute | solution.py:285
  51.9 8.1 %collective-permute-start.6 = (f32[72,128]{1,0:T(8,128)}, f32[72,128]{1,0:T(8,128)S(1)}, u32[]{:S(2)}, u32[]{:S(2)}) collective-permute-start(f32[72,128]{1,0:T(8,128)} %image.1), channel_id=1, source_target_pairs={{0,128},{64,192},{128,0},{192,64},{1,129},{65,193},{129,1},{193,65... | collective-permute-start | bytes 110600 | tf_op jit(solution)/shard_map/ppermute | solution.py:285
  53.3 8.5 %collective-permute-start.5 = (f32[72,128]{1,0:T(8,128)}, f32[72,128]{1,0:T(8,128)S(1)}, u32[]{:S(2)}, u32[]{:S(2)}) collective-permute-start(f32[72,128]{1,0:T(8,128)} %image.1), channel_id=1, source_target_pairs={{0,64},{64,0},{128,192},{192,128},{1,65},{65,1},{129,193},{193,129... | collective-permute-start | bytes 110600 | tf_op jit(solution)/shard_map/ppermute | solution.py:285
  65.2 11.5 %copy-start = (f32[72,128]{1,0:T(8,128)S(1)}, f32[72,128]{1,0:T(8,128)}, u32[]{:S(2)}) copy-start(f32[72,128]{1,0:T(8,128)} %image.1) | copy-start | bytes 110596
  65.2 23.6 %all-to-all-start = ((f32[64,1,17]{2,1,0:T(1,128)}), f32[64,1,17]{2,1,0:T(1,128)S(1)}, u32[]{:S(2)}, u32[]{:S(2)}) async-start(f32[64,1,17]{2,1,0:T(1,128)} %broadcast_in_dim.10), calls=%async_computation | async-start | bytes 65536 | tf_op jit(solution)/shard_map/all_to_all | solution.py:305
  76.7 9.2 %copy-start.1 = (f32[64,128]{1,0:T(8,128)}, f32[64,128]{1,0:T(8,128)S(1)}, u32[]{:S(2)}) copy-start(f32[64,128]{1,0:T(8,128)S(1)} %fusion.grad_ref) | copy-start | bytes 98308
  76.7 13.9 %collective-permute-start.9 = (f32[64,128]{1,0:T(8,128)S(1)}, f32[64,128]{1,0:T(8,128)S(1)}, u32[]{:S(2)}, u32[]{:S(2)}) collective-permute-start(f32[64,128]{1,0:T(8,128)S(1)} %fusion.grad_ref), channel_id=1, source_target_pairs={{1,0},{2,1},{3,2},{4,3},{5,4},{6,5},{7,6},{8,7},{9,8},{10,9},{11,1... | collective-permute-start | bytes 98312 | tf_op jit(solution)/shard_map/ppermute | solution.py:281
  84.0 10.6 %collective-permute-start.8 = (f32[64,128]{1,0:T(8,128)S(1)}, f32[64,128]{1,0:T(8,128)S(1)}, u32[]{:S(2)}, u32[]{:S(2)}) collective-permute-start(f32[64,128]{1,0:T(8,128)S(1)} %fusion.grad_ref), channel_id=1, source_target_pairs={{0,1},{1,2},{2,3},{3,4},{4,5},{5,6},{6,7},{7,8},{8,9},{9,10},{10,1... | collective-permute-start | bytes 98312 | tf_op jit(solution)/shard_map/ppermute | solution.py:281
  90.6 4.0 %copy-start.2 = (f32[64,128]{1,0:T(8,128)}, f32[64,128]{1,0:T(8,128)S(1)}, u32[]{:S(2)}) copy-start(f32[64,128]{1,0:T(8,128)S(1)} %collective-permute-done.9.after_ref) | copy-start | bytes 98308
  94.7 0.6 copy-start.3

commit v2 on v1

v2 whole, which is shorter than its diff:
```python
import functools

import numpy as np
import jax
import jax.numpy as jnp
from jax import lax
from jax.experimental import pallas as pl
from jax.experimental.pallas import tpu as pltpu
from jax.sharding import PartitionSpec as P

FREQS = 64
RADIUS = 20
MARGIN = 64
COLS = 512
TILE_ROWS = 512
FRAME = 640
SOURCES = 64
GROUPS = 4
PER_GROUP = SOURCES // GROUPS
ROWS = TILE_ROWS // GROUPS
MIB = 1024 * 1024
STEEPNESS = 12.0
THRESHOLD = 0.2
STEP = 16
F32 = jnp.float32
BF16 = jnp.bfloat16


def angles(length_used, offset, period):
    position = np.arange(length_used, dtype=np.int32)[:, None] + offset
    frequency = np.arange(FREQS, dtype=np.int32)[None, :] - FREQS // 2
    cycles = np.mod(position * frequency, period).astype(np.float32)
    angle_value = (cycles * np.float32(2.0 * 3.141592653589793 / period)).astype(np.float64)
    return np.cos(angle_value).astype(np.float32), np.sin(angle_value).astype(np.float32)


def make_tables():
    column_cosine, column_sine = angles(COLS, 0, COLS)
    column_forward = np.concatenate([column_cosine, -column_sine], 1)
    frame_cosine, frame_sine = angles(FRAME, 0, FRAME)
    row_forward = np.concatenate([frame_cosine.T, -frame_sine.T], 0)
    owned_cosine, owned_sine = angles(TILE_ROWS, MARGIN, FRAME)
    row_inverse = np.concatenate([owned_cosine, owned_sine], 1) / np.float32(FRAME)
    cosine_scaled = column_cosine.T / np.float32(COLS)
    sine_scaled = column_sine.T / np.float32(COLS)
    upper_block = np.concatenate([cosine_scaled, sine_scaled], 1)
    lower_block = np.concatenate([-sine_scaled, cosine_scaled], 1)
    column_inverse = np.concatenate([upper_block, lower_block], 0)
    chunked = column_inverse.reshape(2 * FREQS, 2, COLS // 128, 128).transpose(0, 2, 1, 3)
    chunked = chunked.reshape(2 * FREQS, 2 * COLS)
    rounded = lambda a: np.ascontiguousarray(a).astype(BF16)
    return [rounded(a) for a in (column_forward, row_forward, row_inverse, chunked)]


COLUMN_FORWARD, ROW_FORWARD, ROW_INVERSE, COLUMN_INVERSE = make_tables()


def dot(a, b):
    return jnp.dot(a, b, preferred_element_type=F32)


def halves_sign(rows, left, right):
    lane = lax.broadcasted_iota(jnp.int32, (rows, 128), 1)
    return jnp.where(lane < FREQS, F32(left), F32(right))


def edge_kernel(first_ref, last_ref, table_ref, weights_ref, shifts_ref, first_out, last_out, packed_ref):
    first_out[...] = dot(jax.nn.sigmoid(first_ref[...]).astype(BF16), table_ref[...]).astype(BF16)
    last_out[...] = dot(jax.nn.sigmoid(last_ref[...]).astype(BF16), table_ref[...]).astype(BF16)
    packed_ref[0:1] = weights_ref[...]
    packed_ref[1:3] = shifts_ref[...].astype(F32)


def edge_spectrum(mask_logits, weights, shifts):
    fixed = lambda i: (0, 0)
    return pl.pallas_call(
        edge_kernel,
        grid=(1,),
        in_specs=[
            pl.BlockSpec((MARGIN, COLS), fixed),
            pl.BlockSpec((MARGIN, COLS), lambda i: (TILE_ROWS // MARGIN - 1, 0)),
            pl.BlockSpec((COLS, 128), fixed),
            pl.BlockSpec((1, PER_GROUP), fixed),
            pl.BlockSpec((2, PER_GROUP), fixed),
        ],
        out_specs=[pl.BlockSpec((MARGIN, 128), fixed), pl.BlockSpec((MARGIN, 128), fixed),
                   pl.BlockSpec((3, PER_GROUP), fixed)],
        out_shape=[jax.ShapeDtypeStruct((MARGIN, 128), BF16), jax.ShapeDtypeStruct((MARGIN, 128), BF16),
                   jax.ShapeDtypeStruct((3, PER_GROUP), F32)],
        compiler_params=pltpu.CompilerParams(vmem_limit_bytes=4 * MIB),
        name="edge_spectrum",
    )(mask_logits, mask_logits, jnp.asarray(COLUMN_FORWARD), weights.reshape(1, PER_GROUP), shifts.T)


def column_kernel(logits_ref, table_ref, out_ref):
    out_ref[...] = dot(jax.nn.sigmoid(logits_ref[...]).astype(BF16), table_ref[...]).astype(BF16)


def column_spectrum(mask_logits):
    return pl.pallas_call(
        column_kernel,
        out_shape=jax.ShapeDtypeStruct((TILE_ROWS, 128), BF16),
        compiler_params=pltpu.CompilerParams(vmem_limit_bytes=6 * MIB),
        name="column_spectrum",
    )(mask_logits, jnp.asarray(COLUMN_FORWARD))


def pupil(scalars, step, j):
    ref, i = scalars[j % GROUPS], step * (STEP // GROUPS) + j // GROUPS
    across, along = ref[1, i], ref[2, i]
    row = lax.broadcasted_iota(jnp.int32, (FREQS, 128), 0) - FREQS // 2
    lane = jnp.bitwise_and(lax.broadcasted_iota(jnp.int32, (FREQS, 128), 1), FREQS - 1) - FREQS // 2
    row, lane = row.astype(F32) - across, lane.astype(F32) - along
    return row * row + lane * lane <= F32(RADIUS * RADIUS)


def image_kernel(group_ref, own_scalars, scalars_1, scalars_2, scalars_3, own_ref, before_ref, after_ref, target_ref, row_forward_ref,
                 row_inverse_ref, row_inverse_t_ref, inverse_ref, inverse_t_ref, out_ref, sums_ref,
                 fields_ref, row_field_ref, intensity_ref, cotangent_ref, spectra_ref, terms_ref, grad_ref, rounded_ref):
    scalars = [own_scalars, scalars_1, scalars_2, scalars_3]
    frame = jnp.concatenate([before_ref[...], own_ref[...], after_ref[...]], 0)
    product = dot(row_forward_ref[...], frame)
    swapped = pltpu.roll(product[FREQS:], FREQS, 1)
    spectrum = (product[:FREQS] + halves_sign(FREQS, -1.0, 1.0) * swapped).astype(BF16).astype(F32)
    spectra_ref[:FREQS] = spectrum
    spectra_ref[FREQS:] = pltpu.roll(spectrum, FREQS, 1) * halves_sign(FREQS, -1.0, 1.0)
    intensity_ref[...] = jnp.zeros_like(intensity_ref)

    steps = SOURCES // STEP

    def image_rows(step):
        blocks = []
        for j in range(STEP):
            inside = pupil(scalars, step, j)
            inside = jnp.concatenate([inside, inside], 0)
            blocks.append(jnp.where(inside, spectra_ref[...], F32(0)).astype(BF16))
        row_field = dot(row_inverse_ref[...], jnp.concatenate(blocks, 1)).astype(BF16)
        for j in range(STEP):
            start = pl.multiple_of((step * STEP + j) * ROWS, ROWS)
            row_field_ref[pl.ds(start, ROWS), :] = row_field[:, 128 * j:128 * (j + 1)]

    def weight(step, j):
        return scalars[j % GROUPS][0, step * (STEP // GROUPS) + j // GROUPS]

    image_rows(0)

    @pl.loop(0, steps)
    def _(step):
        start = pl.multiple_of(step * (STEP * ROWS), STEP * ROWS)
        row_field = row_field_ref[pl.ds(start, STEP * ROWS), :]
        for n in range(4):
            fields = dot(row_field, inverse_ref[:, 256 * n:256 * (n + 1)])
            fields_ref[pl.ds(start, STEP * ROWS), 256 * n:256 * (n + 1)] = fields
            power = fields[:, :128] * fields[:, :128] + fields[:, 128:] * fields[:, 128:]
            total = weight(step, 0) * power[:ROWS]
            for j in range(1, STEP):
                total = total + weight(step, j) * power[j * ROWS:(j + 1) * ROWS]
            intensity_ref[:, 128 * n:128 * (n + 1)] += total
        image_rows(jnp.minimum(step + 1, steps - 1))

    printed = jax.nn.sigmoid(F32(STEEPNESS) * (intensity_ref[...] - F32(THRESHOLD)))
    error_value = printed - target_ref[...].astype(F32)
    cotangent_ref[...] = F32(2.0 * STEEPNESS) * error_value * printed * (F32(1.0) - printed)
    error_rows = jnp.sum(error_value * error_value, 0, keepdims=True)
    error_lanes = (error_rows[:, :128] + error_rows[:, 128:256]) + (error_rows[:, 256:384] + error_rows[:, 384:])
    error_sum = jnp.sum(error_lanes, 1, keepdims=True)
    grad_ref[...] = jnp.zeros_like(grad_ref)

    rounded_ref[...] = jnp.zeros_like(rounded_ref)

    def add_block_grad(step):
        block_grad = dot(row_inverse_t_ref[...], rounded_ref[...])
        total = jnp.zeros((2 * FREQS, 128), F32)
        for j in range(STEP):
            inside = pupil(scalars, step, j)
            inside = jnp.concatenate([inside, inside], 0)
            total = total + jnp.where(inside, block_grad[:, 128 * j:128 * (j + 1)], F32(0))
        grad_ref[...] += total

    @pl.loop(0, steps)
    def _(step):
        start = pl.multiple_of(step * (STEP * ROWS), STEP * ROWS)
        add_block_grad(jnp.maximum(step - 1, 0))
        row_grad = None
        for n in range(4):
            cot = cotangent_ref[:, 128 * n:128 * (n + 1)]
            parts = []
            for j in range(STEP):
                scaling = (F32(2.0) * weight(step, j)) * cot
                at = pl.multiple_of(start + j * ROWS, ROWS)
                fields = fields_ref[pl.ds(at, ROWS), 256 * n:256 * (n + 1)]
                parts.append((jnp.concatenate([scaling, scaling], 1) * fields).astype(BF16))
            part = dot(jnp.concatenate(parts, 0), inverse_t_ref[256 * n:256 * (n + 1), :])
            row_grad = part if row_grad is None else row_grad + part
        row_field = row_field_ref[pl.ds(start, STEP * ROWS), :].astype(F32)
        terms = row_grad * row_field
        rounded = row_grad.astype(BF16)
        for j in range(STEP):
            terms_ref[pl.ds(step * STEP + j, 1), :] = jnp.sum(terms[j * ROWS:(j + 1) * ROWS], 0, keepdims=True)
            rounded_ref[:, 128 * j:128 * (j + 1)] = rounded[j * ROWS:(j + 1) * ROWS]

    add_block_grad(steps - 1)
    grads = grad_ref[...]
    out_ref[...] = grads[:FREQS] + halves_sign(FREQS, 1.0, -1.0) * pltpu.roll(grads[FREQS:], FREQS, 1)
    term = jnp.sum(terms_ref[...], 1, keepdims=True)
    row = lax.broadcasted_iota(jnp.int32, (SOURCES, 128), 0)
    lane = lax.broadcasted_iota(jnp.int32, (SOURCES, 128), 1)
    wanted = (row % GROUPS) * PER_GROUP + row // GROUPS
    term_row = jnp.sum(jnp.where(wanted == lane, term, F32(0)), 0, keepdims=True)
    lane = lax.broadcasted_iota(jnp.int32, (1, 128), 1)
    own = group_ref[0]
    for bit, width in ((1, PER_GROUP), (2, 2 * PER_GROUP)):
        swapped = jnp.where((lane // width) % 2 == 0, pltpu.roll(term_row, 128 - width, 1),
                            pltpu.roll(term_row, width, 1))
        term_row = jnp.where(jnp.bitwise_and(own, bit) != 0, swapped, term_row)
    term_row = jnp.where(lane < SOURCES, term_row, F32(0))
    sums_ref[...] = jnp.broadcast_to(jnp.where(lane == SOURCES, error_sum, term_row)[None], sums_ref.shape)


def image(group, scalars, own, before, after, target, peers):
    fixed = lambda i, g: (0, 0)
    whole = lambda shape: pl.BlockSpec(shape, fixed)
    return pl.pallas_call(
        image_kernel,
        grid_spec=pltpu.PrefetchScalarGridSpec(
            num_scalar_prefetch=1,
            grid=(1,),
            in_specs=[
                *[pl.BlockSpec(memory_space=pltpu.SMEM)] * GROUPS,
                whole((TILE_ROWS, 128)), whole((MARGIN, 128)), whole((MARGIN, 128)),
                pl.BlockSpec((ROWS, COLS), lambda i, g: (g[0], 0)),
                whole((128, FRAME)),
                pl.BlockSpec((ROWS, 128), lambda i, g: (g[0], 0)),
                pl.BlockSpec((128, ROWS), lambda i, g: (0, g[0])),
                whole((128, 2 * COLS)), whole((2 * COLS, 128)),
            ],
            out_specs=[whole((FREQS, 128)), pl.BlockSpec((peers, 1, 128), lambda i, g: (0, 0, 0))],
            scratch_shapes=[
                pltpu.VMEM((SOURCES * ROWS, 2 * COLS), F32),
                pltpu.VMEM((SOURCES * ROWS, 128), BF16),
                pltpu.VMEM((ROWS, COLS), F32),
                pltpu.VMEM((ROWS, COLS), F32),
                pltpu.VMEM((128, 128), F32),
                pltpu.VMEM((SOURCES, 128), F32),
                pltpu.VMEM((128, 128), F32),
                pltpu.VMEM((ROWS, STEP * 128), BF16),
            ],
        ),
        out_shape=[jax.ShapeDtypeStruct((FREQS, 128), F32), jax.ShapeDtypeStruct((peers, 1, 128), F32)],
        compiler_params=pltpu.CompilerParams(vmem_limit_bytes=44 * MIB),
        name="image",
    )(group, *scalars, own, before, after, target, jnp.asarray(ROW_FORWARD), jnp.asarray(ROW_INVERSE),
      jnp.asarray(np.ascontiguousarray(ROW_INVERSE.T)), jnp.asarray(COLUMN_INVERSE),
      jnp.asarray(np.ascontiguousarray(COLUMN_INVERSE.T)))


def split_dot(table, x):
    high = x.astype(BF16)
    low = (x - high.astype(F32)).astype(BF16)
    return dot(jnp.concatenate([table, table], 1), jnp.concatenate([high, low], 0))


def dot_split(x, table):
    high = x.astype(BF16)
    low = (x - high.astype(F32)).astype(BF16)
    return dot(jnp.concatenate([high, low], 1), jnp.concatenate([table, table], 0))


def product_gradient(spectrum_grad):
    lower = pltpu.roll(spectrum_grad, FREQS, 1) * halves_sign(FREQS, 1.0, -1.0)
    return jnp.concatenate([spectrum_grad, lower], 0)


def owned_kernel(grad_ref, logits_ref, row_ref, column_ref, out_ref):
    column_grad = split_dot(row_ref[...], product_gradient(grad_ref[...]))
    opening = jax.nn.sigmoid(logits_ref[...])
    out_ref[...] = dot_split(column_grad, column_ref[...]) * opening * (F32(1.0) - opening)


def owned_gradient(spectrum_grad, mask_logits):
    return pl.pallas_call(
        owned_kernel,
        out_shape=jax.ShapeDtypeStruct((TILE_ROWS, COLS), F32),
        compiler_params=pltpu.CompilerParams(vmem_limit_bytes=8 * MIB),
        name="owned_gradient",
    )(spectrum_grad, mask_logits,
      jnp.asarray(np.ascontiguousarray(ROW_FORWARD.T[MARGIN:MARGIN + TILE_ROWS])),
      jnp.asarray(np.ascontiguousarray(COLUMN_FORWARD.T)))


def last_kernel(group_ref, before_ref, after_ref, logits_ref, row_ref, column_ref, grad_ref, own_ref, beside_ref,
                far_ref, across_ref, weights_ref, out_ref, weight_grad_ref, loss_ref, *, pixels):
    first = pl.program_id(0) == 0
    spectrum_grad = jnp.where(first, before_ref[...], after_ref[...])
    column_grad = split_dot(row_ref[...], product_gradient(spectrum_grad))
    opening = jax.nn.sigmoid(logits_ref[...])
    added = dot_split(column_grad, column_ref[...]) * opening * (F32(1.0) - opening)
    out_ref[...] = grad_ref[...] + added

    @pl.when(first)
    def _():
        total = (own_ref[...] + beside_ref[...]) + (far_ref[...] + across_ref[...])
        row = total
        for bit, width in ((1, PER_GROUP), (2, 2 * PER_GROUP)):
            row = jnp.where(jnp.bitwise_and(group_ref[0], bit) != 0, pltpu.roll(row, 128 - width, 1), row)
        weight_grad_ref[...] = row[:, :PER_GROUP] / (F32(2.0) * weights_ref[...]) / F32(pixels)
        loss_ref[...] = total[:, SOURCES:SOURCES + 1] / F32(pixels)


def last_steps(group, before, after, mask_logits, grad, sums, weights, pixels):
    edge = lambda i: (i * (TILE_ROWS // MARGIN - 1), 0)
    fixed = lambda i: (0, 0)
    rows = np.concatenate([ROW_FORWARD.T[MARGIN + TILE_ROWS:], ROW_FORWARD.T[:MARGIN]], 0)
    return pl.pallas_call(
        functools.partial(last_kernel, pixels=pixels),
        grid=(2,),
        in_specs=[
            pl.BlockSpec(memory_space=pltpu.SMEM),
            pl.BlockSpec((FREQS, 128), fixed), pl.BlockSpec((FREQS, 128), fixed),
            pl.BlockSpec((MARGIN, COLS), edge),
            pl.BlockSpec((MARGIN, 128), lambda i: (i, 0)),
            pl.BlockSpec((128, COLS), fixed),
            pl.BlockSpec((MARGIN, COLS), edge),
            *[pl.BlockSpec((1, 128), fixed)] * GROUPS,
            pl.BlockSpec((1, PER_GROUP), fixed),
        ],
        out_specs=[pl.BlockSpec((MARGIN, COLS), edge), pl.BlockSpec((1, PER_GROUP), fixed),
                   pl.BlockSpec((1, 1), fixed)],
        out_shape=[jax.ShapeDtypeStruct((TILE_ROWS, COLS), F32), jax.ShapeDtypeStruct((1, PER_GROUP), F32),
                   jax.ShapeDtypeStruct((1, 1), F32)],
        input_output_aliases={6: 0},
        compiler_params=pltpu.CompilerParams(vmem_limit_bytes=4 * MIB),
        name="last_steps",
    )(group, before, after, mask_logits, jnp.asarray(np.ascontiguousarray(rows)),
      jnp.asarray(np.ascontiguousarray(COLUMN_FORWARD.T)), grad, *sums, weights.reshape(1, PER_GROUP))


def from_tiles_beside(last, first):
    peers = lax.axis_size("tile")
    up = [(i, i + 1) for i in range(peers - 1)]
    down = [(j, i) for i, j in up]
    return lax.ppermute(last, "tile", up), lax.ppermute(first, "tile", down)


def from_groups(x):
    return [x] + [lax.ppermute(x, "src", [(i, i ^ d) for i in range(GROUPS)]) for d in range(1, GROUPS)]


def on_device(mask_logits, target, weights, shifts):
    peers = lax.axis_size("tile")
    group = lax.axis_index("src").astype(jnp.int32).reshape(1)
    first, last, packed = edge_spectrum(mask_logits, weights, shifts)
    before, after = from_tiles_beside(last, first)
    scalars = from_groups(packed)
    own = column_spectrum(mask_logits)
    partial, sums = image(group, scalars, own, before, after, target, peers)
    chip = partial + lax.ppermute(partial, "src", [(i, i ^ 1) for i in range(GROUPS)])
    far = lax.ppermute(chip, "src", [(i, i ^ 2) for i in range(GROUPS)])
    sums = lax.all_to_all(sums, "tile", 0, 0, tiled=True)
    spectrum_grad = chip + far
    grad_before, grad_after = from_tiles_beside(spectrum_grad, spectrum_grad)
    sums = from_groups(jnp.sum(sums, 0))
    grad = owned_gradient(spectrum_grad, mask_logits)
    mask_grad, weight_grad, loss = last_steps(
        group, grad_before, grad_after, mask_logits, grad, sums, weights, TILE_ROWS * COLS * peers)
    return mask_grad, weight_grad.reshape(PER_GROUP), loss.reshape(())


def solution(mesh):
    placed = (P("tile", None), P("tile", None), P("src"), P("src", None))
    return jax.shard_map(
        on_device,
        mesh=mesh,
        in_specs=placed,
        out_specs=(P("tile", None), P("src"), P()),
        check_vma=False,
    )
```

time: 99.8 us -> 74.8 us (0.75)
  the two profiles are of different devices: /device:TPU:2 before, /device:TPU:1 now
where the time goes in v2:
time: 74.8 us; the launch traced here: 74.5 us
  starting transfers between devices  38.4 us (51%)
  Pallas kernels  18.2 us (24%)
  waiting for transfers between devices  14 us (19%)
  local copies, waits for them, and re-layouts  2.86 us (4%)
  between operations  0.83 us (1%)
    ppermute x6, starting transfers between devices, from_groups(): lax.ppermute(x, 'src', [(i, i ^ d) for i in range(GROUPS)])  15.7 us
    pallas_call x1, Pallas kernels, image(): pl.pallas_call(image_kernel, grid_spec=pltpu.PrefetchScalarGridSpec(num_s...  13.8 us
    all_to_all x1, starting transfers between devices, on_device(): sums = lax.all_to_all(sums, 'tile', 0, 0, tiled=True)  10.9 us
    ppermute x4, starting transfers between devices, from_tiles_beside(): return (lax.ppermute(last, 'tile', up), lax.ppermute(first, 'tile', down))  10.7 us
    ppermute x6, waiting for transfers between devices, from_groups(): lax.ppermute(x, 'src', [(i, i ^ d) for i in range(GROUPS)])  9.65 us
    all_to_all x1, waiting for transfers between devices, on_device(): sums = lax.all_to_all(sums, 'tile', 0, 0, tiled=True)  3.51 us
    unnamed x30, local copies, waits for them, and re-layouts  2.86 us
    pallas_call x1, Pallas kernels, last_steps(): pl.pallas_call(functools.partial(last_kernel, pixels=pixels), grid=(2,),...  2.43 us
  transfers between devices with their start and end apart: 13, of which 5 were waited for; matrix products, arithmetic and copies ran while one was open for 0% of the time, Pallas kernels for 2%

profile of v2, /device:TPU:1, one launch (start us, length us, event | category | flops | bytes accessed | tf_op | source)
XLA Modules:
  0.0 74.5 jit_solution(350022649817078457)
XLA Ops:
  0.7 0.6 copy-done.13
  1.3 1.2 %copy-done = f32[512,512]{1,0:T(8,128)S(1)} copy-done((f32[512,512]{1,0:T(8,128)S(1)}, f32[512,512]{1,0:T(8,128)}, u32[]{:S(2)}) %copy-start) | copy-done | bytes 1048600
  2.6 0.9 %copy-done.4 = bf16[512,128]{1,0:T(8,128)(2,1)S(1)} copy-done((bf16[512,128]{1,0:T(8,128)(2,1)S(1)}, bf16[512,128]{1,0:T(8,128)(2,1)}, u32[]{:S(2)}) %copy-start.4) | copy-done | bytes 131096
  3.5 0.2 edge_spectrum.1
  3.7 4.2 %collective-permute-start.3 = (bf16[64,128]{1,0:T(8,128)(2,1)S(1)}, bf16[64,128]{1,0:T(8,128)(2,1)S(1)}, u32[]{:S(2)}, u32[]{:S(2)}) collective-permute-start(bf16[64,128]{1,0:T(8,128)(2,1)S(1)} %get-tuple-element.12), channel_id=1, source_target_pairs={{0,1},{1,2},{2,3},{3,4},{4,5},{5,6},{6,7},{7,8},{8,9},{9,10},{10,1... | collective-permute-start | bytes 49160 | tf_op jit(solution)/shard_map/ppermute | solution.py:342
  7.8 1.3 %collective-permute-start.4 = (bf16[64,128]{1,0:T(8,128)(2,1)S(1)}, bf16[64,128]{1,0:T(8,128)(2,1)S(1)}, u32[]{:S(2)}, u32[]{:S(2)}) collective-permute-start(bf16[64,128]{1,0:T(8,128)(2,1)S(1)} %get-tuple-element.13), channel_id=1, source_target_pairs={{1,0},{2,1},{3,2},{4,3},{5,4},{6,5},{7,6},{8,7},{9,8},{10,9},{11,1... | collective-permute-start | bytes 49160 | tf_op jit(solution)/shard_map/ppermute | solution.py:342
  9.1 7.8 %collective-permute-start.2 = (f32[3,16]{1,0:T(4,128)S(1)}, f32[3,16]{1,0:T(4,128)S(1)}, u32[]{:S(2)}, u32[]{:S(2)}) collective-permute-start(f32[3,16]{1,0:T(4,128)S(1)} %get-tuple-element.11.own_scalars), channel_id=1, source_target_pairs={{0,192},{64,128},{128,64},{192,0},{1,193},{65,129},{129,65},{193,1... | collective-permute-start | bytes 584 | tf_op jit(solution)/shard_map/ppermute | solution.py:346
  17.0 0.5 collective-permute-start
  17.5 0.3 column_spectrum.1.own_ref
  17.8 0.4 collective-permute-done.2.scalars_3
  18.3 5.4 %collective-permute-done.1.scalars_2 = f32[3,16]{1,0:T(4,128)S(1)} collective-permute-done((f32[3,16]{1,0:T(4,128)S(1)}, f32[3,16]{1,0:T(4,128)S(1)}, u32[]{:S(2)}, u32[]{:S(2)}) %collective-permute-start.1) | collective-permute-done | bytes 224 | tf_op jit(solution)/shard_map/ppermute | solution.py:346
  23.7 13.8 %image.1 = (f32[64,128]{1,0:T(8,128)S(1)}, f32[64,1,128]{2,1,0:T(1,128)}) custom-call(s32[1]{0:T(128)} %bitcast.group_ref, f32[3,16]{1,0:T(4,128)S(1)} %get-tuple-element.11.own_scalars, f32[3,16]{1,0:T(4,128)S(1)} %collective-permute-done.scalars_1, f32[3,16]{1,0:T(4,128)S(1)} %collective-permute-done.1.scalars_2, ...), custom_call_target="tpu_custom_call" | custom-call | tf_op jit(solution)/shard_map/image/pallas_call | solution.py:223
  37.5 0.4 collective-permute-start.5
  37.9 0.9 %collective-permute-done.5 = f32[64,128]{1,0:T(8,128)S(1)} collective-permute-done((f32[64,128]{1,0:T(8,128)S(1)}, f32[64,128]{1,0:T(8,128)S(1)}, u32[]{:S(2)}, u32[]{:S(2)}) %collective-permute-start.5) | collective-permute-done | bytes 32800 | tf_op jit(solution)/shard_map/ppermute | solution.py:357
  38.8 0.6 collective-permute-start.6
  39.4 10.9 %all-to-all-start = ((f32[64,1,128]{2,1,0:T(1,128)}), f32[64,1,128]{2,1,0:T(1,128)S(1)}, u32[]{:S(2)}, u32[]{:S(2)}) async-start(f32[64,1,128]{2,1,0:T(1,128)} %get-tuple-element.15), calls=%async_computation | async-start | bytes 65536 | tf_op jit(solution)/shard_map/all_to_all | solution.py:359
  50.4 1.3 %collective-permute-start.8 = (f32[64,128]{1,0:T(8,128)S(1)}, f32[64,128]{1,0:T(8,128)S(1)}, u32[]{:S(2)}, u32[]{:S(2)}) collective-permute-start(f32[64,128]{1,0:T(8,128)S(1)} %add.7.grad_ref), channel_id=1, source_target_pairs={{1,0},{2,1},{3,2},{4,3},{5,4},{6,5},{7,6},{8,7},{9,8},{10,9},{11,1... | collective-permute-start | bytes 98312 | tf_op jit(solution)/shard_map/ppermute | solution.py:342
  51.7 4.0 %collective-permute-start.7 = (f32[64,128]{1,0:T(8,128)S(1)}, f32[64,128]{1,0:T(8,128)S(1)}, u32[]{:S(2)}, u32[]{:S(2)}) collective-permute-start(f32[64,128]{1,0:T(8,128)S(1)} %add.7.grad_ref), channel_id=1, source_target_pairs={{0,1},{1,2},{2,3},{3,4},{4,5},{5,6},{6,7},{7,8},{8,9},{9,10},{10,1... | collective-permute-start | bytes 98312 | tf_op jit(solution)/shard_map/ppermute | solution.py:342
  55.7 3.5 %all-to-all-done = f32[64,1,128]{2,1,0:T(1,128)S(1)} async-done(((f32[64,1,128]{2,1,0:T(1,128)}), f32[64,1,128]{2,1,0:T(1,128)S(1)}, u32[]{:S(2)}, u32[]{:S(2)}) %all-to-all-start) | async-done | bytes 32800 | tf_op jit(solution)/shard_map/all_to_all | solution.py:359
  59.3 6.4 %collective-permute-start.11 = (f32[1,128]{1,0:T(1,128)S(1)}, f32[1,128]{1,0:T(1,128)S(1)}, u32[]{:S(2)}, u32[]{:S(2)}) collective-permute-start(f32[1,128]{1,0:T(1,128)S(1)} %bitcast.8), channel_id=1, source_target_pairs={{0,192},{64,128},{128,64},{192,0},{1,193},{65,129},{129,65},{193,1... | collective-permute-start | bytes 1544 | tf_op jit(solution)/shard_map/ppermute | solution.py:346
  65.7 1.0 %collective-permute-start.10 = (f32[1,128]{1,0:T(1,128)S(1)}, f32[1,128]{1,0:T(1,128)S(1)}, u32[]{:S(2)}, u32[]{:S(2)}) collective-permute-start(f32[1,128]{1,0:T(1,128)S(1)} %bitcast.9), channel_id=1, source_target_pairs={{0,128},{64,192},{128,0},{192,64},{1,129},{65,193},{129,1},{193,65... | collective-permute-start | bytes 1544 | tf_op jit(solution)/shard_map/ppermute | solution.py:346
  66.7 1.5 %owned_gradient.1.grad_ref = f32[512,512]{1,0:T(8,128)} custom-call(f32[64,128]{1,0:T(8,128)S(1)} %add.7.grad_ref, f32[512,512]{1,0:T(8,128)S(1)} %copy-done.1, bf16[512,128]{1,0:T(8,128)(2,1)S(1)} %copy-done.9, bf16[128,512]{1,0:T(8,128)(2,1)S(1)} %copy-done.3), custom_call_target="tpu_custom_call" | custom-call | tf_op jit(solution)/shard_map/owned_gradient/pallas_call | solution.py:281
  68.2 3.8 %collective-permute-done.10.far_ref = f32[1,128]{1,0:T(1,128)S(1)} collective-permute-done((f32[1,128]{1,0:T(1,128)S(1)}, f32[1,128]{1,0:T(1,128)S(1)}, u32[]{:S(2)}, u32[]{:S(2)}) %collective-permute-start.10) | collective-permute-done | bytes 544 | tf_op jit(solution)/shard_map/ppermute | solution.py:346
  72.1 2.4 %last_steps.1 = (f32[512,512]{1,0:T(8,128)}, f32[1,16]{1,0:T(1,128)}, f32[1,1]{1,0:T(1,128)}) custom-call(s32[1]{0:T(128)} %bitcast.group_ref, f32[64,128]{1,0:T(8,128)S(1)} %collective-permute-done.7.before_ref, f32[64,128]{1,0:T(8,128)S(1)} %collective-permute-done.8.after_ref, f32[512,512]{1,0:T(8,128)S(1)} %copy-done.1, ...), custom_call_target="tpu_custom_call", output_to_operand_aliasing={{0}: (6, {})} | custom-call | tf_op jit(solution)/shard_map/last_steps/pallas_call | solution.py:314
  (40 shorter events, 0.2 us)
Async XLA Ops:
  3.5 14.0 %copy-start.1 = (f32[512,512]{1,0:T(8,128)S(1)}, f32[512,512]{1,0:T(8,128)}, u32[]{:S(2)}) copy-start(f32[512,512]{1,0:T(8,128)} %logits_ref.5) | copy-start | bytes 3145732
  3.5 14.0 %copy-start.5 = (bf16[512,128]{1,0:T(8,128)(2,1)S(1)}, bf16[512,128]{1,0:T(8,128)(2,1)}, u32[]{:S(2)}) copy-start(bf16[512,128]{1,0:T(8,128)(2,1)} %constant.26.clone.table_ref) | copy-start | bytes 393220
  3.5 20.2 %copy-start.7 = (bf16[128,1024]{1,0:T(8,128)(2,1)S(1)}, bf16[128,1024]{1,0:T(8,128)(2,1)}, u32[]{:S(2)}) copy-start(bf16[128,1024]{1,0:T(8,128)(2,1)} %constant.30.clone.inverse_ref) | copy-start | bytes 786436
  3.5 20.2 %copy-start.8 = (bf16[128,640]{1,0:T(8,128)(2,1)S(1)}, bf16[128,640]{1,0:T(8,128)(2,1)}, u32[]{:S(2)}) copy-start(bf16[128,640]{1,0:T(8,128)(2,1)} %constant.27.clone.row_forward_ref) | copy-start | bytes 491524
  3.5 20.2 %copy-start.10 = (bf16[128,512]{1,0:T(8,128)(2,1)S(1)}, bf16[128,512]{1,0:T(8,128)(2,1)}, u32[]{:S(2)}) copy-start(bf16[128,512]{1,0:T(8,128)(2,1)} %constant.29.clone.row_inverse_t_ref) | copy-start | bytes 393220
  3.5 20.2 %copy-start.11 = (bf16[512,128]{1,0:T(8,128)(2,1)S(1)}, bf16[512,128]{1,0:T(8,128)(2,1)}, u32[]{:S(2)}) copy-start(bf16[512,128]{1,0:T(8,128)(2,1)} %constant.28.clone.row_inverse_ref) | copy-start | bytes 393220
  3.7 20.0 %copy-start.2 = (s32[512,512]{1,0:T(8,128)S(1)}, s32[512,512]{1,0:T(8,128)}, u32[]{:S(2)}) copy-start(s32[512,512]{1,0:T(8,128)} %target_ref.1) | copy-start | bytes 3145732
  3.7 19.9 %collective-permute-start.3 = (bf16[64,128]{1,0:T(8,128)(2,1)S(1)}, bf16[64,128]{1,0:T(8,128)(2,1)S(1)}, u32[]{:S(2)}, u32[]{:S(2)}) collective-permute-start(bf16[64,128]{1,0:T(8,128)(2,1)S(1)} %get-tuple-element.12), channel_id=1, source_target_pairs={{0,1},{1,2},{2,3},{3,4},{4,5},{5,6},{6,7},{7,8},{8,9},{9,10},{10,1... | collective-permute-start | bytes 49160 | tf_op jit(solution)/shard_map/ppermute | solution.py:342
  7.8 15.8 %collective-permute-start.4 = (bf16[64,128]{1,0:T(8,128)(2,1)S(1)}, bf16[64,128]{1,0:T(8,128)(2,1)S(1)}, u32[]{:S(2)}, u32[]{:S(2)}) collective-permute-start(bf16[64,128]{1,0:T(8,128)(2,1)S(1)} %get-tuple-element.13), channel_id=1, source_target_pairs={{1,0},{2,1},{3,2},{4,3},{5,4},{6,5},{7,6},{8,7},{9,8},{10,9},{11,1... | collective-permute-start | bytes 49160 | tf_op jit(solution)/shard_map/ppermute | solution.py:342
  9.1 9.1 %collective-permute-start.2 = (f32[3,16]{1,0:T(4,128)S(1)}, f32[3,16]{1,0:T(4,128)S(1)}, u32[]{:S(2)}, u32[]{:S(2)}) collective-permute-start(f32[3,16]{1,0:T(4,128)S(1)} %get-tuple-element.11.own_scalars), channel_id=1, source_target_pairs={{0,192},{64,128},{128,64},{192,0},{1,193},{65,129},{129,65},{193,1... | collective-permute-start | bytes 584 | tf_op jit(solution)/shard_map/ppermute | solution.py:346
  17.0 6.6 %collective-permute-start.1 = (f32[3,16]{1,0:T(4,128)S(1)}, f32[3,16]{1,0:T(4,128)S(1)}, u32[]{:S(2)}, u32[]{:S(2)}) collective-permute-start(f32[3,16]{1,0:T(4,128)S(1)} %get-tuple-element.11.own_scalars), channel_id=1, source_target_pairs={{0,128},{64,192},{128,0},{192,64},{1,129},{65,193},{129,1},{193,65... | collective-permute-start | bytes 584 | tf_op jit(solution)/shard_map/ppermute | solution.py:346
  17.0 6.6 %collective-permute-start = (f32[3,16]{1,0:T(4,128)S(1)}, f32[3,16]{1,0:T(4,128)S(1)}, u32[]{:S(2)}, u32[]{:S(2)}) collective-permute-start(f32[3,16]{1,0:T(4,128)S(1)} %get-tuple-element.11.own_scalars), channel_id=1, source_target_pairs={{0,64},{64,0},{128,192},{192,128},{1,65},{65,1},{129,193},{193,129... | collective-permute-start | bytes 584 | tf_op jit(solution)/shard_map/ppermute | solution.py:346
  17.5 6.2 %copy-start.6 = (bf16[1024,128]{1,0:T(8,128)(2,1)S(1)}, bf16[1024,128]{1,0:T(8,128)(2,1)}, u32[]{:S(2)}) copy-start(bf16[1024,128]{1,0:T(8,128)(2,1)} %constant.31.clone.inverse_t_ref) | copy-start | bytes 786436
  37.5 29.2 %copy-start.3 = (bf16[128,512]{1,0:T(8,128)(2,1)S(1)}, bf16[128,512]{1,0:T(8,128)(2,1)}, u32[]{:S(2)}) copy-start(bf16[128,512]{1,0:T(8,128)(2,1)} %constant.33.clone.column_ref) | copy-start | bytes 393220
  37.5 29.2 %copy-start.9 = (bf16[512,128]{1,0:T(8,128)(2,1)S(1)}, bf16[512,128]{1,0:T(8,128)(2,1)}, u32[]{:S(2)}) copy-start(bf16[512,128]{1,0:T(8,128)(2,1)} %constant.32.clone.row_ref) | copy-start | bytes 393220
  37.5 1.3 %collective-permute-start.5 = (f32[64,128]{1,0:T(8,128)S(1)}, f32[64,128]{1,0:T(8,128)S(1)}, u32[]{:S(2)}, u32[]{:S(2)}) collective-permute-start(f32[64,128]{1,0:T(8,128)S(1)} %get-tuple-element.14), channel_id=1, source_target_pairs={{0,64},{64,0},{128,192},{192,128},{1,65},{65,1},{129,193},{193,129... | collective-permute-start | bytes 98312 | tf_op jit(solution)/shard_map/ppermute | solution.py:357
  38.8 11.6 %collective-permute-start.6 = (f32[64,128]{1,0:T(8,128)S(1)}, f32[64,128]{1,0:T(8,128)S(1)}, u32[]{:S(2)}, u32[]{:S(2)}) collective-permute-start(f32[64,128]{1,0:T(8,128)S(1)} %add.6), channel_id=1, source_target_pairs={{0,128},{64,192},{128,0},{192,64},{1,129},{65,193},{129,1},{193,65... | collective-permute-start | bytes 98312 | tf_op jit(solution)/shard_map/ppermute | solution.py:358
  39.4 19.8 %all-to-all-start = ((f32[64,1,128]{2,1,0:T(1,128)}), f32[64,1,128]{2,1,0:T(1,128)S(1)}, u32[]{:S(2)}, u32[]{:S(2)}) async-start(f32[64,1,128]{2,1,0:T(1,128)} %get-tuple-element.15), calls=%async_computation | async-start | bytes 65536 | tf_op jit(solution)/shard_map/all_to_all | solution.py:359
  50.4 21.7 %collective-permute-start.8 = (f32[64,128]{1,0:T(8,128)S(1)}, f32[64,128]{1,0:T(8,128)S(1)}, u32[]{:S(2)}, u32[]{:S(2)}) collective-permute-start(f32[64,128]{1,0:T(8,128)S(1)} %add.7.grad_ref), channel_id=1, source_target_pairs={{1,0},{2,1},{3,2},{4,3},{5,4},{6,5},{7,6},{8,7},{9,8},{10,9},{11,1... | collective-permute-start | bytes 98312 | tf_op jit(solution)/shard_map/ppermute | solution.py:342
  51.7 20.4 %collective-permute-start.7 = (f32[64,128]{1,0:T(8,128)S(1)}, f32[64,128]{1,0:T(8,128)S(1)}, u32[]{:S(2)}, u32[]{:S(2)}) collective-permute-start(f32[64,128]{1,0:T(8,128)S(1)} %add.7.grad_ref), channel_id=1, source_target_pairs={{0,1},{1,2},{2,3},{3,4},{4,5},{5,6},{6,7},{7,8},{8,9},{9,10},{10,1... | collective-permute-start | bytes 98312 | tf_op jit(solution)/shard_map/ppermute | solution.py:342
  59.3 12.8 %copy-start.12 = (bf16[128,128]{1,0:T(8,128)(2,1)S(1)}, bf16[128,128]{1,0:T(8,128)(2,1)}, u32[]{:S(2)}) copy-start(bf16[128,128]{1,0:T(8,128)(2,1)} %constant.34.clone.row_ref) | copy-start | bytes 98308
  59.3 9.0 %collective-permute-start.11 = (f32[1,128]{1,0:T(1,128)S(1)}, f32[1,128]{1,0:T(1,128)S(1)}, u32[]{:S(2)}, u32[]{:S(2)}) collective-permute-start(f32[1,128]{1,0:T(1,128)S(1)} %bitcast.8), channel_id=1, source_target_pairs={{0,192},{64,128},{128,64},{192,0},{1,193},{65,129},{129,65},{193,1... | collective-permute-start | bytes 1544 | tf_op jit(solution)/shard_map/ppermute | solution.py:346
  65.7 6.3 %collective-permute-start.10 = (f32[1,128]{1,0:T(1,128)S(1)}, f32[1,128]{1,0:T(1,128)S(1)}, u32[]{:S(2)}, u32[]{:S(2)}) collective-permute-start(f32[1,128]{1,0:T(1,128)S(1)} %bitcast.9), channel_id=1, source_target_pairs={{0,128},{64,192},{128,0},{192,64},{1,129},{65,193},{129,1},{193,65... | collective-permute-start | bytes 1544 | tf_op jit(solution)/shard_map/ppermute | solution.py:346
  66.7 5.4 %collective-permute-start.9 = (f32[1,128]{1,0:T(1,128)S(1)}, f32[1,128]{1,0:T(1,128)S(1)}, u32[]{:S(2)}, u32[]{:S(2)}) collective-permute-start(f32[1,128]{1,0:T(1,128)S(1)} %bitcast.10), channel_id=1, source_target_pairs={{0,64},{64,0},{128,192},{192,128},{1,65},{65,1},{129,193},{193,129... | collective-permute-start | bytes 1544 | tf_op jit(solution)/shard_map/ppermute | solution.py:346
  (4 other events, 3.5 us)

commit v3 on v2

v3 whole, which is shorter than its diff:
```python
import functools

import numpy as np
import jax
import jax.numpy as jnp
from jax import lax
from jax.experimental import pallas as pl
from jax.experimental.pallas import tpu as pltpu
from jax.sharding import PartitionSpec as P

FREQS = 64
RADIUS = 20
MARGIN = 64
COLS = 512
TILE_ROWS = 512
FRAME = 640
SOURCES = 64
GROUPS = 4
PER_GROUP = SOURCES // GROUPS
ROWS = TILE_ROWS // GROUPS
MIB = 1024 * 1024
STEEPNESS = 12.0
THRESHOLD = 0.2
STEP = 16
F32 = jnp.float32
BF16 = jnp.bfloat16


def angles(length_used, offset, period):
    position = np.arange(length_used, dtype=np.int32)[:, None] + offset
    frequency = np.arange(FREQS, dtype=np.int32)[None, :] - FREQS // 2
    cycles = np.mod(position * frequency, period).astype(np.float32)
    angle_value = (cycles * np.float32(2.0 * 3.141592653589793 / period)).astype(np.float64)
    return np.cos(angle_value).astype(np.float32), np.sin(angle_value).astype(np.float32)


def make_tables():
    column_cosine, column_sine = angles(COLS, 0, COLS)
    column_forward = np.concatenate([column_cosine, -column_sine], 1)
    frame_cosine, frame_sine = angles(FRAME, 0, FRAME)
    row_forward = np.concatenate([frame_cosine.T, -frame_sine.T], 0)
    owned_cosine, owned_sine = angles(TILE_ROWS, MARGIN, FRAME)
    row_inverse = np.concatenate([owned_cosine, owned_sine], 1) / np.float32(FRAME)
    cosine_scaled = column_cosine.T / np.float32(COLS)
    sine_scaled = column_sine.T / np.float32(COLS)
    upper_block = np.concatenate([cosine_scaled, sine_scaled], 1)
    lower_block = np.concatenate([-sine_scaled, cosine_scaled], 1)
    column_inverse = np.concatenate([upper_block, lower_block], 0)
    chunked = column_inverse.reshape(2 * FREQS, 2, COLS // 128, 128).transpose(0, 2, 1, 3)
    chunked = chunked.reshape(2 * FREQS, 2 * COLS)
    rounded = lambda a: np.ascontiguousarray(a).astype(BF16)
    return [rounded(a) for a in (column_forward, row_forward, row_inverse, chunked)]


COLUMN_FORWARD, ROW_FORWARD, ROW_INVERSE, COLUMN_INVERSE = make_tables()


def stacked(table):
    return np.concatenate([table[:, c:c + 128] for c in range(0, table.shape[1], 128)], 0)


PARTS = [ROW_INVERSE, stacked(ROW_INVERSE.T), COLUMN_INVERSE.T, stacked(COLUMN_INVERSE), stacked(ROW_FORWARD)]
IMAGE_TABLE = np.ascontiguousarray(np.concatenate(PARTS, 0))
INVERSE_T_AT = 2 * TILE_ROWS
INVERSE_AT = INVERSE_T_AT + 2 * COLS
FORWARD_AT = INVERSE_AT + 8 * 128


def dot(a, b):
    return jnp.dot(a, b, preferred_element_type=F32)


def halves_sign(rows, left, right):
    lane = lax.broadcasted_iota(jnp.int32, (rows, 128), 1)
    return jnp.where(lane < FREQS, F32(left), F32(right))


def edge_kernel(group_ref, logits_ref, table_ref, weights_ref, shifts_ref, edge_out, packed_out,
                rows, table, weights, shifts, semaphores):
    start = jnp.where(group_ref[0] % 2 == 0, TILE_ROWS - MARGIN, 0)
    rows_from = logits_ref.at[pl.ds(pl.multiple_of(start, MARGIN), MARGIN), :]
    pairs = ((rows_from, rows), (table_ref, table), (weights_ref, weights), (shifts_ref, shifts))
    copies = [pltpu.make_async_copy(a, b, semaphores.at[i]) for i, (a, b) in enumerate(pairs)]
    for copy in copies:
        copy.start()
    for copy in copies:
        copy.wait()
    edge_out[...] = dot(jax.nn.sigmoid(rows[...]).astype(BF16), table[...]).astype(BF16)
    packed_out[0:1] = weights[...]
    packed_out[1:3] = shifts[...].astype(F32)


def edge_spectrum(group, mask_logits, weights, shifts):
    return pl.pallas_call(
        edge_kernel,
        in_specs=[pl.BlockSpec(memory_space=pltpu.SMEM)] + [pl.BlockSpec(memory_space=pltpu.HBM)] * 4,
        out_shape=[jax.ShapeDtypeStruct((MARGIN, 128), BF16), jax.ShapeDtypeStruct((3, PER_GROUP), F32)],
        scratch_shapes=[
            pltpu.VMEM((MARGIN, COLS), F32), pltpu.VMEM((COLS, 128), BF16),
            pltpu.VMEM((1, PER_GROUP), F32), pltpu.VMEM((2, PER_GROUP), jnp.int32),
            pltpu.SemaphoreType.DMA((4,)),
        ],
        compiler_params=pltpu.CompilerParams(vmem_limit_bytes=60 * MIB),
        name="edge_spectrum",
    )(group, mask_logits, jnp.asarray(COLUMN_FORWARD), weights.reshape(1, PER_GROUP), shifts.T)


def column_kernel(logits_ref, table_ref, image_table_ref, out_ref, image_table_out, semaphore):
    copy = pltpu.make_async_copy(image_table_ref, image_table_out, semaphore)
    copy.start()
    out_ref[...] = dot(jax.nn.sigmoid(logits_ref[...]).astype(BF16), table_ref[...]).astype(BF16)
    copy.wait()


def column_spectrum(mask_logits):
    return pl.pallas_call(
        column_kernel,
        in_specs=[pl.BlockSpec(), pl.BlockSpec(), pl.BlockSpec(memory_space=pltpu.HBM)],
        out_shape=[jax.ShapeDtypeStruct((TILE_ROWS, 128), BF16), jax.ShapeDtypeStruct(IMAGE_TABLE.shape, BF16)],
        scratch_shapes=[pltpu.SemaphoreType.DMA],
        compiler_params=pltpu.CompilerParams(vmem_limit_bytes=8 * MIB),
        name="column_spectrum",
    )(mask_logits, jnp.asarray(COLUMN_FORWARD), jnp.asarray(IMAGE_TABLE))


def pupil(scalars, step, j):
    ref, i = scalars[j % GROUPS], step * (STEP // GROUPS) + j // GROUPS
    across, along = ref[1, i], ref[2, i]
    row = lax.broadcasted_iota(jnp.int32, (FREQS, 128), 0) - FREQS // 2
    lane = jnp.bitwise_and(lax.broadcasted_iota(jnp.int32, (FREQS, 128), 1), FREQS - 1) - FREQS // 2
    row, lane = row.astype(F32) - across, lane.astype(F32) - along
    return row * row + lane * lane <= F32(RADIUS * RADIUS)


def image_kernel(group_ref, own_scalars, scalars_1, scalars_2, scalars_3, own_ref, near_ref, other_ref, target_ref, table_ref, out_ref, sums_ref,
                 fields_ref, row_field_ref, intensity_ref, cotangent_ref, spectra_ref, terms_ref, grad_ref, rounded_ref, frame_ref):
    scalars = [own_scalars, scalars_1, scalars_2, scalars_3]
    def beside(start, count):
        return jnp.concatenate([table_ref[start + 128 * i:start + 128 * (i + 1), :] for i in range(count)], 1)

    row_inverse = table_ref.at[pl.ds(pl.multiple_of(group_ref[0] * ROWS, ROWS), ROWS), :]
    row_inverse_t = table_ref.at[pl.ds(pl.multiple_of(TILE_ROWS + group_ref[0] * 128, 128), 128), :]
    even = group_ref[0] % 2 == 0
    frame_ref[MARGIN:MARGIN + TILE_ROWS] = own_ref[...]

    @pl.when(even)
    def _():
        frame_ref[:MARGIN] = near_ref[...]
        frame_ref[MARGIN + TILE_ROWS:] = other_ref[...]

    @pl.when(jnp.logical_not(even))
    def _():
        frame_ref[:MARGIN] = other_ref[...]
        frame_ref[MARGIN + TILE_ROWS:] = near_ref[...]

    product = dot(beside(FORWARD_AT, FRAME // 128), frame_ref[...])
    swapped = pltpu.roll(product[FREQS:], FREQS, 1)
    spectrum = (product[:FREQS] + halves_sign(FREQS, -1.0, 1.0) * swapped).astype(BF16).astype(F32)
    spectra_ref[:FREQS] = spectrum
    spectra_ref[FREQS:] = pltpu.roll(spectrum, FREQS, 1) * halves_sign(FREQS, -1.0, 1.0)
    intensity_ref[...] = jnp.zeros_like(intensity_ref)

    steps = SOURCES // STEP

    def image_rows(step):
        blocks = []
        for j in range(STEP):
            inside = pupil(scalars, step, j)
            inside = jnp.concatenate([inside, inside], 0)
            blocks.append(jnp.where(inside, spectra_ref[...], F32(0)).astype(BF16))
        row_field = dot(row_inverse[...], jnp.concatenate(blocks, 1)).astype(BF16)
        for j in range(STEP):
            start = pl.multiple_of((step * STEP + j) * ROWS, ROWS)
            row_field_ref[pl.ds(start, ROWS), :] = row_field[:, 128 * j:128 * (j + 1)]

    def weight(step, j):
        return scalars[j % GROUPS][0, step * (STEP // GROUPS) + j // GROUPS]

    image_rows(0)

    @pl.loop(0, steps)
    def _(step):
        start = pl.multiple_of(step * (STEP * ROWS), STEP * ROWS)
        row_field = row_field_ref[pl.ds(start, STEP * ROWS), :]
        for n in range(4):
            fields = dot(row_field, beside(INVERSE_AT + 256 * n, 2))
            fields_ref[pl.ds(start, STEP * ROWS), 256 * n:256 * (n + 1)] = fields
            power = fields[:, :128] * fields[:, :128] + fields[:, 128:] * fields[:, 128:]
            total = weight(step, 0) * power[:ROWS]
            for j in range(1, STEP):
                total = total + weight(step, j) * power[j * ROWS:(j + 1) * ROWS]
            intensity_ref[:, 128 * n:128 * (n + 1)] += total
        image_rows(jnp.minimum(step + 1, steps - 1))

    printed = jax.nn.sigmoid(F32(STEEPNESS) * (intensity_ref[...] - F32(THRESHOLD)))
    error_value = printed - target_ref[...].astype(F32)
    cotangent_ref[...] = F32(2.0 * STEEPNESS) * error_value * printed * (F32(1.0) - printed)
    error_rows = jnp.sum(error_value * error_value, 0, keepdims=True)
    error_lanes = (error_rows[:, :128] + error_rows[:, 128:256]) + (error_rows[:, 256:384] + error_rows[:, 384:])
    error_sum = jnp.sum(error_lanes, 1, keepdims=True)
    grad_ref[...] = jnp.zeros_like(grad_ref)

    rounded_ref[...] = jnp.zeros_like(rounded_ref)

    def add_block_grad(step):
        block_grad = dot(row_inverse_t[...], rounded_ref[...])
        total = jnp.zeros((2 * FREQS, 128), F32)
        for j in range(STEP):
            inside = pupil(scalars, step, j)
            inside = jnp.concatenate([inside, inside], 0)
            total = total + jnp.where(inside, block_grad[:, 128 * j:128 * (j + 1)], F32(0))
        grad_ref[...] += total

    @pl.loop(0, steps)
    def _(step):
        start = pl.multiple_of(step * (STEP * ROWS), STEP * ROWS)
        add_block_grad(jnp.maximum(step - 1, 0))
        row_grad = None
        for n in range(4):
            cot = cotangent_ref[:, 128 * n:128 * (n + 1)]
            parts = []
            for j in range(STEP):
                scaling = (F32(2.0) * weight(step, j)) * cot
                at = pl.multiple_of(start + j * ROWS, ROWS)
                fields = fields_ref[pl.ds(at, ROWS), 256 * n:256 * (n + 1)]
                parts.append((jnp.concatenate([scaling, scaling], 1) * fields).astype(BF16))
            part = dot(jnp.concatenate(parts, 0), table_ref[INVERSE_T_AT + 256 * n:INVERSE_T_AT + 256 * (n + 1), :])
            row_grad = part if row_grad is None else row_grad + part
        row_field = row_field_ref[pl.ds(start, STEP * ROWS), :].astype(F32)
        terms = row_grad * row_field
        rounded = row_grad.astype(BF16)
        for j in range(STEP):
            terms_ref[pl.ds(step * STEP + j, 1), :] = jnp.sum(terms[j * ROWS:(j + 1) * ROWS], 0, keepdims=True)
            rounded_ref[:, 128 * j:128 * (j + 1)] = rounded[j * ROWS:(j + 1) * ROWS]

    add_block_grad(steps - 1)
    grads = grad_ref[...]
    out_ref[...] = grads[:FREQS] + halves_sign(FREQS, 1.0, -1.0) * pltpu.roll(grads[FREQS:], FREQS, 1)
    term = jnp.sum(terms_ref[...], 1, keepdims=True)
    row = lax.broadcasted_iota(jnp.int32, (SOURCES, 128), 0)
    lane = lax.broadcasted_iota(jnp.int32, (SOURCES, 128), 1)
    wanted = (row % GROUPS) * PER_GROUP + row // GROUPS
    term_row = jnp.sum(jnp.where(wanted == lane, term, F32(0)), 0, keepdims=True)
    lane = lax.broadcasted_iota(jnp.int32, (1, 128), 1)
    own = group_ref[0]
    for bit, width in ((1, PER_GROUP), (2, 2 * PER_GROUP)):
        swapped = jnp.where((lane // width) % 2 == 0, pltpu.roll(term_row, 128 - width, 1),
                            pltpu.roll(term_row, width, 1))
        term_row = jnp.where(jnp.bitwise_and(own, bit) != 0, swapped, term_row)
    term_row = jnp.where(lane < SOURCES, term_row, F32(0))
    sums_ref[...] = jnp.broadcast_to(jnp.where(lane == SOURCES, error_sum, term_row)[None], sums_ref.shape)


def image(group, scalars, own, near, other, target, table, peers):
    fixed = lambda i, g: (0, 0)
    whole = lambda shape: pl.BlockSpec(shape, fixed)
    return pl.pallas_call(
        image_kernel,
        grid_spec=pltpu.PrefetchScalarGridSpec(
            num_scalar_prefetch=1,
            grid=(1,),
            in_specs=[
                *[pl.BlockSpec(memory_space=pltpu.SMEM)] * GROUPS,
                whole((TILE_ROWS, 128)), whole((MARGIN, 128)), whole((MARGIN, 128)),
                pl.BlockSpec((ROWS, COLS), lambda i, g: (g[0], 0)),
                whole(IMAGE_TABLE.shape),
            ],
            out_specs=[whole((FREQS, 128)), pl.BlockSpec((peers, 1, 128), lambda i, g: (0, 0, 0))],
            scratch_shapes=[
                pltpu.VMEM((SOURCES * ROWS, 2 * COLS), F32),
                pltpu.VMEM((SOURCES * ROWS, 128), BF16),
                pltpu.VMEM((ROWS, COLS), F32),
                pltpu.VMEM((ROWS, COLS), F32),
                pltpu.VMEM((128, 128), F32),
                pltpu.VMEM((SOURCES, 128), F32),
                pltpu.VMEM((128, 128), F32),
                pltpu.VMEM((ROWS, STEP * 128), BF16),
                pltpu.VMEM((FRAME, 128), BF16),
            ],
        ),
        out_shape=[jax.ShapeDtypeStruct((FREQS, 128), F32), jax.ShapeDtypeStruct((peers, 1, 128), F32)],
        compiler_params=pltpu.CompilerParams(vmem_limit_bytes=44 * MIB),
        name="image",
    )(group, *scalars, own, near, other, target, table)


def split_dot(table, x):
    high = x.astype(BF16)
    low = (x - high.astype(F32)).astype(BF16)
    return dot(jnp.concatenate([table, table], 1), jnp.concatenate([high, low], 0))


def dot_split(x, table):
    high = x.astype(BF16)
    low = (x - high.astype(F32)).astype(BF16)
    return dot(jnp.concatenate([high, low], 1), jnp.concatenate([table, table], 0))


def product_gradient(spectrum_grad):
    lower = pltpu.roll(spectrum_grad, FREQS, 1) * halves_sign(FREQS, 1.0, -1.0)
    return jnp.concatenate([spectrum_grad, lower], 0)


def owned_kernel(grad_ref, logits_ref, row_ref, column_ref, out_ref, edges_ref, slope_ref):
    column_grad = split_dot(row_ref[...], product_gradient(grad_ref[...]))
    opening = jax.nn.sigmoid(logits_ref[...])
    slope = opening * (F32(1.0) - opening)
    out = dot_split(column_grad, column_ref[...]) * slope
    out_ref[...] = out
    edges_ref[:MARGIN] = out[:MARGIN]
    edges_ref[MARGIN:] = out[TILE_ROWS - MARGIN:]
    slope_ref[:MARGIN] = slope[:MARGIN]
    slope_ref[MARGIN:] = slope[TILE_ROWS - MARGIN:]


def owned_gradient(spectrum_grad, mask_logits):
    return pl.pallas_call(
        owned_kernel,
        out_shape=[jax.ShapeDtypeStruct((n, COLS), F32) for n in (TILE_ROWS, 2 * MARGIN, 2 * MARGIN)],
        compiler_params=pltpu.CompilerParams(vmem_limit_bytes=10 * MIB),
        name="owned_gradient",
    )(spectrum_grad, mask_logits,
      jnp.asarray(np.ascontiguousarray(ROW_FORWARD.T[MARGIN:MARGIN + TILE_ROWS])),
      jnp.asarray(np.ascontiguousarray(COLUMN_FORWARD.T)))


def last_kernel(group_ref, near_ref, other_ref, edges_ref, slope_ref, row_ref, column_ref, own_ref, beside_ref,
                far_ref, across_ref, weights_ref, grad_ref, out_ref, weight_grad_ref, loss_ref,
                rows_ref, semaphores, *, pixels):
    del grad_ref
    even = group_ref[0] % 2 == 0
    before = jnp.where(even, near_ref[...], other_ref[...])
    after = jnp.where(even, other_ref[...], near_ref[...])
    column_grad = jnp.concatenate([split_dot(row_ref[:MARGIN], product_gradient(before)),
                                   split_dot(row_ref[MARGIN:], product_gradient(after))], 0)
    rows_ref[...] = edges_ref[...] + dot_split(column_grad, column_ref[...]) * slope_ref[...]
    copies = [
        pltpu.make_async_copy(rows_ref.at[pl.ds(0, MARGIN), :], out_ref.at[pl.ds(0, MARGIN), :], semaphores.at[0]),
        pltpu.make_async_copy(rows_ref.at[pl.ds(MARGIN, MARGIN), :],
                              out_ref.at[pl.ds(TILE_ROWS - MARGIN, MARGIN), :], semaphores.at[1]),
    ]
    for copy in copies:
        copy.start()
    total = (own_ref[...] + beside_ref[...]) + (far_ref[...] + across_ref[...])
    row = total
    for bit, width in ((1, PER_GROUP), (2, 2 * PER_GROUP)):
        row = jnp.where(jnp.bitwise_and(group_ref[0], bit) != 0, pltpu.roll(row, 128 - width, 1), row)
    weight_grad_ref[...] = row[:, :PER_GROUP] / (F32(2.0) * weights_ref[...]) / F32(pixels)
    loss_ref[...] = total[:, SOURCES:SOURCES + 1] / F32(pixels)
    for copy in copies:
        copy.wait()


def last_steps(group, near, other, edges, slope, grad, sums, weights, pixels):
    rows = np.concatenate([ROW_FORWARD.T[MARGIN + TILE_ROWS:], ROW_FORWARD.T[:MARGIN]], 0)
    block = pl.BlockSpec()
    hbm = pl.BlockSpec(memory_space=pltpu.HBM)
    return pl.pallas_call(
        functools.partial(last_kernel, pixels=pixels),
        in_specs=[pl.BlockSpec(memory_space=pltpu.SMEM)] + [block] * 11 + [hbm],
        out_specs=[hbm, block, block],
        out_shape=[jax.ShapeDtypeStruct((TILE_ROWS, COLS), F32), jax.ShapeDtypeStruct((1, PER_GROUP), F32),
                   jax.ShapeDtypeStruct((1, 1), F32)],
        scratch_shapes=[pltpu.VMEM((2 * MARGIN, COLS), F32), pltpu.SemaphoreType.DMA((2,))],
        input_output_aliases={12: 0},
        compiler_params=pltpu.CompilerParams(vmem_limit_bytes=4 * MIB),
        name="last_steps",
    )(group, near, other, edges, slope, jnp.asarray(np.ascontiguousarray(rows)),
      jnp.asarray(np.ascontiguousarray(COLUMN_FORWARD.T)), *sums, weights.reshape(1, PER_GROUP), grad)


def from_tile_beside(x):
    peers = lax.axis_size("tile")
    pairs = [(s * peers + i, s * peers + j) for s in range(GROUPS) for i in range(peers)
             for j in [i + 1 - 2 * (s % 2)] if 0 <= j < peers]
    return lax.ppermute(x, ("src", "tile"), pairs)


def from_group(x, d):
    return lax.ppermute(x, "src", [(i, i ^ d) for i in range(GROUPS)])


def from_core(x):
    return from_group(x, 1)


def from_chip(x):
    return from_group(x, 2)


def on_device(mask_logits, target, weights, shifts):
    peers = lax.axis_size("tile")
    group = lax.axis_index("src").astype(jnp.int32).reshape(1)
    edge, packed = edge_spectrum(group, mask_logits, weights, shifts)
    near = from_tile_beside(edge)
    packed_far = from_chip(packed)
    packed_core = from_core(packed)
    own, table = column_spectrum(mask_logits)
    near, packed_far, own = lax.optimization_barrier((near, packed_far, own))
    scalars = [packed, packed_core, packed_far, from_core(packed_far)]
    partial, sums = image(group, scalars, own, near, from_core(near), target, table, peers)
    chip = partial + from_core(partial)
    far = from_chip(chip)
    sums = lax.all_to_all(sums, "tile", 0, 0, tiled=True)
    spectrum_grad = chip + far
    near_grad = from_tile_beside(spectrum_grad)
    sums = jnp.sum(sums, 0)
    sums_far = from_chip(sums)
    grad, edges, slope = owned_gradient(spectrum_grad, mask_logits)
    near_grad, sums_far, edges = lax.optimization_barrier((near_grad, sums_far, edges))
    sums = [sums, from_core(sums), sums_far, from_core(sums_far)]
    mask_grad, weight_grad, loss = last_steps(
        group, near_grad, from_core(near_grad), edges, slope, grad, sums, weights, TILE_ROWS * COLS * peers)
    return mask_grad, weight_grad.reshape(PER_GROUP), loss.reshape(())


def solution(mesh):
    placed = (P("tile", None), P("tile", None), P("src"), P("src", None))
    return jax.shard_map(
        on_device,
        mesh=mesh,
        in_specs=placed,
        out_specs=(P("tile", None), P("src"), P()),
        check_vma=False,
    )
```

time: 74.8 us -> 70.3 us (0.940)
  starting transfers between devices: 38.4 us -> 33.5 us
  Pallas kernels: 18.2 us -> 19.4 us
  local copies, waits for them, and re-layouts: 2.86 us -> 1.88 us
    all_to_all x1, waiting for transfers between devices: 3.51 us -> 7.51 us  [on_device(): sums = lax.all_to_all(sums, 'tile', 0, 0, tiled=True)]
    ppermute x12, waiting for transfers between devices: 10.5 us -> 6.91 us  [the longest x10 6.9 us: from_group(): return lax.ppermute(x, 'src', [(i, i ^ d) for i in range(GROUPS)])]
    ppermute x12, starting transfers between devices: 27.5 us -> 24 us  [the longest x10 21.4 us: from_group(): return lax.ppermute(x, 'src', [(i, i ^ d) for i in range(GROUPS)])]
    all_to_all x1, starting transfers between devices: 10.9 us -> 9.47 us  [on_device(): sums = lax.all_to_all(sums, 'tile', 0, 0, tiled=True)]
    pallas_call x4, Pallas kernels: 4.45 us -> 5.56 us  [the longest x1 1.87 us: edge_spectrum(): pl.pallas_call(edge_kernel, in_specs=[pl.BlockSpec(memory_space=pltpu.SME...]
    unnamed x30 -> x18, local copies, waits for them, and re-layouts: 2.86 us -> 1.88 us
  transfers between devices with their start and end apart: 13 -> 13, of which waited for: 5 -> 7; matrix products, arithmetic and copies ran while one was open for 0% -> 0% of each run, Pallas kernels for 2% -> 3%
where the time goes in v3:
time: 70.3 us; the launch traced here: 70.1 us
  starting transfers between devices  33.5 us (48%)
  Pallas kernels  19.4 us (28%)
  waiting for transfers between devices  14.4 us (20%)
  local copies, waits for them, and re-layouts  1.88 us (3%)
  between operations  0.77 us (1%)
    ppermute x10, starting transfers between devices, from_group(): return lax.ppermute(x, 'src', [(i, i ^ d) for i in range(GROUPS)])  21.4 us
    pallas_call x1, Pallas kernels, image(): pl.pallas_call(image_kernel, grid_spec=pltpu.PrefetchScalarGridSpec(num_s...  13.9 us
    all_to_all x1, starting transfers between devices, on_device(): sums = lax.all_to_all(sums, 'tile', 0, 0, tiled=True)  9.47 us
    all_to_all x1, waiting for transfers between devices, on_device(): sums = lax.all_to_all(sums, 'tile', 0, 0, tiled=True)  7.51 us
    ppermute x10, waiting for transfers between devices, from_group(): return lax.ppermute(x, 'src', [(i, i ^ d) for i in range(GROUPS)])  6.9 us
    ppermute x2, starting transfers between devices, from_tile_beside(): return lax.ppermute(x, ('src', 'tile'), pairs)  2.58 us
    unnamed x18, local copies, waits for them, and re-layouts  1.88 us
    pallas_call x1, Pallas kernels, edge_spectrum(): pl.pallas_call(edge_kernel, in_specs=[pl.BlockSpec(memory_space=pltpu.SME...  1.87 us
  transfers between devices with their start and end apart: 13, of which 7 were waited for; matrix products, arithmetic and copies ran while one was open for 0% of the time, Pallas kernels for 3%

profile of v3, /device:TPU:1, one launch (start us, length us, event | category | flops | bytes accessed | tf_op | source)
XLA Modules:
  0.0 70.1 jit_solution(3014360664690733734)
XLA Ops:
  0.7 1.9 %edge_spectrum.1 = (bf16[64,128]{1,0:T(8,128)(2,1)}, f32[3,16]{1,0:T(4,128)}) custom-call(s32[1]{0:T(128)} %bitcast.group_ref, f32[512,512]{1,0:T(8,128)} %logits_ref.5, bf16[512,128]{1,0:T(8,128)(2,1)} %constant.18.clone.table_ref, f32[1,16]{1,0:T(1,128)} %bitcast.6, s32[2,16]{1,0:T(2,128)} %bitcast.11), custom_call_target="tpu_custom_call" | custom-call | tf_op jit(solution)/shard_map/edge_spectrum/pallas_call | solution.py:94
  2.5 1.3 %collective-permute-start.1 = (bf16[64,128]{1,0:T(8,128)(2,1)}, bf16[64,128]{1,0:T(8,128)(2,1)S(1)}, u32[]{:S(2)}, u32[]{:S(2)}) collective-permute-start(bf16[64,128]{1,0:T(8,128)(2,1)} %get-tuple-element.22), channel_id=1, source_target_pairs={{0,1},{1,2},{2,3},{3,4},{4,5},{5,6},{6,7},{7,8},{8,9},{9,10},{10,1... | collective-permute-start | bytes 49160 | tf_op jit(solution)/shard_map/ppermute | solution.py:376
  3.9 7.8 %collective-permute-start.2 = (f32[3,16]{1,0:T(4,128)S(1)}, f32[3,16]{1,0:T(4,128)S(1)}, u32[]{:S(2)}, u32[]{:S(2)}) collective-permute-start(f32[3,16]{1,0:T(4,128)S(1)} %copy-done.7), channel_id=1, source_target_pairs={{0,128},{64,192},{128,0},{192,64},{1,129},{65,193},{129,1},{193,65... | collective-permute-start | bytes 584 | tf_op jit(solution)/shard_map/ppermute | solution.py:380
  11.7 1.2 %copy-done.2 = bf16[3712,128]{1,0:T(8,128)(2,1)S(1)} copy-done((bf16[3712,128]{1,0:T(8,128)(2,1)S(1)}, bf16[3712,128]{1,0:T(8,128)(2,1)}, u32[]{:S(2)}) %copy-start.2) | copy-done | bytes 950296
  12.9 0.6 column_spectrum.1
  13.5 3.2 %collective-permute-start.4 = (bf16[64,128]{1,0:T(8,128)(2,1)S(1)}, bf16[64,128]{1,0:T(8,128)(2,1)S(1)}, u32[]{:S(2)}, u32[]{:S(2)}) collective-permute-start(bf16[64,128]{1,0:T(8,128)(2,1)S(1)} %collective-permute-done.1.near_ref), channel_id=1, source_target_pairs={{0,64},{64,0},{128,192},{192,128},{1,65},{65,1},{129,193},{193,129... | collective-permute-start | bytes 49160 | tf_op jit(solution)/shard_map/ppermute | solution.py:380
  16.8 0.4 collective-permute-start.3
  17.2 0.7 collective-permute-done.scalars_1
  18.1 13.9 %image.1 = (f32[64,128]{1,0:T(8,128)S(1)}, f32[64,1,128]{2,1,0:T(1,128)}) custom-call(s32[1]{0:T(128)} %bitcast.group_ref, f32[3,16]{1,0:T(4,128)S(1)} %copy-done.7, f32[3,16]{1,0:T(4,128)S(1)} %collective-permute-done.scalars_1, f32[3,16]{1,0:T(4,128)S(1)} %collective-permute-done.2.scalars_2, f32[3,16]{1,0:T(4,128)S(1)} %collective-permute-done.3.scalars_3, ...), custom_call_target="tpu_custom_call" | custom-call | tf_op jit(solution)/shard_map/image/pallas_call | solution.py:257
  32.0 0.3 collective-permute-start.5
  32.3 0.9 %collective-permute-done.5 = f32[64,128]{1,0:T(8,128)S(1)} collective-permute-done((f32[64,128]{1,0:T(8,128)S(1)}, f32[64,128]{1,0:T(8,128)S(1)}, u32[]{:S(2)}, u32[]{:S(2)}) %collective-permute-start.5) | collective-permute-done | bytes 32800 | tf_op jit(solution)/shard_map/ppermute | solution.py:380
  33.2 5.3 %collective-permute-start.6 = (f32[64,128]{1,0:T(8,128)S(1)}, f32[64,128]{1,0:T(8,128)S(1)}, u32[]{:S(2)}, u32[]{:S(2)}) collective-permute-start(f32[64,128]{1,0:T(8,128)S(1)} %add.6), channel_id=1, source_target_pairs={{0,128},{64,192},{128,0},{192,64},{1,129},{65,193},{129,1},{193,65... | collective-permute-start | bytes 98312 | tf_op jit(solution)/shard_map/ppermute | solution.py:380
  38.5 9.5 %all-to-all-start = ((f32[64,1,128]{2,1,0:T(1,128)}), f32[64,1,128]{2,1,0:T(1,128)S(1)}, u32[]{:S(2)}, u32[]{:S(2)}) async-start(f32[64,1,128]{2,1,0:T(1,128)} %get-tuple-element.29), calls=%async_computation | async-start | bytes 65536 | tf_op jit(solution)/shard_map/all_to_all | solution.py:404
  48.0 1.3 %collective-permute-start.7 = (f32[64,128]{1,0:T(8,128)S(1)}, f32[64,128]{1,0:T(8,128)S(1)}, u32[]{:S(2)}, u32[]{:S(2)}) collective-permute-start(f32[64,128]{1,0:T(8,128)S(1)} %add.7.grad_ref), channel_id=1, source_target_pairs={{0,1},{1,2},{2,3},{3,4},{4,5},{5,6},{6,7},{7,8},{8,9},{9,10},{10,1... | collective-permute-start | bytes 98312 | tf_op jit(solution)/shard_map/ppermute | solution.py:376
  49.3 7.5 %all-to-all-done = f32[64,1,128]{2,1,0:T(1,128)S(1)} async-done(((f32[64,1,128]{2,1,0:T(1,128)}), f32[64,1,128]{2,1,0:T(1,128)S(1)}, u32[]{:S(2)}, u32[]{:S(2)}) %all-to-all-start) | async-done | bytes 32800 | tf_op jit(solution)/shard_map/all_to_all | solution.py:404
  56.9 0.5 collective-permute-start.8
  57.4 1.5 %owned_gradient.1 = (f32[512,512]{1,0:T(8,128)}, f32[128,512]{1,0:T(8,128)S(1)}, f32[128,512]{1,0:T(8,128)S(1)}) custom-call(f32[64,128]{1,0:T(8,128)S(1)} %add.7.grad_ref, f32[512,512]{1,0:T(8,128)S(1)} %copy-done, bf16[512,128]{1,0:T(8,128)(2,1)S(1)} %copy-done.5, bf16[128,512]{1,0:T(8,128)(2,1)S(1)} %copy-done.4), custom_call_target="tpu_custom_call" | custom-call | tf_op jit(solution)/shard_map/owned_gradient/pallas_call | solution.py:317
  58.9 4.4 %collective-permute-done.8.far_ref = f32[1,128]{1,0:T(1,128)S(1)} collective-permute-done((f32[1,128]{1,0:T(1,128)S(1)}, f32[1,128]{1,0:T(1,128)S(1)}, u32[]{:S(2)}, u32[]{:S(2)}) %collective-permute-start.8) | collective-permute-done | bytes 544 | tf_op jit(solution)/shard_map/ppermute | solution.py:380
  63.3 3.2 %collective-permute-start.9 = (f32[64,128]{1,0:T(8,128)S(1)}, f32[64,128]{1,0:T(8,128)S(1)}, u32[]{:S(2)}, u32[]{:S(2)}) collective-permute-start(f32[64,128]{1,0:T(8,128)S(1)} %collective-permute-done.7.near_ref), channel_id=1, source_target_pairs={{0,64},{64,0},{128,192},{192,128},{1,65},{65,1},{129,193},{193,129... | collective-permute-start | bytes 98312 | tf_op jit(solution)/shard_map/ppermute | solution.py:380
  66.5 0.5 collective-permute-start.11
  67.0 0.7 collective-permute-done.10.beside_ref
  67.7 0.2 collective-permute-done.11.across_ref
  67.8 0.7 copy-done.8
  68.5 1.6 %last_steps.1 = (f32[512,512]{1,0:T(8,128)}, f32[1,16]{1,0:T(1,128)}, f32[1,1]{1,0:T(1,128)}) custom-call(s32[1]{0:T(128)} %bitcast.group_ref, f32[64,128]{1,0:T(8,128)S(1)} %collective-permute-done.7.near_ref, f32[64,128]{1,0:T(8,128)S(1)} %collective-permute-done.9.other_ref, ...), custom_call_target="tpu_custom_call", output_to_operand_aliasing={{0}: (12, {})} | custom-call | tf_op jit(solution)/shard_map/last_steps/pallas_call | solution.py:358
  (28 shorter events, 0.4 us)
Async XLA Ops:
  0.6 11.1 %copy-start = (f32[512,512]{1,0:T(8,128)S(1)}, f32[512,512]{1,0:T(8,128)}, u32[]{:S(2)}) copy-start(f32[512,512]{1,0:T(8,128)} %logits_ref.5) | copy-start | bytes 3145732
  0.6 11.0 %copy-start.3 = (bf16[512,128]{1,0:T(8,128)(2,1)S(1)}, bf16[512,128]{1,0:T(8,128)(2,1)}, u32[]{:S(2)}) copy-start(bf16[512,128]{1,0:T(8,128)(2,1)} %constant.18.clone.table_ref) | copy-start | bytes 393220
  2.5 1.3 %copy-start.7 = (f32[3,16]{1,0:T(4,128)S(1)}, f32[3,16]{1,0:T(4,128)}, u32[]{:S(2)}) copy-start(f32[3,16]{1,0:T(4,128)} %get-tuple-element.21.own_scalars) | copy-start | bytes 580
  2.5 10.9 %collective-permute-start.1 = (bf16[64,128]{1,0:T(8,128)(2,1)}, bf16[64,128]{1,0:T(8,128)(2,1)S(1)}, u32[]{:S(2)}, u32[]{:S(2)}) collective-permute-start(bf16[64,128]{1,0:T(8,128)(2,1)} %get-tuple-element.22), channel_id=1, source_target_pairs={{0,1},{1,2},{2,3},{3,4},{4,5},{5,6},{6,7},{7,8},{8,9},{9,10},{10,1... | collective-permute-start | bytes 49160 | tf_op jit(solution)/shard_map/ppermute | solution.py:376
  3.9 14.2 %copy-start.1 = (s32[512,512]{1,0:T(8,128)S(1)}, s32[512,512]{1,0:T(8,128)}, u32[]{:S(2)}) copy-start(s32[512,512]{1,0:T(8,128)} %target_ref.1) | copy-start | bytes 3145732
  3.9 9.6 %collective-permute-start.2 = (f32[3,16]{1,0:T(4,128)S(1)}, f32[3,16]{1,0:T(4,128)S(1)}, u32[]{:S(2)}, u32[]{:S(2)}) collective-permute-start(f32[3,16]{1,0:T(4,128)S(1)} %copy-done.7), channel_id=1, source_target_pairs={{0,128},{64,192},{128,0},{192,64},{1,129},{65,193},{129,1},{193,65... | collective-permute-start | bytes 584 | tf_op jit(solution)/shard_map/ppermute | solution.py:380
  11.7 1.2 %copy-start.2 = (bf16[3712,128]{1,0:T(8,128)(2,1)S(1)}, bf16[3712,128]{1,0:T(8,128)(2,1)}, u32[]{:S(2)}) copy-start(bf16[3712,128]{1,0:T(8,128)(2,1)} %constant.19.clone.image_table_ref) | copy-start | bytes 2850820
  13.5 4.6 %collective-permute-start.4 = (bf16[64,128]{1,0:T(8,128)(2,1)S(1)}, bf16[64,128]{1,0:T(8,128)(2,1)S(1)}, u32[]{:S(2)}, u32[]{:S(2)}) collective-permute-start(bf16[64,128]{1,0:T(8,128)(2,1)S(1)} %collective-permute-done.1.near_ref), channel_id=1, source_target_pairs={{0,64},{64,0},{128,192},{192,128},{1,65},{65,1},{129,193},{193,129... | collective-permute-start | bytes 49160 | tf_op jit(solution)/shard_map/ppermute | solution.py:380
  16.7 1.2 %collective-permute-start = (f32[3,16]{1,0:T(4,128)S(1)}, f32[3,16]{1,0:T(4,128)S(1)}, u32[]{:S(2)}, u32[]{:S(2)}) collective-permute-start(f32[3,16]{1,0:T(4,128)S(1)} %copy-done.7), channel_id=1, source_target_pairs={{0,64},{64,0},{128,192},{192,128},{1,65},{65,1},{129,193},{193,129... | collective-permute-start | bytes 584 | tf_op jit(solution)/shard_map/ppermute | solution.py:380
  16.8 1.2 %collective-permute-start.3 = (f32[3,16]{1,0:T(4,128)S(1)}, f32[3,16]{1,0:T(4,128)S(1)}, u32[]{:S(2)}, u32[]{:S(2)}) collective-permute-start(f32[3,16]{1,0:T(4,128)S(1)} %collective-permute-done.2.scalars_2), channel_id=1, source_target_pairs={{0,64},{64,0},{128,192},{192,128},{1,65},{65,1},{129,193},{193,129... | collective-permute-start | bytes 584 | tf_op jit(solution)/shard_map/ppermute | solution.py:380
  32.0 25.4 %copy-start.4 = (bf16[128,512]{1,0:T(8,128)(2,1)S(1)}, bf16[128,512]{1,0:T(8,128)(2,1)}, u32[]{:S(2)}) copy-start(bf16[128,512]{1,0:T(8,128)(2,1)} %constant.21.clone.column_ref) | copy-start | bytes 393220
  32.0 25.4 %copy-start.5 = (bf16[512,128]{1,0:T(8,128)(2,1)S(1)}, bf16[512,128]{1,0:T(8,128)(2,1)}, u32[]{:S(2)}) copy-start(bf16[512,128]{1,0:T(8,128)(2,1)} %constant.20.clone.row_ref) | copy-start | bytes 393220
  32.0 1.2 %collective-permute-start.5 = (f32[64,128]{1,0:T(8,128)S(1)}, f32[64,128]{1,0:T(8,128)S(1)}, u32[]{:S(2)}, u32[]{:S(2)}) collective-permute-start(f32[64,128]{1,0:T(8,128)S(1)} %get-tuple-element.28), channel_id=1, source_target_pairs={{0,64},{64,0},{128,192},{192,128},{1,65},{65,1},{129,193},{193,129... | collective-permute-start | bytes 98312 | tf_op jit(solution)/shard_map/ppermute | solution.py:380
  33.2 14.8 %collective-permute-start.6 = (f32[64,128]{1,0:T(8,128)S(1)}, f32[64,128]{1,0:T(8,128)S(1)}, u32[]{:S(2)}, u32[]{:S(2)}) collective-permute-start(f32[64,128]{1,0:T(8,128)S(1)} %add.6), channel_id=1, source_target_pairs={{0,128},{64,192},{128,0},{192,64},{1,129},{65,193},{129,1},{193,65... | collective-permute-start | bytes 98312 | tf_op jit(solution)/shard_map/ppermute | solution.py:380
  38.5 18.3 %all-to-all-start = ((f32[64,1,128]{2,1,0:T(1,128)}), f32[64,1,128]{2,1,0:T(1,128)S(1)}, u32[]{:S(2)}, u32[]{:S(2)}) async-start(f32[64,1,128]{2,1,0:T(1,128)} %get-tuple-element.29), calls=%async_computation | async-start | bytes 65536 | tf_op jit(solution)/shard_map/all_to_all | solution.py:404
  48.0 15.3 %collective-permute-start.7 = (f32[64,128]{1,0:T(8,128)S(1)}, f32[64,128]{1,0:T(8,128)S(1)}, u32[]{:S(2)}, u32[]{:S(2)}) collective-permute-start(f32[64,128]{1,0:T(8,128)S(1)} %add.7.grad_ref), channel_id=1, source_target_pairs={{0,1},{1,2},{2,3},{3,4},{4,5},{5,6},{6,7},{7,8},{8,9},{9,10},{10,1... | collective-permute-start | bytes 98312 | tf_op jit(solution)/shard_map/ppermute | solution.py:376
  56.9 11.0 %copy-start.6 = (bf16[128,128]{1,0:T(8,128)(2,1)S(1)}, bf16[128,128]{1,0:T(8,128)(2,1)}, u32[]{:S(2)}) copy-start(bf16[128,128]{1,0:T(8,128)(2,1)} %constant.22.clone.row_ref) | copy-start | bytes 98308
  56.9 6.4 %collective-permute-start.8 = (f32[1,128]{1,0:T(1,128)S(1)}, f32[1,128]{1,0:T(1,128)S(1)}, u32[]{:S(2)}, u32[]{:S(2)}) collective-permute-start(f32[1,128]{1,0:T(1,128)S(1)} %bitcast.8), channel_id=1, source_target_pairs={{0,128},{64,192},{128,0},{192,64},{1,129},{65,193},{129,1},{193,65... | collective-permute-start | bytes 1544 | tf_op jit(solution)/shard_map/ppermute | solution.py:380
  63.3 4.5 %collective-permute-start.9 = (f32[64,128]{1,0:T(8,128)S(1)}, f32[64,128]{1,0:T(8,128)S(1)}, u32[]{:S(2)}, u32[]{:S(2)}) collective-permute-start(f32[64,128]{1,0:T(8,128)S(1)} %collective-permute-done.7.near_ref), channel_id=1, source_target_pairs={{0,64},{64,0},{128,192},{192,128},{1,65},{65,1},{129,193},{193,129... | collective-permute-start | bytes 98312 | tf_op jit(solution)/shard_map/ppermute | solution.py:380
  66.5 1.2 %collective-permute-start.10 = (f32[1,128]{1,0:T(1,128)S(1)}, f32[1,128]{1,0:T(1,128)S(1)}, u32[]{:S(2)}, u32[]{:S(2)}) collective-permute-start(f32[1,128]{1,0:T(1,128)S(1)} %bitcast.9), channel_id=1, source_target_pairs={{0,64},{64,0},{128,192},{192,128},{1,65},{65,1},{129,193},{193,129... | collective-permute-start | bytes 1544 | tf_op jit(solution)/shard_map/ppermute | solution.py:380
  66.5 1.3 %collective-permute-start.11 = (f32[1,128]{1,0:T(1,128)S(1)}, f32[1,128]{1,0:T(1,128)S(1)}, u32[]{:S(2)}, u32[]{:S(2)}) collective-permute-start(f32[1,128]{1,0:T(1,128)S(1)} %collective-permute-done.8.far_ref), channel_id=1, source_target_pairs={{0,64},{64,0},{128,192},{192,128},{1,65},{65,1},{129,193},{193,129... | collective-permute-start | bytes 1544 | tf_op jit(solution)/shard_map/ppermute | solution.py:380
  67.8 0.7 copy-start.8

commit v4 on v3

--- a/solution.py
+++ b/solution.py
@@ -132,7 +132,7 @@
     return row * row + lane * lane <= F32(RADIUS * RADIUS)
 
 
-def image_kernel(group_ref, own_scalars, scalars_1, scalars_2, scalars_3, own_ref, near_ref, other_ref, target_ref, table_ref, out_ref, sums_ref,
+def image_kernel(group_ref, own_scalars, scalars_1, scalars_2, scalars_3, own_ref, near_ref, other_ref, target_ref, table_ref, out_ref,
                  fields_ref, row_field_ref, intensity_ref, cotangent_ref, spectra_ref, terms_ref, grad_ref, rounded_ref, frame_ref):
     scalars = [own_scalars, scalars_1, scalars_2, scalars_3]
     def beside(start, count):
@@ -235,7 +235,7 @@
 
     add_block_grad(steps - 1)
     grads = grad_ref[...]
-    out_ref[...] = grads[:FREQS] + halves_sign(FREQS, 1.0, -1.0) * pltpu.roll(grads[FREQS:], FREQS, 1)
+    out_ref[:FREQS] = grads[:FREQS] + halves_sign(FREQS, 1.0, -1.0) * pltpu.roll(grads[FREQS:], FREQS, 1)
     term = jnp.sum(terms_ref[...], 1, keepdims=True)
     row = lax.broadcasted_iota(jnp.int32, (SOURCES, 128), 0)
     lane = lax.broadcasted_iota(jnp.int32, (SOURCES, 128), 1)
@@ -248,10 +248,10 @@
                             pltpu.roll(term_row, width, 1))
         term_row = jnp.where(jnp.bitwise_and(own, bit) != 0, swapped, term_row)
     term_row = jnp.where(lane < SOURCES, term_row, F32(0))
-    sums_ref[...] = jnp.broadcast_to(jnp.where(lane == SOURCES, error_sum, term_row)[None], sums_ref.shape)
-
-
-def image(group, scalars, own, near, other, target, table, peers):
+    out_ref[FREQS:] = jnp.broadcast_to(jnp.where(lane == SOURCES, error_sum, term_row), (8, 128))
+
+
+def image(group, scalars, own, near, other, target, table):
     fixed = lambda i, g: (0, 0)
     whole = lambda shape: pl.BlockSpec(shape, fixed)
     return pl.pallas_call(
@@ -265,7 +265,7 @@
                 pl.BlockSpec((ROWS, COLS), lambda i, g: (g[0], 0)),
                 whole(IMAGE_TABLE.shape),
             ],
-            out_specs=[whole((FREQS, 128)), pl.BlockSpec((peers, 1, 128), lambda i, g: (0, 0, 0))],
+            out_specs=whole((FREQS + 8, 128)),
             scratch_shapes=[
                 pltpu.VMEM((SOURCES * ROWS, 2 * COLS), F32),
                 pltpu.VMEM((SOURCES * ROWS, 128), BF16),
@@ -278,10 +278,25 @@
                 pltpu.VMEM((FRAME, 128), BF16),
             ],
         ),
-        out_shape=[jax.ShapeDtypeStruct((FREQS, 128), F32), jax.ShapeDtypeStruct((peers, 1, 128), F32)],
+        out_shape=jax.ShapeDtypeStruct((FREQS + 8, 128), F32),
         compiler_params=pltpu.CompilerParams(vmem_limit_bytes=44 * MIB),
         name="image",
     )(group, *scalars, own, near, other, target, table)
+
+
+def total_kernel(chip_ref, far_ref, grad_ref, sums_ref):
+    grad_ref[...] = chip_ref[:FREQS] + far_ref[:FREQS]
+    row = chip_ref[FREQS:FREQS + 1] + far_ref[FREQS:FREQS + 1]
+    sums_ref[...] = jnp.broadcast_to(row[None], sums_ref.shape)
+
+
+def total(chip, far, peers):
+    return pl.pallas_call(
+        total_kernel,
+        out_shape=[jax.ShapeDtypeStruct((FREQS, 128), F32), jax.ShapeDtypeStruct((peers, 1, 128), F32)],
+        compiler_params=pltpu.CompilerParams(vmem_limit_bytes=1 * MIB),
+        name="total",
+    )(chip, far)
 
 
 def split_dot(table, x):
@@ -324,8 +339,8 @@
       jnp.asarray(np.ascontiguousarray(COLUMN_FORWARD.T)))
 
 
-def last_kernel(group_ref, near_ref, other_ref, edges_ref, slope_ref, row_ref, column_ref, own_ref, beside_ref,
-                far_ref, across_ref, weights_ref, grad_ref, out_ref, weight_grad_ref, loss_ref,
+def last_kernel(group_ref, near_ref, other_ref, edges_ref, slope_ref, row_ref, column_ref, sums_ref,
+                packed_ref, grad_ref, out_ref, weight_grad_ref, loss_ref,
                 rows_ref, semaphores, *, pixels):
     del grad_ref
     even = group_ref[0] % 2 == 0
@@ -341,32 +356,32 @@
     ]
     for copy in copies:
         copy.start()
-    total = (own_ref[...] + beside_ref[...]) + (far_ref[...] + across_ref[...])
+    total = jnp.sum(sums_ref[...], 0)
     row = total
     for bit, width in ((1, PER_GROUP), (2, 2 * PER_GROUP)):
         row = jnp.where(jnp.bitwise_and(group_ref[0], bit) != 0, pltpu.roll(row, 128 - width, 1), row)
-    weight_grad_ref[...] = row[:, :PER_GROUP] / (F32(2.0) * weights_ref[...]) / F32(pixels)
+    weight_grad_ref[...] = row[:, :PER_GROUP] / (F32(2.0) * packed_ref[0:1]) / F32(pixels)
     loss_ref[...] = total[:, SOURCES:SOURCES + 1] / F32(pixels)
     for copy in copies:
         copy.wait()
 
 
-def last_steps(group, near, other, edges, slope, grad, sums, weights, pixels):
+def last_steps(group, near, other, edges, slope, grad, sums, packed, pixels):
     rows = np.concatenate([ROW_FORWARD.T[MARGIN + TILE_ROWS:], ROW_FORWARD.T[:MARGIN]], 0)
     block = pl.BlockSpec()
     hbm = pl.BlockSpec(memory_space=pltpu.HBM)
     return pl.pallas_call(
         functools.partial(last_kernel, pixels=pixels),
-        in_specs=[pl.BlockSpec(memory_space=pltpu.SMEM)] + [block] * 11 + [hbm],
+        in_specs=[pl.BlockSpec(memory_space=pltpu.SMEM)] + [block] * 8 + [hbm],
         out_specs=[hbm, block, block],
         out_shape=[jax.ShapeDtypeStruct((TILE_ROWS, COLS), F32), jax.ShapeDtypeStruct((1, PER_GROUP), F32),
                    jax.ShapeDtypeStruct((1, 1), F32)],
         scratch_shapes=[pltpu.VMEM((2 * MARGIN, COLS), F32), pltpu.SemaphoreType.DMA((2,))],
-        input_output_aliases={12: 0},
+        input_output_aliases={9: 0},
         compiler_params=pltpu.CompilerParams(vmem_limit_bytes=4 * MIB),
         name="last_steps",
     )(group, near, other, edges, slope, jnp.asarray(np.ascontiguousarray(rows)),
-      jnp.asarray(np.ascontiguousarray(COLUMN_FORWARD.T)), *sums, weights.reshape(1, PER_GROUP), grad)
+      jnp.asarray(np.ascontiguousarray(COLUMN_FORWARD.T)), sums, packed, grad)
 
 
 def from_tile_beside(x):
@@ -398,19 +413,15 @@
     own, table = column_spectrum(mask_logits)
     near, packed_far, own = lax.optimization_barrier((near, packed_far, own))
     scalars = [packed, packed_core, packed_far, from_core(packed_far)]
-    partial, sums = image(group, scalars, own, near, from_core(near), target, table, peers)
+    partial = image(group, scalars, own, near, from_core(near), target, table)
     chip = partial + from_core(partial)
-    far = from_chip(chip)
+    spectrum_grad, sums = total(chip, from_chip(chip), peers)
+    near_grad = from_tile_beside(spectrum_grad)
     sums = lax.all_to_all(sums, "tile", 0, 0, tiled=True)
-    spectrum_grad = chip + far
-    near_grad = from_tile_beside(spectrum_grad)
-    sums = jnp.sum(sums, 0)
-    sums_far = from_chip(sums)
     grad, edges, slope = owned_gradient(spectrum_grad, mask_logits)
-    near_grad, sums_far, edges = lax.optimization_barrier((near_grad, sums_far, edges))
-    sums = [sums, from_core(sums), sums_far, from_core(sums_far)]
+    near_grad, edges = lax.optimization_barrier((near_grad, edges))
     mask_grad, weight_grad, loss = last_steps(
-        group, near_grad, from_core(near_grad), edges, slope, grad, sums, weights, TILE_ROWS * COLS * peers)
+        group, near_grad, from_core(near_grad), edges, slope, grad, sums, packed, TILE_ROWS * COLS * peers)
     return mask_grad, weight_grad.reshape(PER_GROUP), loss.reshape(())
 
 

time: 70.3 us -> 66.6 us (0.947)
  the two profiles are of different devices: /device:TPU:1 before, /device:TPU:2 now
where the time goes in v4:
time: 66.6 us; the launch traced here: 66.4 us
  starting transfers between devices  32.2 us (48%)
  Pallas kernels  19.5 us (29%)
  waiting for transfers between devices  12.7 us (19%)
  local copies, waits for them, and re-layouts  1.23 us (2%)
  between operations  0.78 us (1%)
    ppermute x7, starting transfers between devices, from_group(): return lax.ppermute(x, 'src', [(i, i ^ d) for i in range(GROUPS)])  15.1 us
    pallas_call x1, Pallas kernels, image(): pl.pallas_call(image_kernel, grid_spec=pltpu.PrefetchScalarGridSpec(num_s...  13.3 us
    all_to_all x1, starting transfers between devices, on_device(): sums = lax.all_to_all(sums, 'tile', 0, 0, tiled=True)  11.7 us
    all_to_all x1, waiting for transfers between devices, on_device(): sums = lax.all_to_all(sums, 'tile', 0, 0, tiled=True)  7.61 us
    ppermute x2, starting transfers between devices, from_tile_beside(): return lax.ppermute(x, ('src', 'tile'), pairs)  5.39 us
    ppermute x7, waiting for transfers between devices, from_group(): return lax.ppermute(x, 'src', [(i, i ^ d) for i in range(GROUPS)])  5.07 us
    pallas_call x1, Pallas kernels, edge_spectrum(): pl.pallas_call(edge_kernel, in_specs=[pl.BlockSpec(memory_space=pltpu.SME...  1.87 us
    pallas_call x1, Pallas kernels, last_steps(): pl.pallas_call(functools.partial(last_kernel, pixels=pixels), in_specs=[p...  1.6 us
  transfers between devices with their start and end apart: 10, of which 5 were waited for; matrix products, arithmetic and copies ran while one was open for 0% of the time, Pallas kernels for 3%

profile of v4, /device:TPU:2, one launch (start us, length us, event | category | flops | bytes accessed | tf_op | source)
XLA Modules:
  0.0 66.4 jit_solution(7819128727838570227)
XLA Ops:
  0.6 0.0 copy-start.3
  0.7 1.9 %edge_spectrum.1 = (bf16[64,128]{1,0:T(8,128)(2,1)}, f32[3,16]{1,0:T(4,128)}) custom-call(s32[1]{0:T(128)} %bitcast.group_ref, f32[512,512]{1,0:T(8,128)} %logits_ref.5, bf16[512,128]{1,0:T(8,128)(2,1)} %constant.16.clone.table_ref, f32[1,16]{1,0:T(1,128)} %bitcast.6, s32[2,16]{1,0:T(2,128)} %bitcast.5), custom_call_target="tpu_custom_call" | custom-call | tf_op jit(solution)/shard_map/edge_spectrum/pallas_call | solution.py:94
  2.5 3.5 %collective-permute-start.1 = (bf16[64,128]{1,0:T(8,128)(2,1)}, bf16[64,128]{1,0:T(8,128)(2,1)S(1)}, u32[]{:S(2)}, u32[]{:S(2)}) collective-permute-start(bf16[64,128]{1,0:T(8,128)(2,1)} %get-tuple-element.21), channel_id=1, source_target_pairs={{0,1},{1,2},{2,3},{3,4},{4,5},{5,6},{6,7},{7,8},{8,9},{9,10},{10,1... | collective-permute-start | bytes 49160 | tf_op jit(solution)/shard_map/ppermute | solution.py:391
  6.0 0.0 copy-start.1
  6.1 7.3 %collective-permute-start.2 = (f32[3,16]{1,0:T(4,128)S(1)}, f32[3,16]{1,0:T(4,128)S(1)}, u32[]{:S(2)}, u32[]{:S(2)}) collective-permute-start(f32[3,16]{1,0:T(4,128)S(1)} %copy-done.7), channel_id=1, source_target_pairs={{0,128},{64,192},{128,0},{192,64},{1,129},{65,193},{129,1},{193,65... | collective-permute-start | bytes 584 | tf_op jit(solution)/shard_map/ppermute | solution.py:395
  13.3 1.2 %copy-done.2 = bf16[3712,128]{1,0:T(8,128)(2,1)S(1)} copy-done((bf16[3712,128]{1,0:T(8,128)(2,1)S(1)}, bf16[3712,128]{1,0:T(8,128)(2,1)}, u32[]{:S(2)}) %copy-start.2) | copy-done | bytes 950296
  14.5 0.6 column_spectrum.1
  15.2 2.4 %collective-permute-start.4 = (bf16[64,128]{1,0:T(8,128)(2,1)S(1)}, bf16[64,128]{1,0:T(8,128)(2,1)S(1)}, u32[]{:S(2)}, u32[]{:S(2)}) collective-permute-start(bf16[64,128]{1,0:T(8,128)(2,1)S(1)} %collective-permute-done.1.near_ref), channel_id=1, source_target_pairs={{0,64},{64,0},{128,192},{192,128},{1,65},{65,1},{129,193},{193,129... | collective-permute-start | bytes 49160 | tf_op jit(solution)/shard_map/ppermute | solution.py:395
  17.5 0.5 collective-permute-start.3
  18.0 0.7 collective-permute-done.scalars_1
  18.7 0.2 collective-permute-done.3.scalars_3
  18.9 13.3 %image.1 = f32[72,128]{1,0:T(8,128)S(1)} custom-call(s32[1]{0:T(128)} %bitcast.group_ref, f32[3,16]{1,0:T(4,128)S(1)} %copy-done.7, f32[3,16]{1,0:T(4,128)S(1)} %collective-permute-done.scalars_1, f32[3,16]{1,0:T(4,128)S(1)} %collective-permute-done.2.scalars_2, f32[3,16]{1,0:T(4,128)S(1)} %collective-permute-done.3.scalars_3, ...), custom_call_target="tpu_custom_call" | custom-call | tf_op jit(solution)/shard_map/image/pallas_call | solution.py:257
  32.2 0.0 copy-start.4
  32.2 0.4 collective-permute-start.5
  32.6 0.9 %collective-permute-done.5 = f32[72,128]{1,0:T(8,128)S(1)} collective-permute-done((f32[72,128]{1,0:T(8,128)S(1)}, f32[72,128]{1,0:T(8,128)S(1)}, u32[]{:S(2)}, u32[]{:S(2)}) %collective-permute-start.5) | collective-permute-done | bytes 36896 | tf_op jit(solution)/shard_map/ppermute | solution.py:395
  33.5 4.5 %collective-permute-start.6 = (f32[72,128]{1,0:T(8,128)S(1)}, f32[72,128]{1,0:T(8,128)S(1)}, u32[]{:S(2)}, u32[]{:S(2)}) collective-permute-start(f32[72,128]{1,0:T(8,128)S(1)} %add.3.chip_ref), channel_id=1, source_target_pairs={{0,128},{64,192},{128,0},{192,64},{1,129},{65,193},{129,1},{193,65... | collective-permute-start | bytes 110600 | tf_op jit(solution)/shard_map/ppermute | solution.py:395
  38.0 3.4 %collective-permute-done.6.far_ref = f32[72,128]{1,0:T(8,128)S(1)} collective-permute-done((f32[72,128]{1,0:T(8,128)S(1)}, f32[72,128]{1,0:T(8,128)S(1)}, u32[]{:S(2)}, u32[]{:S(2)}) %collective-permute-start.6) | collective-permute-done | bytes 36896 | tf_op jit(solution)/shard_map/ppermute | solution.py:395
  41.4 0.6 total.1
  42.0 1.9 %collective-permute-start.7 = (f32[64,128]{1,0:T(8,128)S(1)}, f32[64,128]{1,0:T(8,128)S(1)}, u32[]{:S(2)}, u32[]{:S(2)}) collective-permute-start(f32[64,128]{1,0:T(8,128)S(1)} %get-tuple-element.27.grad_ref), channel_id=1, source_target_pairs={{0,1},{1,2},{2,3},{3,4},{4,5},{5,6},{6,7},{7,8},{8,9},{9,10},{10,1... | collective-permute-start | bytes 98312 | tf_op jit(solution)/shard_map/ppermute | solution.py:391
  43.9 11.7 %all-to-all-start = ((f32[64,1,128]{2,1,0:T(1,128)}), f32[64,1,128]{2,1,0:T(1,128)S(1)}, u32[]{:S(2)}, u32[]{:S(2)}) async-start(f32[64,1,128]{2,1,0:T(1,128)} %get-tuple-element.32), calls=%async_computation | async-start | bytes 65536 | tf_op jit(solution)/shard_map/all_to_all | solution.py:420
  55.7 0.0 copy-start.6
  55.7 1.5 %owned_gradient.1 = (f32[512,512]{1,0:T(8,128)}, f32[128,512]{1,0:T(8,128)S(1)}, f32[128,512]{1,0:T(8,128)S(1)}) custom-call(f32[64,128]{1,0:T(8,128)S(1)} %get-tuple-element.27.grad_ref, f32[512,512]{1,0:T(8,128)S(1)} %copy-done, bf16[512,128]{1,0:T(8,128)(2,1)S(1)} %copy-done.5, bf16[128,512]{1,0:T(8,128)(2,1)S(1)} %copy-done.4), custom_call_target="tpu_custom_call" | custom-call | tf_op jit(solution)/shard_map/owned_gradient/pallas_call | solution.py:332
  57.2 7.6 %all-to-all-done.sums_ref = f32[64,1,128]{2,1,0:T(1,128)S(1)} async-done(((f32[64,1,128]{2,1,0:T(1,128)}), f32[64,1,128]{2,1,0:T(1,128)S(1)}, u32[]{:S(2)}, u32[]{:S(2)}) %all-to-all-start) | async-done | bytes 32800 | tf_op jit(solution)/shard_map/all_to_all | solution.py:420
  64.8 1.6 %last_steps.1 = (f32[512,512]{1,0:T(8,128)}, f32[1,16]{1,0:T(1,128)}, f32[1,1]{1,0:T(1,128)}) custom-call(s32[1]{0:T(128)} %bitcast.group_ref, f32[64,128]{1,0:T(8,128)S(1)} %collective-permute-done.7.near_ref, f32[64,128]{1,0:T(8,128)S(1)} %collective-permute-done.8.other_ref, ...), custom_call_target="tpu_custom_call", output_to_operand_aliasing={{0}: (9, {})} | custom-call | tf_op jit(solution)/shard_map/last_steps/pallas_call | solution.py:373
  (19 shorter events, 0.0 us)
Async XLA Ops:
  0.6 12.7 %copy-start = (f32[512,512]{1,0:T(8,128)S(1)}, f32[512,512]{1,0:T(8,128)}, u32[]{:S(2)}) copy-start(f32[512,512]{1,0:T(8,128)} %logits_ref.5) | copy-start | bytes 3145732
  0.6 12.7 %copy-start.3 = (bf16[512,128]{1,0:T(8,128)(2,1)S(1)}, bf16[512,128]{1,0:T(8,128)(2,1)}, u32[]{:S(2)}) copy-start(bf16[512,128]{1,0:T(8,128)(2,1)} %constant.16.clone.table_ref) | copy-start | bytes 393220
  2.5 3.5 %copy-start.7 = (f32[3,16]{1,0:T(4,128)S(1)}, f32[3,16]{1,0:T(4,128)}, u32[]{:S(2)}) copy-start(f32[3,16]{1,0:T(4,128)} %get-tuple-element.20.own_scalars.packed_ref) | copy-start | bytes 580
  2.5 12.6 %collective-permute-start.1 = (bf16[64,128]{1,0:T(8,128)(2,1)}, bf16[64,128]{1,0:T(8,128)(2,1)S(1)}, u32[]{:S(2)}, u32[]{:S(2)}) collective-permute-start(bf16[64,128]{1,0:T(8,128)(2,1)} %get-tuple-element.21), channel_id=1, source_target_pairs={{0,1},{1,2},{2,3},{3,4},{4,5},{5,6},{6,7},{7,8},{8,9},{9,10},{10,1... | collective-permute-start | bytes 49160 | tf_op jit(solution)/shard_map/ppermute | solution.py:391
  6.0 12.8 %copy-start.1 = (s32[512,512]{1,0:T(8,128)S(1)}, s32[512,512]{1,0:T(8,128)}, u32[]{:S(2)}) copy-start(s32[512,512]{1,0:T(8,128)} %target_ref.1) | copy-start | bytes 3145732
  6.1 9.1 %collective-permute-start.2 = (f32[3,16]{1,0:T(4,128)S(1)}, f32[3,16]{1,0:T(4,128)S(1)}, u32[]{:S(2)}, u32[]{:S(2)}) collective-permute-start(f32[3,16]{1,0:T(4,128)S(1)} %copy-done.7), channel_id=1, source_target_pairs={{0,128},{64,192},{128,0},{192,64},{1,129},{65,193},{129,1},{193,65... | collective-permute-start | bytes 584 | tf_op jit(solution)/shard_map/ppermute | solution.py:395
  13.3 1.2 %copy-start.2 = (bf16[3712,128]{1,0:T(8,128)(2,1)S(1)}, bf16[3712,128]{1,0:T(8,128)(2,1)}, u32[]{:S(2)}) copy-start(bf16[3712,128]{1,0:T(8,128)(2,1)} %constant.17.clone.image_table_ref) | copy-start | bytes 2850820
  15.2 3.7 %collective-permute-start.4 = (bf16[64,128]{1,0:T(8,128)(2,1)S(1)}, bf16[64,128]{1,0:T(8,128)(2,1)S(1)}, u32[]{:S(2)}, u32[]{:S(2)}) collective-permute-start(bf16[64,128]{1,0:T(8,128)(2,1)S(1)} %collective-permute-done.1.near_ref), channel_id=1, source_target_pairs={{0,64},{64,0},{128,192},{192,128},{1,65},{65,1},{129,193},{193,129... | collective-permute-start | bytes 49160 | tf_op jit(solution)/shard_map/ppermute | solution.py:395
  17.5 1.2 %collective-permute-start = (f32[3,16]{1,0:T(4,128)S(1)}, f32[3,16]{1,0:T(4,128)S(1)}, u32[]{:S(2)}, u32[]{:S(2)}) collective-permute-start(f32[3,16]{1,0:T(4,128)S(1)} %copy-done.7), channel_id=1, source_target_pairs={{0,64},{64,0},{128,192},{192,128},{1,65},{65,1},{129,193},{193,129... | collective-permute-start | bytes 584 | tf_op jit(solution)/shard_map/ppermute | solution.py:395
  17.5 1.3 %collective-permute-start.3 = (f32[3,16]{1,0:T(4,128)S(1)}, f32[3,16]{1,0:T(4,128)S(1)}, u32[]{:S(2)}, u32[]{:S(2)}) collective-permute-start(f32[3,16]{1,0:T(4,128)S(1)} %collective-permute-done.2.scalars_2), channel_id=1, source_target_pairs={{0,64},{64,0},{128,192},{192,128},{1,65},{65,1},{129,193},{193,129... | collective-permute-start | bytes 584 | tf_op jit(solution)/shard_map/ppermute | solution.py:395
  18.9 36.8 %copy-start.5 = (bf16[512,128]{1,0:T(8,128)(2,1)S(1)}, bf16[512,128]{1,0:T(8,128)(2,1)}, u32[]{:S(2)}) copy-start(bf16[512,128]{1,0:T(8,128)(2,1)} %constant.18.clone.row_ref) | copy-start | bytes 393220
  32.2 23.4 %copy-start.4 = (bf16[128,512]{1,0:T(8,128)(2,1)S(1)}, bf16[128,512]{1,0:T(8,128)(2,1)}, u32[]{:S(2)}) copy-start(bf16[128,512]{1,0:T(8,128)(2,1)} %constant.19.clone.column_ref) | copy-start | bytes 393220
  32.2 1.3 %collective-permute-start.5 = (f32[72,128]{1,0:T(8,128)S(1)}, f32[72,128]{1,0:T(8,128)S(1)}, u32[]{:S(2)}, u32[]{:S(2)}) collective-permute-start(f32[72,128]{1,0:T(8,128)S(1)} %image.1), channel_id=1, source_target_pairs={{0,64},{64,0},{128,192},{192,128},{1,65},{65,1},{129,193},{193,129... | collective-permute-start | bytes 110600 | tf_op jit(solution)/shard_map/ppermute | solution.py:395
  33.5 7.9 %collective-permute-start.6 = (f32[72,128]{1,0:T(8,128)S(1)}, f32[72,128]{1,0:T(8,128)S(1)}, u32[]{:S(2)}, u32[]{:S(2)}) collective-permute-start(f32[72,128]{1,0:T(8,128)S(1)} %add.3.chip_ref), channel_id=1, source_target_pairs={{0,128},{64,192},{128,0},{192,64},{1,129},{65,193},{129,1},{193,65... | collective-permute-start | bytes 110600 | tf_op jit(solution)/shard_map/ppermute | solution.py:395
  42.0 15.2 %collective-permute-start.7 = (f32[64,128]{1,0:T(8,128)S(1)}, f32[64,128]{1,0:T(8,128)S(1)}, u32[]{:S(2)}, u32[]{:S(2)}) collective-permute-start(f32[64,128]{1,0:T(8,128)S(1)} %get-tuple-element.27.grad_ref), channel_id=1, source_target_pairs={{0,1},{1,2},{2,3},{3,4},{4,5},{5,6},{6,7},{7,8},{8,9},{9,10},{10,1... | collective-permute-start | bytes 98312 | tf_op jit(solution)/shard_map/ppermute | solution.py:391
  43.9 20.9 %all-to-all-start = ((f32[64,1,128]{2,1,0:T(1,128)}), f32[64,1,128]{2,1,0:T(1,128)S(1)}, u32[]{:S(2)}, u32[]{:S(2)}) async-start(f32[64,1,128]{2,1,0:T(1,128)} %get-tuple-element.32), calls=%async_computation | async-start | bytes 65536 | tf_op jit(solution)/shard_map/all_to_all | solution.py:420
  55.7 9.1 %copy-start.6 = (bf16[128,128]{1,0:T(8,128)(2,1)S(1)}, bf16[128,128]{1,0:T(8,128)(2,1)}, u32[]{:S(2)}) copy-start(bf16[128,128]{1,0:T(8,128)(2,1)} %constant.20.clone.row_ref) | copy-start | bytes 98308
  57.2 7.6 %collective-permute-start.8 = (f32[64,128]{1,0:T(8,128)S(1)}, f32[64,128]{1,0:T(8,128)S(1)}, u32[]{:S(2)}, u32[]{:S(2)}) collective-permute-start(f32[64,128]{1,0:T(8,128)S(1)} %collective-permute-done.7.near_ref), channel_id=1, source_target_pairs={{0,64},{64,0},{128,192},{192,128},{1,65},{65,1},{129,193},{193,129... | collective-permute-start | bytes 98312 | tf_op jit(solution)/shard_map/ppermute | solution.py:395

commit v5 on v4

--- a/solution.py
+++ b/solution.py
@@ -386,8 +386,14 @@
 
 def from_tile_beside(x):
     peers = lax.axis_size("tile")
-    pairs = [(s * peers + i, s * peers + j) for s in range(GROUPS) for i in range(peers)
-             for j in [i + 1 - 2 * (s % 2)] if 0 <= j < peers]
+    plane = peers // 4
+    pairs = []
+    for group in range(GROUPS):
+        for i in range(peers):
+            j = i + 1 - 2 * (group % 2)
+            if 0 <= j < peers:
+                other = group if i // plane == j // plane else group ^ 2
+                pairs.append((group * peers + i, other * peers + j))
     return lax.ppermute(x, ("src", "tile"), pairs)
 
 

time: 66.6 us -> 67 us (level)
  waiting for transfers between devices: 12.7 us -> 14.8 us
  starting transfers between devices: 32.2 us -> 30.5 us
    ppermute x7, waiting for transfers between devices: 5.07 us -> 7.14 us  [from_group(): return lax.ppermute(x, 'src', [(i, i ^ d) for i in range(GROUPS)])]
    all_to_all x1, starting transfers between devices: 11.7 us -> 10.8 us  [on_device(): sums = lax.all_to_all(sums, 'tile', 0, 0, tiled=True)]
    ppermute x7, starting transfers between devices: 15.1 us -> 14.3 us  [from_group(): return lax.ppermute(x, 'src', [(i, i ^ d) for i in range(GROUPS)])]
where the time goes in v5:
time: 67 us; the launch traced here: 66.8 us
  starting transfers between devices  30.5 us (46%)
  Pallas kernels  19.5 us (29%)
  waiting for transfers between devices  14.8 us (22%)
  local copies, waits for them, and re-layouts  1.23 us (2%)
  between operations  0.78 us (1%)
    ppermute x7, starting transfers between devices, from_group(): return lax.ppermute(x, 'src', [(i, i ^ d) for i in range(GROUPS)])  14.3 us
    pallas_call x1, Pallas kernels, image(): pl.pallas_call(image_kernel, grid_spec=pltpu.PrefetchScalarGridSpec(num_s...  13.3 us
    all_to_all x1, starting transfers between devices, on_device(): sums = lax.all_to_all(sums, 'tile', 0, 0, tiled=True)  10.8 us
    all_to_all x1, waiting for transfers between devices, on_device(): sums = lax.all_to_all(sums, 'tile', 0, 0, tiled=True)  7.61 us
    ppermute x7, waiting for transfers between devices, from_group(): return lax.ppermute(x, 'src', [(i, i ^ d) for i in range(GROUPS)])  7.14 us
    ppermute x2, starting transfers between devices, from_tile_beside(): return lax.ppermute(x, ('src', 'tile'), pairs)  5.39 us
    pallas_call x1, Pallas kernels, edge_spectrum(): pl.pallas_call(edge_kernel, in_specs=[pl.BlockSpec(memory_space=pltpu.SME...  1.87 us
    pallas_call x1, Pallas kernels, last_steps(): pl.pallas_call(functools.partial(last_kernel, pixels=pixels), in_specs=[p...  1.61 us
  transfers between devices with their start and end apart: 10, of which 5 were waited for; matrix products, arithmetic and copies ran while one was open for 0% of the time, Pallas kernels for 3%

profile of v5, /device:TPU:2, one launch (start us, length us, event | category | flops | bytes accessed | tf_op | source)
XLA Modules:
  0.0 66.8 jit_solution(3844348261153312510)
XLA Ops:
  0.6 0.0 copy-start.3
  0.7 1.9 %edge_spectrum.1 = (bf16[64,128]{1,0:T(8,128)(2,1)}, f32[3,16]{1,0:T(4,128)}) custom-call(s32[1]{0:T(128)} %bitcast.group_ref, f32[512,512]{1,0:T(8,128)} %logits_ref.5, bf16[512,128]{1,0:T(8,128)(2,1)} %constant.16.clone.table_ref, f32[1,16]{1,0:T(1,128)} %bitcast.6, s32[2,16]{1,0:T(2,128)} %bitcast.5), custom_call_target="tpu_custom_call" | custom-call | tf_op jit(solution)/shard_map/edge_spectrum/pallas_call | solution.py:94
  2.5 3.5 %collective-permute-start.1 = (bf16[64,128]{1,0:T(8,128)(2,1)}, bf16[64,128]{1,0:T(8,128)(2,1)S(1)}, u32[]{:S(2)}, u32[]{:S(2)}) collective-permute-start(bf16[64,128]{1,0:T(8,128)(2,1)} %get-tuple-element.21), channel_id=1, source_target_pairs={{0,1},{1,2},{2,3},{3,4},{4,5},{5,6},{6,7},{7,8},{8,9},{9,10},{10,1... | collective-permute-start | bytes 49160 | tf_op jit(solution)/shard_map/ppermute | solution.py:397
  6.0 0.0 copy-start.1
  6.1 7.3 %collective-permute-start.2 = (f32[3,16]{1,0:T(4,128)S(1)}, f32[3,16]{1,0:T(4,128)S(1)}, u32[]{:S(2)}, u32[]{:S(2)}) collective-permute-start(f32[3,16]{1,0:T(4,128)S(1)} %copy-done.7), channel_id=1, source_target_pairs={{0,128},{64,192},{128,0},{192,64},{1,129},{65,193},{129,1},{193,65... | collective-permute-start | bytes 584 | tf_op jit(solution)/shard_map/ppermute | solution.py:401
  13.3 1.2 %copy-done.2 = bf16[3712,128]{1,0:T(8,128)(2,1)S(1)} copy-done((bf16[3712,128]{1,0:T(8,128)(2,1)S(1)}, bf16[3712,128]{1,0:T(8,128)(2,1)}, u32[]{:S(2)}) %copy-start.2) | copy-done | bytes 950296
  14.5 0.6 column_spectrum.1
  15.2 3.6 %collective-permute-start.4 = (bf16[64,128]{1,0:T(8,128)(2,1)S(1)}, bf16[64,128]{1,0:T(8,128)(2,1)S(1)}, u32[]{:S(2)}, u32[]{:S(2)}) collective-permute-start(bf16[64,128]{1,0:T(8,128)(2,1)S(1)} %collective-permute-done.1.near_ref), channel_id=1, source_target_pairs={{0,64},{64,0},{128,192},{192,128},{1,65},{65,1},{129,193},{193,129... | collective-permute-start | bytes 49160 | tf_op jit(solution)/shard_map/ppermute | solution.py:401
  18.8 0.5 collective-permute-start.3
  19.3 0.7 collective-permute-done.scalars_1
  19.9 0.2 collective-permute-done.3.scalars_3
  20.1 13.3 %image.1 = f32[72,128]{1,0:T(8,128)S(1)} custom-call(s32[1]{0:T(128)} %bitcast.group_ref, f32[3,16]{1,0:T(4,128)S(1)} %copy-done.7, f32[3,16]{1,0:T(4,128)S(1)} %collective-permute-done.scalars_1, f32[3,16]{1,0:T(4,128)S(1)} %collective-permute-done.2.scalars_2, f32[3,16]{1,0:T(4,128)S(1)} %collective-permute-done.3.scalars_3, ...), custom_call_target="tpu_custom_call" | custom-call | tf_op jit(solution)/shard_map/image/pallas_call | solution.py:257
  33.4 0.0 copy-start.4
  33.4 0.4 collective-permute-start.5
  33.9 0.9 %collective-permute-done.5 = f32[72,128]{1,0:T(8,128)S(1)} collective-permute-done((f32[72,128]{1,0:T(8,128)S(1)}, f32[72,128]{1,0:T(8,128)S(1)}, u32[]{:S(2)}, u32[]{:S(2)}) %collective-permute-start.5) | collective-permute-done | bytes 36896 | tf_op jit(solution)/shard_map/ppermute | solution.py:401
  34.8 2.4 %collective-permute-start.6 = (f32[72,128]{1,0:T(8,128)S(1)}, f32[72,128]{1,0:T(8,128)S(1)}, u32[]{:S(2)}, u32[]{:S(2)}) collective-permute-start(f32[72,128]{1,0:T(8,128)S(1)} %add.3.chip_ref), channel_id=1, source_target_pairs={{0,128},{64,192},{128,0},{192,64},{1,129},{65,193},{129,1},{193,65... | collective-permute-start | bytes 110600 | tf_op jit(solution)/shard_map/ppermute | solution.py:401
  37.2 5.5 %collective-permute-done.6.far_ref = f32[72,128]{1,0:T(8,128)S(1)} collective-permute-done((f32[72,128]{1,0:T(8,128)S(1)}, f32[72,128]{1,0:T(8,128)S(1)}, u32[]{:S(2)}, u32[]{:S(2)}) %collective-permute-start.6) | collective-permute-done | bytes 36896 | tf_op jit(solution)/shard_map/ppermute | solution.py:401
  42.6 0.6 total.1
  43.3 1.9 %collective-permute-start.7 = (f32[64,128]{1,0:T(8,128)S(1)}, f32[64,128]{1,0:T(8,128)S(1)}, u32[]{:S(2)}, u32[]{:S(2)}) collective-permute-start(f32[64,128]{1,0:T(8,128)S(1)} %get-tuple-element.27.grad_ref), channel_id=1, source_target_pairs={{0,1},{1,2},{2,3},{3,4},{4,5},{5,6},{6,7},{7,8},{8,9},{9,10},{10,1... | collective-permute-start | bytes 98312 | tf_op jit(solution)/shard_map/ppermute | solution.py:397
  45.2 10.8 %all-to-all-start = ((f32[64,1,128]{2,1,0:T(1,128)}), f32[64,1,128]{2,1,0:T(1,128)S(1)}, u32[]{:S(2)}, u32[]{:S(2)}) async-start(f32[64,1,128]{2,1,0:T(1,128)} %get-tuple-element.32), calls=%async_computation | async-start | bytes 65536 | tf_op jit(solution)/shard_map/all_to_all | solution.py:426
  56.0 0.0 copy-start.6
  56.0 1.5 %owned_gradient.1 = (f32[512,512]{1,0:T(8,128)}, f32[128,512]{1,0:T(8,128)S(1)}, f32[128,512]{1,0:T(8,128)S(1)}) custom-call(f32[64,128]{1,0:T(8,128)S(1)} %get-tuple-element.27.grad_ref, f32[512,512]{1,0:T(8,128)S(1)} %copy-done, bf16[512,128]{1,0:T(8,128)(2,1)S(1)} %copy-done.5, bf16[128,512]{1,0:T(8,128)(2,1)S(1)} %copy-done.4), custom_call_target="tpu_custom_call" | custom-call | tf_op jit(solution)/shard_map/owned_gradient/pallas_call | solution.py:332
  57.5 7.6 %all-to-all-done.sums_ref = f32[64,1,128]{2,1,0:T(1,128)S(1)} async-done(((f32[64,1,128]{2,1,0:T(1,128)}), f32[64,1,128]{2,1,0:T(1,128)S(1)}, u32[]{:S(2)}, u32[]{:S(2)}) %all-to-all-start) | async-done | bytes 32800 | tf_op jit(solution)/shard_map/all_to_all | solution.py:426
  65.2 1.6 %last_steps.1 = (f32[512,512]{1,0:T(8,128)}, f32[1,16]{1,0:T(1,128)}, f32[1,1]{1,0:T(1,128)}) custom-call(s32[1]{0:T(128)} %bitcast.group_ref, f32[64,128]{1,0:T(8,128)S(1)} %collective-permute-done.7.near_ref, f32[64,128]{1,0:T(8,128)S(1)} %collective-permute-done.8.other_ref, ...), custom_call_target="tpu_custom_call", output_to_operand_aliasing={{0}: (9, {})} | custom-call | tf_op jit(solution)/shard_map/last_steps/pallas_call | solution.py:373
  (19 shorter events, 0.0 us)
Async XLA Ops:
  0.6 12.7 %copy-start = (f32[512,512]{1,0:T(8,128)S(1)}, f32[512,512]{1,0:T(8,128)}, u32[]{:S(2)}) copy-start(f32[512,512]{1,0:T(8,128)} %logits_ref.5) | copy-start | bytes 3145732
  0.6 12.7 %copy-start.3 = (bf16[512,128]{1,0:T(8,128)(2,1)S(1)}, bf16[512,128]{1,0:T(8,128)(2,1)}, u32[]{:S(2)}) copy-start(bf16[512,128]{1,0:T(8,128)(2,1)} %constant.16.clone.table_ref) | copy-start | bytes 393220
  2.5 3.5 %copy-start.7 = (f32[3,16]{1,0:T(4,128)S(1)}, f32[3,16]{1,0:T(4,128)}, u32[]{:S(2)}) copy-start(f32[3,16]{1,0:T(4,128)} %get-tuple-element.20.own_scalars.packed_ref) | copy-start | bytes 580
  2.5 12.6 %collective-permute-start.1 = (bf16[64,128]{1,0:T(8,128)(2,1)}, bf16[64,128]{1,0:T(8,128)(2,1)S(1)}, u32[]{:S(2)}, u32[]{:S(2)}) collective-permute-start(bf16[64,128]{1,0:T(8,128)(2,1)} %get-tuple-element.21), channel_id=1, source_target_pairs={{0,1},{1,2},{2,3},{3,4},{4,5},{5,6},{6,7},{7,8},{8,9},{9,10},{10,1... | collective-permute-start | bytes 49160 | tf_op jit(solution)/shard_map/ppermute | solution.py:397
  6.0 14.0 %copy-start.1 = (s32[512,512]{1,0:T(8,128)S(1)}, s32[512,512]{1,0:T(8,128)}, u32[]{:S(2)}) copy-start(s32[512,512]{1,0:T(8,128)} %target_ref.1) | copy-start | bytes 3145732
  6.1 9.1 %collective-permute-start.2 = (f32[3,16]{1,0:T(4,128)S(1)}, f32[3,16]{1,0:T(4,128)S(1)}, u32[]{:S(2)}, u32[]{:S(2)}) collective-permute-start(f32[3,16]{1,0:T(4,128)S(1)} %copy-done.7), channel_id=1, source_target_pairs={{0,128},{64,192},{128,0},{192,64},{1,129},{65,193},{129,1},{193,65... | collective-permute-start | bytes 584 | tf_op jit(solution)/shard_map/ppermute | solution.py:401
  13.3 1.2 %copy-start.2 = (bf16[3712,128]{1,0:T(8,128)(2,1)S(1)}, bf16[3712,128]{1,0:T(8,128)(2,1)}, u32[]{:S(2)}) copy-start(bf16[3712,128]{1,0:T(8,128)(2,1)} %constant.17.clone.image_table_ref) | copy-start | bytes 2850820
  15.2 4.9 %collective-permute-start.4 = (bf16[64,128]{1,0:T(8,128)(2,1)S(1)}, bf16[64,128]{1,0:T(8,128)(2,1)S(1)}, u32[]{:S(2)}, u32[]{:S(2)}) collective-permute-start(bf16[64,128]{1,0:T(8,128)(2,1)S(1)} %collective-permute-done.1.near_ref), channel_id=1, source_target_pairs={{0,64},{64,0},{128,192},{192,128},{1,65},{65,1},{129,193},{193,129... | collective-permute-start | bytes 49160 | tf_op jit(solution)/shard_map/ppermute | solution.py:401
  18.8 1.2 %collective-permute-start = (f32[3,16]{1,0:T(4,128)S(1)}, f32[3,16]{1,0:T(4,128)S(1)}, u32[]{:S(2)}, u32[]{:S(2)}) collective-permute-start(f32[3,16]{1,0:T(4,128)S(1)} %copy-done.7), channel_id=1, source_target_pairs={{0,64},{64,0},{128,192},{192,128},{1,65},{65,1},{129,193},{193,129... | collective-permute-start | bytes 584 | tf_op jit(solution)/shard_map/ppermute | solution.py:401
  18.8 1.3 %collective-permute-start.3 = (f32[3,16]{1,0:T(4,128)S(1)}, f32[3,16]{1,0:T(4,128)S(1)}, u32[]{:S(2)}, u32[]{:S(2)}) collective-permute-start(f32[3,16]{1,0:T(4,128)S(1)} %collective-permute-done.2.scalars_2), channel_id=1, source_target_pairs={{0,64},{64,0},{128,192},{192,128},{1,65},{65,1},{129,193},{193,129... | collective-permute-start | bytes 584 | tf_op jit(solution)/shard_map/ppermute | solution.py:401
  20.1 35.9 %copy-start.5 = (bf16[512,128]{1,0:T(8,128)(2,1)S(1)}, bf16[512,128]{1,0:T(8,128)(2,1)}, u32[]{:S(2)}) copy-start(bf16[512,128]{1,0:T(8,128)(2,1)} %constant.18.clone.row_ref) | copy-start | bytes 393220
  33.4 22.6 %copy-start.4 = (bf16[128,512]{1,0:T(8,128)(2,1)S(1)}, bf16[128,512]{1,0:T(8,128)(2,1)}, u32[]{:S(2)}) copy-start(bf16[128,512]{1,0:T(8,128)(2,1)} %constant.19.clone.column_ref) | copy-start | bytes 393220
  33.4 1.3 %collective-permute-start.5 = (f32[72,128]{1,0:T(8,128)S(1)}, f32[72,128]{1,0:T(8,128)S(1)}, u32[]{:S(2)}, u32[]{:S(2)}) collective-permute-start(f32[72,128]{1,0:T(8,128)S(1)} %image.1), channel_id=1, source_target_pairs={{0,64},{64,0},{128,192},{192,128},{1,65},{65,1},{129,193},{193,129... | collective-permute-start | bytes 110600 | tf_op jit(solution)/shard_map/ppermute | solution.py:401
  34.8 7.9 %collective-permute-start.6 = (f32[72,128]{1,0:T(8,128)S(1)}, f32[72,128]{1,0:T(8,128)S(1)}, u32[]{:S(2)}, u32[]{:S(2)}) collective-permute-start(f32[72,128]{1,0:T(8,128)S(1)} %add.3.chip_ref), channel_id=1, source_target_pairs={{0,128},{64,192},{128,0},{192,64},{1,129},{65,193},{129,1},{193,65... | collective-permute-start | bytes 110600 | tf_op jit(solution)/shard_map/ppermute | solution.py:401
  43.3 14.3 %collective-permute-start.7 = (f32[64,128]{1,0:T(8,128)S(1)}, f32[64,128]{1,0:T(8,128)S(1)}, u32[]{:S(2)}, u32[]{:S(2)}) collective-permute-start(f32[64,128]{1,0:T(8,128)S(1)} %get-tuple-element.27.grad_ref), channel_id=1, source_target_pairs={{0,1},{1,2},{2,3},{3,4},{4,5},{5,6},{6,7},{7,8},{8,9},{9,10},{10,1... | collective-permute-start | bytes 98312 | tf_op jit(solution)/shard_map/ppermute | solution.py:397
  45.2 20.0 %all-to-all-start = ((f32[64,1,128]{2,1,0:T(1,128)}), f32[64,1,128]{2,1,0:T(1,128)S(1)}, u32[]{:S(2)}, u32[]{:S(2)}) async-start(f32[64,1,128]{2,1,0:T(1,128)} %get-tuple-element.32), calls=%async_computation | async-start | bytes 65536 | tf_op jit(solution)/shard_map/all_to_all | solution.py:426
  56.0 9.1 %copy-start.6 = (bf16[128,128]{1,0:T(8,128)(2,1)S(1)}, bf16[128,128]{1,0:T(8,128)(2,1)}, u32[]{:S(2)}) copy-start(bf16[128,128]{1,0:T(8,128)(2,1)} %constant.20.clone.row_ref) | copy-start | bytes 98308
  57.5 7.6 %collective-permute-start.8 = (f32[64,128]{1,0:T(8,128)S(1)}, f32[64,128]{1,0:T(8,128)S(1)}, u32[]{:S(2)}, u32[]{:S(2)}) collective-permute-start(f32[64,128]{1,0:T(8,128)S(1)} %collective-permute-done.7.near_ref), channel_id=1, source_target_pairs={{0,64},{64,0},{128,192},{192,128},{1,65},{65,1},{129,193},{193,129... | collective-permute-start | bytes 98312 | tf_op jit(solution)/shard_map/ppermute | solution.py:401

commit v6 on v3

--- a/solution.py
+++ b/solution.py
@@ -7,6 +7,7 @@
 from jax.experimental import pallas as pl
 from jax.experimental.pallas import tpu as pltpu
 from jax.sharding import PartitionSpec as P
+
 
 FREQS = 64
 RADIUS = 20
@@ -135,6 +136,7 @@
 def image_kernel(group_ref, own_scalars, scalars_1, scalars_2, scalars_3, own_ref, near_ref, other_ref, target_ref, table_ref, out_ref, sums_ref,
                  fields_ref, row_field_ref, intensity_ref, cotangent_ref, spectra_ref, terms_ref, grad_ref, rounded_ref, frame_ref):
     scalars = [own_scalars, scalars_1, scalars_2, scalars_3]
+
     def beside(start, count):
         return jnp.concatenate([table_ref[start + 128 * i:start + 128 * (i + 1), :] for i in range(count)], 1)
 
@@ -325,7 +327,7 @@
 
 
 def last_kernel(group_ref, near_ref, other_ref, edges_ref, slope_ref, row_ref, column_ref, own_ref, beside_ref,
-                far_ref, across_ref, weights_ref, grad_ref, out_ref, weight_grad_ref, loss_ref,
+                far_ref, across_ref, packed_ref, grad_ref, out_ref, weight_grad_ref, loss_ref,
                 rows_ref, semaphores, *, pixels):
     del grad_ref
     even = group_ref[0] % 2 == 0
@@ -345,13 +347,13 @@
     row = total
     for bit, width in ((1, PER_GROUP), (2, 2 * PER_GROUP)):
         row = jnp.where(jnp.bitwise_and(group_ref[0], bit) != 0, pltpu.roll(row, 128 - width, 1), row)
-    weight_grad_ref[...] = row[:, :PER_GROUP] / (F32(2.0) * weights_ref[...]) / F32(pixels)
+    weight_grad_ref[...] = row[:, :PER_GROUP] / (F32(2.0) * packed_ref[0:1]) / F32(pixels)
     loss_ref[...] = total[:, SOURCES:SOURCES + 1] / F32(pixels)
     for copy in copies:
         copy.wait()
 
 
-def last_steps(group, near, other, edges, slope, grad, sums, weights, pixels):
+def last_steps(group, near, other, edges, slope, grad, sums, packed, pixels):
     rows = np.concatenate([ROW_FORWARD.T[MARGIN + TILE_ROWS:], ROW_FORWARD.T[:MARGIN]], 0)
     block = pl.BlockSpec()
     hbm = pl.BlockSpec(memory_space=pltpu.HBM)
@@ -366,7 +368,7 @@
         compiler_params=pltpu.CompilerParams(vmem_limit_bytes=4 * MIB),
         name="last_steps",
     )(group, near, other, edges, slope, jnp.asarray(np.ascontiguousarray(rows)),
-      jnp.asarray(np.ascontiguousarray(COLUMN_FORWARD.T)), *sums, weights.reshape(1, PER_GROUP), grad)
+      jnp.asarray(np.ascontiguousarray(COLUMN_FORWARD.T)), *sums, packed, grad)
 
 
 def from_tile_beside(x):
@@ -399,10 +401,10 @@
     near, packed_far, own = lax.optimization_barrier((near, packed_far, own))
     scalars = [packed, packed_core, packed_far, from_core(packed_far)]
     partial, sums = image(group, scalars, own, near, from_core(near), target, table, peers)
-    chip = partial + from_core(partial)
-    far = from_chip(chip)
     sums = lax.all_to_all(sums, "tile", 0, 0, tiled=True)
-    spectrum_grad = chip + far
+    beside = from_core(partial)
+    chip = partial + beside
+    spectrum_grad = chip + from_chip(chip)
     near_grad = from_tile_beside(spectrum_grad)
     sums = jnp.sum(sums, 0)
     sums_far = from_chip(sums)
@@ -410,7 +412,7 @@
     near_grad, sums_far, edges = lax.optimization_barrier((near_grad, sums_far, edges))
     sums = [sums, from_core(sums), sums_far, from_core(sums_far)]
     mask_grad, weight_grad, loss = last_steps(
-        group, near_grad, from_core(near_grad), edges, slope, grad, sums, weights, TILE_ROWS * COLS * peers)
+        group, near_grad, from_core(near_grad), edges, slope, grad, sums, packed, TILE_ROWS * COLS * peers)
     return mask_grad, weight_grad.reshape(PER_GROUP), loss.reshape(())
 
 

time: 70.3 us -> 69.7 us (level)
    unnamed x18 -> x16, local copies, waits for them, and re-layouts: 1.88 us -> 1.22 us
where the time goes in v6:
time: 69.7 us; the launch traced here: 69.4 us
  starting transfers between devices  33.5 us (48%)
  Pallas kernels  19.5 us (28%)
  waiting for transfers between devices  14.4 us (21%)
  local copies, waits for them, and re-layouts  1.22 us (2%)
  between operations  0.76 us (1%)
    ppermute x10, starting transfers between devices, from_group(): return lax.ppermute(x, 'src', [(i, i ^ d) for i in range(GROUPS)])  21.4 us
    pallas_call x1, Pallas kernels, image(): pl.pallas_call(image_kernel, grid_spec=pltpu.PrefetchScalarGridSpec(num_s...  13.9 us
    all_to_all x1, starting transfers between devices, on_device(): sums = lax.all_to_all(sums, 'tile', 0, 0, tiled=True)  9.47 us
    all_to_all x1, waiting for transfers between devices, on_device(): sums = lax.all_to_all(sums, 'tile', 0, 0, tiled=True)  7.51 us
    ppermute x10, waiting for transfers between devices, from_group(): return lax.ppermute(x, 'src', [(i, i ^ d) for i in range(GROUPS)])  6.89 us
    ppermute x2, starting transfers between devices, from_tile_beside(): return lax.ppermute(x, ('src', 'tile'), pairs)  2.58 us
    pallas_call x1, Pallas kernels, edge_spectrum(): pl.pallas_call(edge_kernel, in_specs=[pl.BlockSpec(memory_space=pltpu.SME...  1.87 us
    pallas_call x1, Pallas kernels, last_steps(): pl.pallas_call(functools.partial(last_kernel, pixels=pixels), in_specs=[p...  1.61 us
  transfers between devices with their start and end apart: 13, of which 7 were waited for; matrix products, arithmetic and copies ran while one was open for 0% of the time, Pallas kernels for 3%

profile of v6, /device:TPU:1, one launch (start us, length us, event | category | flops | bytes accessed | tf_op | source)
XLA Modules:
  0.0 69.4 jit_solution(2792750100580640748)
XLA Ops:
  0.7 1.9 %edge_spectrum.1 = (bf16[64,128]{1,0:T(8,128)(2,1)}, f32[3,16]{1,0:T(4,128)}) custom-call(s32[1]{0:T(128)} %bitcast.group_ref, f32[512,512]{1,0:T(8,128)} %logits_ref.5, bf16[512,128]{1,0:T(8,128)(2,1)} %constant.18.clone.table_ref, f32[1,16]{1,0:T(1,128)} %bitcast.10, s32[2,16]{1,0:T(2,128)} %bitcast.9), custom_call_target="tpu_custom_call" | custom-call | tf_op jit(solution)/shard_map/edge_spectrum/pallas_call | solution.py:95
  2.5 1.3 %collective-permute-start.1 = (bf16[64,128]{1,0:T(8,128)(2,1)}, bf16[64,128]{1,0:T(8,128)(2,1)S(1)}, u32[]{:S(2)}, u32[]{:S(2)}) collective-permute-start(bf16[64,128]{1,0:T(8,128)(2,1)} %get-tuple-element.22), channel_id=1, source_target_pairs={{0,1},{1,2},{2,3},{3,4},{4,5},{5,6},{6,7},{7,8},{8,9},{9,10},{10,1... | collective-permute-start | bytes 49160 | tf_op jit(solution)/shard_map/ppermute | solution.py:378
  3.9 7.8 %collective-permute-start.2 = (f32[3,16]{1,0:T(4,128)S(1)}, f32[3,16]{1,0:T(4,128)S(1)}, u32[]{:S(2)}, u32[]{:S(2)}) collective-permute-start(f32[3,16]{1,0:T(4,128)S(1)} %copy-done.7), channel_id=1, source_target_pairs={{0,128},{64,192},{128,0},{192,64},{1,129},{65,193},{129,1},{193,65... | collective-permute-start | bytes 584 | tf_op jit(solution)/shard_map/ppermute | solution.py:382
  11.7 1.2 %copy-done.2 = bf16[3712,128]{1,0:T(8,128)(2,1)S(1)} copy-done((bf16[3712,128]{1,0:T(8,128)(2,1)S(1)}, bf16[3712,128]{1,0:T(8,128)(2,1)}, u32[]{:S(2)}) %copy-start.2) | copy-done | bytes 950296
  12.9 0.6 column_spectrum.1
  13.5 3.2 %collective-permute-start.4 = (bf16[64,128]{1,0:T(8,128)(2,1)S(1)}, bf16[64,128]{1,0:T(8,128)(2,1)S(1)}, u32[]{:S(2)}, u32[]{:S(2)}) collective-permute-start(bf16[64,128]{1,0:T(8,128)(2,1)S(1)} %collective-permute-done.1.near_ref), channel_id=1, source_target_pairs={{0,64},{64,0},{128,192},{192,128},{1,65},{65,1},{129,193},{193,129... | collective-permute-start | bytes 49160 | tf_op jit(solution)/shard_map/ppermute | solution.py:382
  16.8 0.4 collective-permute-start.3
  17.2 0.7 collective-permute-done.scalars_1
  17.9 0.2 collective-permute-done.3.scalars_3
  18.1 13.9 %image.1 = (f32[64,128]{1,0:T(8,128)S(1)}, f32[64,1,128]{2,1,0:T(1,128)}) custom-call(s32[1]{0:T(128)} %bitcast.group_ref, f32[3,16]{1,0:T(4,128)S(1)} %copy-done.7, f32[3,16]{1,0:T(4,128)S(1)} %collective-permute-done.scalars_1, f32[3,16]{1,0:T(4,128)S(1)} %collective-permute-done.2.scalars_2, f32[3,16]{1,0:T(4,128)S(1)} %collective-permute-done.3.scalars_3, ...), custom_call_target="tpu_custom_call" | custom-call | tf_op jit(solution)/shard_map/image/pallas_call | solution.py:259
  31.9 0.3 collective-permute-start.5
  32.3 0.9 %collective-permute-done.5 = f32[64,128]{1,0:T(8,128)S(1)} collective-permute-done((f32[64,128]{1,0:T(8,128)S(1)}, f32[64,128]{1,0:T(8,128)S(1)}, u32[]{:S(2)}, u32[]{:S(2)}) %collective-permute-start.5) | collective-permute-done | bytes 32800 | tf_op jit(solution)/shard_map/ppermute | solution.py:382
  33.2 5.3 %collective-permute-start.6 = (f32[64,128]{1,0:T(8,128)S(1)}, f32[64,128]{1,0:T(8,128)S(1)}, u32[]{:S(2)}, u32[]{:S(2)}) collective-permute-start(f32[64,128]{1,0:T(8,128)S(1)} %add.6), channel_id=1, source_target_pairs={{0,128},{64,192},{128,0},{192,64},{1,129},{65,193},{129,1},{193,65... | collective-permute-start | bytes 98312 | tf_op jit(solution)/shard_map/ppermute | solution.py:382
  38.5 9.5 %all-to-all-start = ((f32[64,1,128]{2,1,0:T(1,128)}), f32[64,1,128]{2,1,0:T(1,128)S(1)}, u32[]{:S(2)}, u32[]{:S(2)}) async-start(f32[64,1,128]{2,1,0:T(1,128)} %get-tuple-element.29), calls=%async_computation | async-start | bytes 65536 | tf_op jit(solution)/shard_map/all_to_all | solution.py:404
  48.0 1.3 %collective-permute-start.7 = (f32[64,128]{1,0:T(8,128)S(1)}, f32[64,128]{1,0:T(8,128)S(1)}, u32[]{:S(2)}, u32[]{:S(2)}) collective-permute-start(f32[64,128]{1,0:T(8,128)S(1)} %add.7.grad_ref), channel_id=1, source_target_pairs={{0,1},{1,2},{2,3},{3,4},{4,5},{5,6},{6,7},{7,8},{8,9},{9,10},{10,1... | collective-permute-start | bytes 98312 | tf_op jit(solution)/shard_map/ppermute | solution.py:378
  49.3 7.5 %all-to-all-done = f32[64,1,128]{2,1,0:T(1,128)S(1)} async-done(((f32[64,1,128]{2,1,0:T(1,128)}), f32[64,1,128]{2,1,0:T(1,128)S(1)}, u32[]{:S(2)}, u32[]{:S(2)}) %all-to-all-start) | async-done | bytes 32800 | tf_op jit(solution)/shard_map/all_to_all | solution.py:404
  56.9 0.5 collective-permute-start.8
  57.4 1.5 %owned_gradient.1 = (f32[512,512]{1,0:T(8,128)}, f32[128,512]{1,0:T(8,128)S(1)}, f32[128,512]{1,0:T(8,128)S(1)}) custom-call(f32[64,128]{1,0:T(8,128)S(1)} %add.7.grad_ref, f32[512,512]{1,0:T(8,128)S(1)} %copy-done, bf16[512,128]{1,0:T(8,128)(2,1)S(1)} %copy-done.5, bf16[128,512]{1,0:T(8,128)(2,1)S(1)} %copy-done.4), custom_call_target="tpu_custom_call" | custom-call | tf_op jit(solution)/shard_map/owned_gradient/pallas_call | solution.py:319
  58.9 4.4 %collective-permute-done.8.far_ref = f32[1,128]{1,0:T(1,128)S(1)} collective-permute-done((f32[1,128]{1,0:T(1,128)S(1)}, f32[1,128]{1,0:T(1,128)S(1)}, u32[]{:S(2)}, u32[]{:S(2)}) %collective-permute-start.8) | collective-permute-done | bytes 544 | tf_op jit(solution)/shard_map/ppermute | solution.py:382
  63.3 3.2 %collective-permute-start.9 = (f32[64,128]{1,0:T(8,128)S(1)}, f32[64,128]{1,0:T(8,128)S(1)}, u32[]{:S(2)}, u32[]{:S(2)}) collective-permute-start(f32[64,128]{1,0:T(8,128)S(1)} %collective-permute-done.7.near_ref), channel_id=1, source_target_pairs={{0,64},{64,0},{128,192},{192,128},{1,65},{65,1},{129,193},{193,129... | collective-permute-start | bytes 98312 | tf_op jit(solution)/shard_map/ppermute | solution.py:382
  66.5 0.5 collective-permute-start.11
  67.0 0.7 collective-permute-done.10.beside_ref
  67.7 0.2 collective-permute-done.11.across_ref
  67.8 1.6 %last_steps.1 = (f32[512,512]{1,0:T(8,128)}, f32[1,16]{1,0:T(1,128)}, f32[1,1]{1,0:T(1,128)}) custom-call(s32[1]{0:T(128)} %bitcast.group_ref, f32[64,128]{1,0:T(8,128)S(1)} %collective-permute-done.7.near_ref, f32[64,128]{1,0:T(8,128)S(1)} %collective-permute-done.9.other_ref, ...), custom_call_target="tpu_custom_call", output_to_operand_aliasing={{0}: (12, {})} | custom-call | tf_op jit(solution)/shard_map/last_steps/pallas_call | solution.py:360
  (26 shorter events, 0.2 us)
Async XLA Ops:
  0.6 11.1 %copy-start = (f32[512,512]{1,0:T(8,128)S(1)}, f32[512,512]{1,0:T(8,128)}, u32[]{:S(2)}) copy-start(f32[512,512]{1,0:T(8,128)} %logits_ref.5) | copy-start | bytes 3145732
  0.6 11.0 %copy-start.3 = (bf16[512,128]{1,0:T(8,128)(2,1)S(1)}, bf16[512,128]{1,0:T(8,128)(2,1)}, u32[]{:S(2)}) copy-start(bf16[512,128]{1,0:T(8,128)(2,1)} %constant.18.clone.table_ref) | copy-start | bytes 393220
  2.5 1.3 %copy-start.7 = (f32[3,16]{1,0:T(4,128)S(1)}, f32[3,16]{1,0:T(4,128)}, u32[]{:S(2)}) copy-start(f32[3,16]{1,0:T(4,128)} %get-tuple-element.21.own_scalars.packed_ref) | copy-start | bytes 580
  2.5 10.9 %collective-permute-start.1 = (bf16[64,128]{1,0:T(8,128)(2,1)}, bf16[64,128]{1,0:T(8,128)(2,1)S(1)}, u32[]{:S(2)}, u32[]{:S(2)}) collective-permute-start(bf16[64,128]{1,0:T(8,128)(2,1)} %get-tuple-element.22), channel_id=1, source_target_pairs={{0,1},{1,2},{2,3},{3,4},{4,5},{5,6},{6,7},{7,8},{8,9},{9,10},{10,1... | collective-permute-start | bytes 49160 | tf_op jit(solution)/shard_map/ppermute | solution.py:378
  3.9 14.2 %copy-start.1 = (s32[512,512]{1,0:T(8,128)S(1)}, s32[512,512]{1,0:T(8,128)}, u32[]{:S(2)}) copy-start(s32[512,512]{1,0:T(8,128)} %target_ref.1) | copy-start | bytes 3145732
  3.9 9.6 %collective-permute-start.2 = (f32[3,16]{1,0:T(4,128)S(1)}, f32[3,16]{1,0:T(4,128)S(1)}, u32[]{:S(2)}, u32[]{:S(2)}) collective-permute-start(f32[3,16]{1,0:T(4,128)S(1)} %copy-done.7), channel_id=1, source_target_pairs={{0,128},{64,192},{128,0},{192,64},{1,129},{65,193},{129,1},{193,65... | collective-permute-start | bytes 584 | tf_op jit(solution)/shard_map/ppermute | solution.py:382
  11.7 1.2 %copy-start.2 = (bf16[3712,128]{1,0:T(8,128)(2,1)S(1)}, bf16[3712,128]{1,0:T(8,128)(2,1)}, u32[]{:S(2)}) copy-start(bf16[3712,128]{1,0:T(8,128)(2,1)} %constant.19.clone.image_table_ref) | copy-start | bytes 2850820
  13.5 4.6 %collective-permute-start.4 = (bf16[64,128]{1,0:T(8,128)(2,1)S(1)}, bf16[64,128]{1,0:T(8,128)(2,1)S(1)}, u32[]{:S(2)}, u32[]{:S(2)}) collective-permute-start(bf16[64,128]{1,0:T(8,128)(2,1)S(1)} %collective-permute-done.1.near_ref), channel_id=1, source_target_pairs={{0,64},{64,0},{128,192},{192,128},{1,65},{65,1},{129,193},{193,129... | collective-permute-start | bytes 49160 | tf_op jit(solution)/shard_map/ppermute | solution.py:382
  16.7 1.2 %collective-permute-start = (f32[3,16]{1,0:T(4,128)S(1)}, f32[3,16]{1,0:T(4,128)S(1)}, u32[]{:S(2)}, u32[]{:S(2)}) collective-permute-start(f32[3,16]{1,0:T(4,128)S(1)} %copy-done.7), channel_id=1, source_target_pairs={{0,64},{64,0},{128,192},{192,128},{1,65},{65,1},{129,193},{193,129... | collective-permute-start | bytes 584 | tf_op jit(solution)/shard_map/ppermute | solution.py:382
  16.8 1.2 %collective-permute-start.3 = (f32[3,16]{1,0:T(4,128)S(1)}, f32[3,16]{1,0:T(4,128)S(1)}, u32[]{:S(2)}, u32[]{:S(2)}) collective-permute-start(f32[3,16]{1,0:T(4,128)S(1)} %collective-permute-done.2.scalars_2), channel_id=1, source_target_pairs={{0,64},{64,0},{128,192},{192,128},{1,65},{65,1},{129,193},{193,129... | collective-permute-start | bytes 584 | tf_op jit(solution)/shard_map/ppermute | solution.py:382
  31.9 25.5 %copy-start.4 = (bf16[128,512]{1,0:T(8,128)(2,1)S(1)}, bf16[128,512]{1,0:T(8,128)(2,1)}, u32[]{:S(2)}) copy-start(bf16[128,512]{1,0:T(8,128)(2,1)} %constant.21.clone.column_ref) | copy-start | bytes 393220
  31.9 25.5 %copy-start.5 = (bf16[512,128]{1,0:T(8,128)(2,1)S(1)}, bf16[512,128]{1,0:T(8,128)(2,1)}, u32[]{:S(2)}) copy-start(bf16[512,128]{1,0:T(8,128)(2,1)} %constant.20.clone.row_ref) | copy-start | bytes 393220
  31.9 1.2 %collective-permute-start.5 = (f32[64,128]{1,0:T(8,128)S(1)}, f32[64,128]{1,0:T(8,128)S(1)}, u32[]{:S(2)}, u32[]{:S(2)}) collective-permute-start(f32[64,128]{1,0:T(8,128)S(1)} %get-tuple-element.28), channel_id=1, source_target_pairs={{0,64},{64,0},{128,192},{192,128},{1,65},{65,1},{129,193},{193,129... | collective-permute-start | bytes 98312 | tf_op jit(solution)/shard_map/ppermute | solution.py:382
  33.2 14.8 %collective-permute-start.6 = (f32[64,128]{1,0:T(8,128)S(1)}, f32[64,128]{1,0:T(8,128)S(1)}, u32[]{:S(2)}, u32[]{:S(2)}) collective-permute-start(f32[64,128]{1,0:T(8,128)S(1)} %add.6), channel_id=1, source_target_pairs={{0,128},{64,192},{128,0},{192,64},{1,129},{65,193},{129,1},{193,65... | collective-permute-start | bytes 98312 | tf_op jit(solution)/shard_map/ppermute | solution.py:382
  38.5 18.3 %all-to-all-start = ((f32[64,1,128]{2,1,0:T(1,128)}), f32[64,1,128]{2,1,0:T(1,128)S(1)}, u32[]{:S(2)}, u32[]{:S(2)}) async-start(f32[64,1,128]{2,1,0:T(1,128)} %get-tuple-element.29), calls=%async_computation | async-start | bytes 65536 | tf_op jit(solution)/shard_map/all_to_all | solution.py:404
  48.0 15.3 %collective-permute-start.7 = (f32[64,128]{1,0:T(8,128)S(1)}, f32[64,128]{1,0:T(8,128)S(1)}, u32[]{:S(2)}, u32[]{:S(2)}) collective-permute-start(f32[64,128]{1,0:T(8,128)S(1)} %add.7.grad_ref), channel_id=1, source_target_pairs={{0,1},{1,2},{2,3},{3,4},{4,5},{5,6},{6,7},{7,8},{8,9},{9,10},{10,1... | collective-permute-start | bytes 98312 | tf_op jit(solution)/shard_map/ppermute | solution.py:378
  56.9 11.0 %copy-start.6 = (bf16[128,128]{1,0:T(8,128)(2,1)S(1)}, bf16[128,128]{1,0:T(8,128)(2,1)}, u32[]{:S(2)}) copy-start(bf16[128,128]{1,0:T(8,128)(2,1)} %constant.22.clone.row_ref) | copy-start | bytes 98308
  56.9 6.4 %collective-permute-start.8 = (f32[1,128]{1,0:T(1,128)S(1)}, f32[1,128]{1,0:T(1,128)S(1)}, u32[]{:S(2)}, u32[]{:S(2)}) collective-permute-start(f32[1,128]{1,0:T(1,128)S(1)} %bitcast.6), channel_id=1, source_target_pairs={{0,128},{64,192},{128,0},{192,64},{1,129},{65,193},{129,1},{193,65... | collective-permute-start | bytes 1544 | tf_op jit(solution)/shard_map/ppermute | solution.py:382
  63.3 4.5 %collective-permute-start.9 = (f32[64,128]{1,0:T(8,128)S(1)}, f32[64,128]{1,0:T(8,128)S(1)}, u32[]{:S(2)}, u32[]{:S(2)}) collective-permute-start(f32[64,128]{1,0:T(8,128)S(1)} %collective-permute-done.7.near_ref), channel_id=1, source_target_pairs={{0,64},{64,0},{128,192},{192,128},{1,65},{65,1},{129,193},{193,129... | collective-permute-start | bytes 98312 | tf_op jit(solution)/shard_map/ppermute | solution.py:382
  66.5 1.2 %collective-permute-start.10 = (f32[1,128]{1,0:T(1,128)S(1)}, f32[1,128]{1,0:T(1,128)S(1)}, u32[]{:S(2)}, u32[]{:S(2)}) collective-permute-start(f32[1,128]{1,0:T(1,128)S(1)} %bitcast.7), channel_id=1, source_target_pairs={{0,64},{64,0},{128,192},{192,128},{1,65},{65,1},{129,193},{193,129... | collective-permute-start | bytes 1544 | tf_op jit(solution)/shard_map/ppermute | solution.py:382
  66.5 1.3 %collective-permute-start.11 = (f32[1,128]{1,0:T(1,128)S(1)}, f32[1,128]{1,0:T(1,128)S(1)}, u32[]{:S(2)}, u32[]{:S(2)}) collective-permute-start(f32[1,128]{1,0:T(1,128)S(1)} %collective-permute-done.8.far_ref), channel_id=1, source_target_pairs={{0,64},{64,0},{128,192},{192,128},{1,65},{65,1},{129,193},{193,129... | collective-permute-start | bytes 1544 | tf_op jit(solution)/shard_map/ppermute | solution.py:382

commit v7 on v4

--- a/solution.py
+++ b/solution.py
@@ -6,7 +6,8 @@
 from jax import lax
 from jax.experimental import pallas as pl
 from jax.experimental.pallas import tpu as pltpu
-from jax.sharding import PartitionSpec as P
+from jax.sharding import Mesh, PartitionSpec as P
+
 
 FREQS = 64
 RADIUS = 20
@@ -16,6 +17,8 @@
 FRAME = 640
 SOURCES = 64
 GROUPS = 4
+PLANES = 4
+PLANE = 16
 PER_GROUP = SOURCES // GROUPS
 ROWS = TILE_ROWS // GROUPS
 MIB = 1024 * 1024
@@ -132,9 +135,10 @@
     return row * row + lane * lane <= F32(RADIUS * RADIUS)
 
 
-def image_kernel(group_ref, own_scalars, scalars_1, scalars_2, scalars_3, own_ref, near_ref, other_ref, target_ref, table_ref, out_ref,
+def image_kernel(group_ref, own_scalars, scalars_1, scalars_2, scalars_3, own_ref, near_ref, other_ref, target_ref, table_ref, out_ref, sums_ref,
                  fields_ref, row_field_ref, intensity_ref, cotangent_ref, spectra_ref, terms_ref, grad_ref, rounded_ref, frame_ref):
     scalars = [own_scalars, scalars_1, scalars_2, scalars_3]
+
     def beside(start, count):
         return jnp.concatenate([table_ref[start + 128 * i:start + 128 * (i + 1), :] for i in range(count)], 1)
 
@@ -235,7 +239,7 @@
 
     add_block_grad(steps - 1)
     grads = grad_ref[...]
-    out_ref[:FREQS] = grads[:FREQS] + halves_sign(FREQS, 1.0, -1.0) * pltpu.roll(grads[FREQS:], FREQS, 1)
+    out_ref[...] = grads[:FREQS] + halves_sign(FREQS, 1.0, -1.0) * pltpu.roll(grads[FREQS:], FREQS, 1)
     term = jnp.sum(terms_ref[...], 1, keepdims=True)
     row = lax.broadcasted_iota(jnp.int32, (SOURCES, 128), 0)
     lane = lax.broadcasted_iota(jnp.int32, (SOURCES, 128), 1)
@@ -248,7 +252,7 @@
                             pltpu.roll(term_row, width, 1))
         term_row = jnp.where(jnp.bitwise_and(own, bit) != 0, swapped, term_row)
     term_row = jnp.where(lane < SOURCES, term_row, F32(0))
-    out_ref[FREQS:] = jnp.broadcast_to(jnp.where(lane == SOURCES, error_sum, term_row), (8, 128))
+    sums_ref[...] = jnp.broadcast_to(jnp.where(lane == SOURCES, error_sum, term_row)[None], sums_ref.shape)
 
 
 def image(group, scalars, own, near, other, target, table):
@@ -265,7 +269,7 @@
                 pl.BlockSpec((ROWS, COLS), lambda i, g: (g[0], 0)),
                 whole(IMAGE_TABLE.shape),
             ],
-            out_specs=whole((FREQS + 8, 128)),
+            out_specs=[whole((FREQS, 128)), pl.BlockSpec((PLANE, 1, 128), lambda i, g: (0, 0, 0))],
             scratch_shapes=[
                 pltpu.VMEM((SOURCES * ROWS, 2 * COLS), F32),
                 pltpu.VMEM((SOURCES * ROWS, 128), BF16),
@@ -278,25 +282,23 @@
                 pltpu.VMEM((FRAME, 128), BF16),
             ],
         ),
-        out_shape=jax.ShapeDtypeStruct((FREQS + 8, 128), F32),
+        out_shape=[jax.ShapeDtypeStruct((FREQS, 128), F32), jax.ShapeDtypeStruct((PLANE, 1, 128), F32)],
         compiler_params=pltpu.CompilerParams(vmem_limit_bytes=44 * MIB),
         name="image",
     )(group, *scalars, own, near, other, target, table)
 
 
-def total_kernel(chip_ref, far_ref, grad_ref, sums_ref):
-    grad_ref[...] = chip_ref[:FREQS] + far_ref[:FREQS]
-    row = chip_ref[FREQS:FREQS + 1] + far_ref[FREQS:FREQS + 1]
-    sums_ref[...] = jnp.broadcast_to(row[None], sums_ref.shape)
-
-
-def total(chip, far, peers):
-    return pl.pallas_call(
-        total_kernel,
-        out_shape=[jax.ShapeDtypeStruct((FREQS, 128), F32), jax.ShapeDtypeStruct((peers, 1, 128), F32)],
+def regroup_kernel(rows_ref, out_ref):
+    out_ref[...] = jnp.broadcast_to(jnp.sum(rows_ref[...], 0)[None], out_ref.shape)
+
+
+def regroup(rows):
+    return pl.pallas_call(
+        regroup_kernel,
+        out_shape=jax.ShapeDtypeStruct((GROUPS * PLANES, 1, 128), F32),
         compiler_params=pltpu.CompilerParams(vmem_limit_bytes=1 * MIB),
-        name="total",
-    )(chip, far)
+        name="regroup",
+    )(rows)
 
 
 def split_dot(table, x):
@@ -385,10 +387,10 @@
 
 
 def from_tile_beside(x):
-    peers = lax.axis_size("tile")
+    peers = PLANES * PLANE
     pairs = [(s * peers + i, s * peers + j) for s in range(GROUPS) for i in range(peers)
              for j in [i + 1 - 2 * (s % 2)] if 0 <= j < peers]
-    return lax.ppermute(x, ("src", "tile"), pairs)
+    return lax.ppermute(x, ("src", "plane", "spot"), pairs)
 
 
 def from_group(x, d):
@@ -404,7 +406,6 @@
 
 
 def on_device(mask_logits, target, weights, shifts):
-    peers = lax.axis_size("tile")
     group = lax.axis_index("src").astype(jnp.int32).reshape(1)
     edge, packed = edge_spectrum(group, mask_logits, weights, shifts)
     near = from_tile_beside(edge)
@@ -413,24 +414,30 @@
     own, table = column_spectrum(mask_logits)
     near, packed_far, own = lax.optimization_barrier((near, packed_far, own))
     scalars = [packed, packed_core, packed_far, from_core(packed_far)]
-    partial = image(group, scalars, own, near, from_core(near), target, table)
-    chip = partial + from_core(partial)
-    spectrum_grad, sums = total(chip, from_chip(chip), peers)
+    partial, sums = image(group, scalars, own, near, from_core(near), target, table)
+    sums = lax.all_to_all(sums, "spot", 0, 0, tiled=True)
+    beside = from_core(partial)
+    chip = partial + beside
+    far = from_chip(chip)
+    sums = regroup(sums)
+    sums = lax.all_to_all(sums, ("src", "plane"), 0, 0, tiled=True)
+    spectrum_grad = chip + far
     near_grad = from_tile_beside(spectrum_grad)
-    sums = lax.all_to_all(sums, "tile", 0, 0, tiled=True)
     grad, edges, slope = owned_gradient(spectrum_grad, mask_logits)
     near_grad, edges = lax.optimization_barrier((near_grad, edges))
     mask_grad, weight_grad, loss = last_steps(
-        group, near_grad, from_core(near_grad), edges, slope, grad, sums, packed, TILE_ROWS * COLS * peers)
+        group, near_grad, from_core(near_grad), edges, slope, grad, sums, packed,
+        TILE_ROWS * COLS * PLANES * PLANE)
     return mask_grad, weight_grad.reshape(PER_GROUP), loss.reshape(())
 
 
 def solution(mesh):
-    placed = (P("tile", None), P("tile", None), P("src"), P("src", None))
+    split = Mesh(mesh.devices.reshape(GROUPS, PLANES, PLANE), ("src", "plane", "spot"))
+    tile = ("plane", "spot")
     return jax.shard_map(
         on_device,
-        mesh=mesh,
-        in_specs=placed,
-        out_specs=(P("tile", None), P("src"), P()),
+        mesh=split,
+        in_specs=(P(tile, None), P(tile, None), P("src"), P("src", None)),
+        out_specs=(P(tile, None), P("src"), P()),
         check_vma=False,
     )

time: 66.6 us -> 84 us (1.26)
  the two profiles are of different devices: /device:TPU:2 before, /device:TPU:1 now
where the time goes in v7:
time: 84 us; the launch traced here: 83.6 us
  blocking collectives  36.1 us (43%)
  starting transfers between devices  21.8 us (26%)
  Pallas kernels  18.9 us (22%)
  waiting for transfers between devices  4.9 us (6%)
  local copies, waits for them, and re-layouts  1.23 us (1%)
    all_to_all x1, blocking collectives, on_device(): sums = lax.all_to_all(sums, ('src', 'plane'), 0, 0, tiled=True)  20.2 us
    ppermute x7, starting transfers between devices, from_group(): return lax.ppermute(x, 'src', [(i, i ^ d) for i in range(GROUPS)])  19.2 us
    all_to_all x1, blocking collectives, on_device(): sums = lax.all_to_all(sums, 'spot', 0, 0, tiled=True)  15.9 us
    pallas_call x1, Pallas kernels, image(): pl.pallas_call(image_kernel, grid_spec=pltpu.PrefetchScalarGridSpec(num_s...  13.3 us
    ppermute x7, waiting for transfers between devices, from_group(): return lax.ppermute(x, 'src', [(i, i ^ d) for i in range(GROUPS)])  3.07 us
    ppermute x2, starting transfers between devices, from_tile_beside(): return lax.ppermute(x, ('src', 'plane', 'spot'), pairs)  2.57 us
    pallas_call x1, Pallas kernels, edge_spectrum(): pl.pallas_call(edge_kernel, in_specs=[pl.BlockSpec(memory_space=pltpu.SME...  1.87 us
    ppermute x2, waiting for transfers between devices, from_tile_beside(): return lax.ppermute(x, ('src', 'plane', 'spot'), pairs)  1.84 us
  transfers between devices with their start and end apart: 9, of which 5 were waited for; matrix products, arithmetic and copies ran while one was open for 0% of the time, Pallas kernels for 3%

profile of v7, /device:TPU:1, one launch (start us, length us, event | category | flops | bytes accessed | tf_op | source)
XLA Modules:
  0.0 83.6 jit_solution(10460510173519007107)
XLA Ops:
  0.6 0.0 copy-start.3
  0.7 1.9 %edge_spectrum.1 = (bf16[64,128]{1,0:T(8,128)(2,1)}, f32[3,16]{1,0:T(4,128)}) custom-call(s32[1]{0:T(128)} %bitcast.group_ref, f32[512,512]{1,0:T(8,128)} %logits_ref.5, bf16[512,128]{1,0:T(8,128)(2,1)} %constant.16.clone.table_ref, f32[1,16]{1,0:T(1,128)} %bitcast.6, s32[2,16]{1,0:T(2,128)} %bitcast.5), custom_call_target="tpu_custom_call" | custom-call | tf_op jit(solution)/shard_map/edge_spectrum/pallas_call | solution.py:97
  2.5 1.3 %collective-permute-start.1 = (bf16[64,128]{1,0:T(8,128)(2,1)}, bf16[64,128]{1,0:T(8,128)(2,1)S(1)}, u32[]{:S(2)}, u32[]{:S(2)}) collective-permute-start(bf16[64,128]{1,0:T(8,128)(2,1)} %get-tuple-element.21), channel_id=1, source_target_pairs={{0,1},{1,2},{2,3},{3,4},{4,5},{5,6},{6,7},{7,8},{8,9},{9,10},{10,1... | collective-permute-start | bytes 49160 | tf_op jit(solution)/shard_map/ppermute | solution.py:393
  3.9 7.8 %collective-permute-start.2 = (f32[3,16]{1,0:T(4,128)S(1)}, f32[3,16]{1,0:T(4,128)S(1)}, u32[]{:S(2)}, u32[]{:S(2)}) collective-permute-start(f32[3,16]{1,0:T(4,128)S(1)} %copy-done.7), channel_id=1, source_target_pairs={{0,128},{64,192},{128,0},{192,64},{1,129},{65,193},{129,1},{193,65... | collective-permute-start | bytes 584 | tf_op jit(solution)/shard_map/ppermute | solution.py:397
  11.7 1.2 %copy-done.2 = bf16[3712,128]{1,0:T(8,128)(2,1)S(1)} copy-done((bf16[3712,128]{1,0:T(8,128)(2,1)S(1)}, bf16[3712,128]{1,0:T(8,128)(2,1)}, u32[]{:S(2)}) %copy-start.2) | copy-done | bytes 950296
  12.9 0.6 column_spectrum.1
  13.5 3.2 %collective-permute-start.4 = (bf16[64,128]{1,0:T(8,128)(2,1)S(1)}, bf16[64,128]{1,0:T(8,128)(2,1)S(1)}, u32[]{:S(2)}, u32[]{:S(2)}) collective-permute-start(bf16[64,128]{1,0:T(8,128)(2,1)S(1)} %collective-permute-done.1.near_ref), channel_id=1, source_target_pairs={{0,64},{64,0},{128,192},{192,128},{1,65},{65,1},{129,193},{193,129... | collective-permute-start | bytes 49160 | tf_op jit(solution)/shard_map/ppermute | solution.py:397
  16.7 0.1 collective-permute-start
  16.8 0.4 collective-permute-start.3
  17.2 0.7 collective-permute-done.scalars_1
  17.9 0.2 collective-permute-done.3.scalars_3
  18.1 13.3 %image.1 = (f32[64,128]{1,0:T(8,128)S(1)}, f32[16,1,128]{2,1,0:T(1,128)S(1)}) custom-call(s32[1]{0:T(128)} %bitcast.group_ref, f32[3,16]{1,0:T(4,128)S(1)} %copy-done.7, f32[3,16]{1,0:T(4,128)S(1)} %collective-permute-done.scalars_1, f32[3,16]{1,0:T(4,128)S(1)} %collective-permute-done.2.scalars_2, f32[3,16]{1,0:T(4,128)S(1)} %collective-permute-done.3.scalars_3, ...), custom_call_target="tpu_custom_call" | custom-call | tf_op jit(solution)/shard_map/image/pallas_call | solution.py:261
  31.4 0.0 copy-start.4
  31.4 0.4 collective-permute-start.5
  31.9 0.9 %collective-permute-done.5 = f32[64,128]{1,0:T(8,128)S(1)} collective-permute-done((f32[64,128]{1,0:T(8,128)S(1)}, f32[64,128]{1,0:T(8,128)S(1)}, u32[]{:S(2)}, u32[]{:S(2)}) %collective-permute-start.5) | collective-permute-done | bytes 32800 | tf_op jit(solution)/shard_map/ppermute | solution.py:397
  32.7 5.3 %collective-permute-start.6 = (f32[64,128]{1,0:T(8,128)S(1)}, f32[64,128]{1,0:T(8,128)S(1)}, u32[]{:S(2)}, u32[]{:S(2)}) collective-permute-start(f32[64,128]{1,0:T(8,128)S(1)} %add.6), channel_id=1, source_target_pairs={{0,128},{64,192},{128,0},{192,64},{1,129},{65,193},{129,1},{193,65... | collective-permute-start | bytes 98312 | tf_op jit(solution)/shard_map/ppermute | solution.py:397
  38.0 1.4 %collective-permute-done.6 = f32[64,128]{1,0:T(8,128)S(1)} collective-permute-done((f32[64,128]{1,0:T(8,128)S(1)}, f32[64,128]{1,0:T(8,128)S(1)}, u32[]{:S(2)}, u32[]{:S(2)}) %collective-permute-start.6) | collective-permute-done | bytes 32800 | tf_op jit(solution)/shard_map/ppermute | solution.py:397
  39.4 1.3 %collective-permute-start.7 = (f32[64,128]{1,0:T(8,128)S(1)}, f32[64,128]{1,0:T(8,128)S(1)}, u32[]{:S(2)}, u32[]{:S(2)}) collective-permute-start(f32[64,128]{1,0:T(8,128)S(1)} %add.7.grad_ref), channel_id=1, source_target_pairs={{0,1},{1,2},{2,3},{3,4},{4,5},{5,6},{6,7},{7,8},{8,9},{9,10},{10,1... | collective-permute-start | bytes 98312 | tf_op jit(solution)/shard_map/ppermute | solution.py:393
  40.7 1.5 %owned_gradient.1 = (f32[512,512]{1,0:T(8,128)}, f32[128,512]{1,0:T(8,128)S(1)}, f32[128,512]{1,0:T(8,128)S(1)}) custom-call(f32[64,128]{1,0:T(8,128)S(1)} %add.7.grad_ref, f32[512,512]{1,0:T(8,128)S(1)} %copy-done, bf16[512,128]{1,0:T(8,128)(2,1)S(1)} %copy-done.5, bf16[128,512]{1,0:T(8,128)(2,1)S(1)} %copy-done.4), custom_call_target="tpu_custom_call" | custom-call | tf_op jit(solution)/shard_map/owned_gradient/pallas_call | solution.py:334
  42.2 1.8 %collective-permute-done.7.near_ref = f32[64,128]{1,0:T(8,128)S(1)} collective-permute-done((f32[64,128]{1,0:T(8,128)S(1)}, f32[64,128]{1,0:T(8,128)S(1)}, u32[]{:S(2)}, u32[]{:S(2)}) %collective-permute-start.7) | collective-permute-done | bytes 32800 | tf_op jit(solution)/shard_map/ppermute | solution.py:393
  44.1 1.9 %collective-permute-start.8 = (f32[64,128]{1,0:T(8,128)S(1)}, f32[64,128]{1,0:T(8,128)S(1)}, u32[]{:S(2)}, u32[]{:S(2)}) collective-permute-start(f32[64,128]{1,0:T(8,128)S(1)} %collective-permute-done.7.near_ref), channel_id=1, source_target_pairs={{0,64},{64,0},{128,192},{192,128},{1,65},{65,1},{129,193},{193,129... | collective-permute-start | bytes 98312 | tf_op jit(solution)/shard_map/ppermute | solution.py:397
  46.0 15.9 %all_to_all.10.rows_ref = f32[16,1,128]{2,1,0:T(1,128)S(1)} all-to-all(f32[16,1,128]{2,1,0:T(1,128)S(1)} %get-tuple-element.32), channel_id=1, replica_groups=mesh['src'=4,'plane'=4,'spot'=16] {'spot'}, dimensions={0} | all-to-all | bytes 16384 | tf_op jit(solution)/shard_map/all_to_all | solution.py:418
  61.9 20.2 %all_to_all.11.sums_ref = f32[16,1,128]{2,1,0:T(1,128)S(1)} all-to-all(f32[16,1,128]{2,1,0:T(1,128)S(1)} %regroup.1), channel_id=1, replica_groups=mesh['src'=4,'plane'=4,'spot'=16] {'src','plane'}, dimensions={0} | all-to-all | bytes 16384 | tf_op jit(solution)/shard_map/all_to_all | solution.py:423
  82.0 1.6 %last_steps.1 = (f32[512,512]{1,0:T(8,128)}, f32[1,16]{1,0:T(1,128)}, f32[1,1]{1,0:T(1,128)}) custom-call(s32[1]{0:T(128)} %bitcast.group_ref, f32[64,128]{1,0:T(8,128)S(1)} %collective-permute-done.7.near_ref, f32[64,128]{1,0:T(8,128)S(1)} %collective-permute-done.8.other_ref, ...), custom_call_target="tpu_custom_call", output_to_operand_aliasing={{0}: (9, {})} | custom-call | tf_op jit(solution)/shard_map/last_steps/pallas_call | solution.py:375
  (20 shorter events, 0.1 us)
Async XLA Ops:
  0.6 11.1 %copy-start = (f32[512,512]{1,0:T(8,128)S(1)}, f32[512,512]{1,0:T(8,128)}, u32[]{:S(2)}) copy-start(f32[512,512]{1,0:T(8,128)} %logits_ref.5) | copy-start | bytes 3145732
  0.6 11.0 %copy-start.3 = (bf16[512,128]{1,0:T(8,128)(2,1)S(1)}, bf16[512,128]{1,0:T(8,128)(2,1)}, u32[]{:S(2)}) copy-start(bf16[512,128]{1,0:T(8,128)(2,1)} %constant.16.clone.table_ref) | copy-start | bytes 393220
  2.5 1.3 %copy-start.7 = (f32[3,16]{1,0:T(4,128)S(1)}, f32[3,16]{1,0:T(4,128)}, u32[]{:S(2)}) copy-start(f32[3,16]{1,0:T(4,128)} %get-tuple-element.20.own_scalars.packed_ref) | copy-start | bytes 580
  2.5 10.9 %collective-permute-start.1 = (bf16[64,128]{1,0:T(8,128)(2,1)}, bf16[64,128]{1,0:T(8,128)(2,1)S(1)}, u32[]{:S(2)}, u32[]{:S(2)}) collective-permute-start(bf16[64,128]{1,0:T(8,128)(2,1)} %get-tuple-element.21), channel_id=1, source_target_pairs={{0,1},{1,2},{2,3},{3,4},{4,5},{5,6},{6,7},{7,8},{8,9},{9,10},{10,1... | collective-permute-start | bytes 49160 | tf_op jit(solution)/shard_map/ppermute | solution.py:393
  3.9 14.2 %copy-start.1 = (s32[512,512]{1,0:T(8,128)S(1)}, s32[512,512]{1,0:T(8,128)}, u32[]{:S(2)}) copy-start(s32[512,512]{1,0:T(8,128)} %target_ref.1) | copy-start | bytes 3145732
  3.9 9.6 %collective-permute-start.2 = (f32[3,16]{1,0:T(4,128)S(1)}, f32[3,16]{1,0:T(4,128)S(1)}, u32[]{:S(2)}, u32[]{:S(2)}) collective-permute-start(f32[3,16]{1,0:T(4,128)S(1)} %copy-done.7), channel_id=1, source_target_pairs={{0,128},{64,192},{128,0},{192,64},{1,129},{65,193},{129,1},{193,65... | collective-permute-start | bytes 584 | tf_op jit(solution)/shard_map/ppermute | solution.py:397
  11.7 1.2 %copy-start.2 = (bf16[3712,128]{1,0:T(8,128)(2,1)S(1)}, bf16[3712,128]{1,0:T(8,128)(2,1)}, u32[]{:S(2)}) copy-start(bf16[3712,128]{1,0:T(8,128)(2,1)} %constant.17.clone.image_table_ref) | copy-start | bytes 2850820
  13.5 4.6 %collective-permute-start.4 = (bf16[64,128]{1,0:T(8,128)(2,1)S(1)}, bf16[64,128]{1,0:T(8,128)(2,1)S(1)}, u32[]{:S(2)}, u32[]{:S(2)}) collective-permute-start(bf16[64,128]{1,0:T(8,128)(2,1)S(1)} %collective-permute-done.1.near_ref), channel_id=1, source_target_pairs={{0,64},{64,0},{128,192},{192,128},{1,65},{65,1},{129,193},{193,129... | collective-permute-start | bytes 49160 | tf_op jit(solution)/shard_map/ppermute | solution.py:397
  16.7 1.2 %collective-permute-start = (f32[3,16]{1,0:T(4,128)S(1)}, f32[3,16]{1,0:T(4,128)S(1)}, u32[]{:S(2)}, u32[]{:S(2)}) collective-permute-start(f32[3,16]{1,0:T(4,128)S(1)} %copy-done.7), channel_id=1, source_target_pairs={{0,64},{64,0},{128,192},{192,128},{1,65},{65,1},{129,193},{193,129... | collective-permute-start | bytes 584 | tf_op jit(solution)/shard_map/ppermute | solution.py:397
  16.8 1.2 %collective-permute-start.3 = (f32[3,16]{1,0:T(4,128)S(1)}, f32[3,16]{1,0:T(4,128)S(1)}, u32[]{:S(2)}, u32[]{:S(2)}) collective-permute-start(f32[3,16]{1,0:T(4,128)S(1)} %collective-permute-done.2.scalars_2), channel_id=1, source_target_pairs={{0,64},{64,0},{128,192},{192,128},{1,65},{65,1},{129,193},{193,129... | collective-permute-start | bytes 584 | tf_op jit(solution)/shard_map/ppermute | solution.py:397
  18.1 22.7 %copy-start.5 = (bf16[512,128]{1,0:T(8,128)(2,1)S(1)}, bf16[512,128]{1,0:T(8,128)(2,1)}, u32[]{:S(2)}) copy-start(bf16[512,128]{1,0:T(8,128)(2,1)} %constant.18.clone.row_ref) | copy-start | bytes 393220
  31.4 9.3 %copy-start.4 = (bf16[128,512]{1,0:T(8,128)(2,1)S(1)}, bf16[128,512]{1,0:T(8,128)(2,1)}, u32[]{:S(2)}) copy-start(bf16[128,512]{1,0:T(8,128)(2,1)} %constant.19.clone.column_ref) | copy-start | bytes 393220
  31.4 1.3 %collective-permute-start.5 = (f32[64,128]{1,0:T(8,128)S(1)}, f32[64,128]{1,0:T(8,128)S(1)}, u32[]{:S(2)}, u32[]{:S(2)}) collective-permute-start(f32[64,128]{1,0:T(8,128)S(1)} %get-tuple-element.27), channel_id=1, source_target_pairs={{0,64},{64,0},{128,192},{192,128},{1,65},{65,1},{129,193},{193,129... | collective-permute-start | bytes 98312 | tf_op jit(solution)/shard_map/ppermute | solution.py:397
  32.7 6.7 %collective-permute-start.6 = (f32[64,128]{1,0:T(8,128)S(1)}, f32[64,128]{1,0:T(8,128)S(1)}, u32[]{:S(2)}, u32[]{:S(2)}) collective-permute-start(f32[64,128]{1,0:T(8,128)S(1)} %add.6), channel_id=1, source_target_pairs={{0,128},{64,192},{128,0},{192,64},{1,129},{65,193},{129,1},{193,65... | collective-permute-start | bytes 98312 | tf_op jit(solution)/shard_map/ppermute | solution.py:397
  39.4 4.6 %collective-permute-start.7 = (f32[64,128]{1,0:T(8,128)S(1)}, f32[64,128]{1,0:T(8,128)S(1)}, u32[]{:S(2)}, u32[]{:S(2)}) collective-permute-start(f32[64,128]{1,0:T(8,128)S(1)} %add.7.grad_ref), channel_id=1, source_target_pairs={{0,1},{1,2},{2,3},{3,4},{4,5},{5,6},{6,7},{7,8},{8,9},{9,10},{10,1... | collective-permute-start | bytes 98312 | tf_op jit(solution)/shard_map/ppermute | solution.py:393
  42.2 39.8 %copy-start.6 = (bf16[128,128]{1,0:T(8,128)(2,1)S(1)}, bf16[128,128]{1,0:T(8,128)(2,1)}, u32[]{:S(2)}) copy-start(bf16[128,128]{1,0:T(8,128)(2,1)} %constant.20.clone.row_ref) | copy-start | bytes 98308
  44.1 38.0 %collective-permute-start.8 = (f32[64,128]{1,0:T(8,128)S(1)}, f32[64,128]{1,0:T(8,128)S(1)}, u32[]{:S(2)}, u32[]{:S(2)}) collective-permute-start(f32[64,128]{1,0:T(8,128)S(1)} %collective-permute-done.7.near_ref), channel_id=1, source_target_pairs={{0,64},{64,0},{128,192},{192,128},{1,65},{65,1},{129,193},{193,129... | collective-permute-start | bytes 98312 | tf_op jit(solution)/shard_map/ppermute | solution.py:397

commit v8 on v5

--- a/solution.py
+++ b/solution.py
@@ -7,6 +7,7 @@
 from jax.experimental import pallas as pl
 from jax.experimental.pallas import tpu as pltpu
 from jax.sharding import PartitionSpec as P
+
 
 FREQS = 64
 RADIUS = 20
@@ -21,7 +22,7 @@
 MIB = 1024 * 1024
 STEEPNESS = 12.0
 THRESHOLD = 0.2
-STEP = 16
+STEP = 32
 F32 = jnp.float32
 BF16 = jnp.bfloat16
 
@@ -135,6 +136,7 @@
 def image_kernel(group_ref, own_scalars, scalars_1, scalars_2, scalars_3, own_ref, near_ref, other_ref, target_ref, table_ref, out_ref,
                  fields_ref, row_field_ref, intensity_ref, cotangent_ref, spectra_ref, terms_ref, grad_ref, rounded_ref, frame_ref):
     scalars = [own_scalars, scalars_1, scalars_2, scalars_3]
+
     def beside(start, count):
         return jnp.concatenate([table_ref[start + 128 * i:start + 128 * (i + 1), :] for i in range(count)], 1)
 
@@ -409,12 +411,18 @@
     return from_group(x, 2)
 
 
+def from_group_nearby(x):
+    peers = lax.axis_size("tile")
+    pairs = [(s * peers + i, (s ^ 2) * peers + (i ^ 8)) for s in range(GROUPS) for i in range(peers)]
+    return lax.ppermute(x, ("src", "tile"), pairs)
+
+
 def on_device(mask_logits, target, weights, shifts):
     peers = lax.axis_size("tile")
     group = lax.axis_index("src").astype(jnp.int32).reshape(1)
     edge, packed = edge_spectrum(group, mask_logits, weights, shifts)
+    packed_far = from_group_nearby(packed)
     near = from_tile_beside(edge)
-    packed_far = from_chip(packed)
     packed_core = from_core(packed)
     own, table = column_spectrum(mask_logits)
     near, packed_far, own = lax.optimization_barrier((near, packed_far, own))
@@ -422,8 +430,8 @@
     partial = image(group, scalars, own, near, from_core(near), target, table)
     chip = partial + from_core(partial)
     spectrum_grad, sums = total(chip, from_chip(chip), peers)
+    sums = lax.all_to_all(sums, "tile", 0, 0, tiled=True)
     near_grad = from_tile_beside(spectrum_grad)
-    sums = lax.all_to_all(sums, "tile", 0, 0, tiled=True)
     grad, edges, slope = owned_gradient(spectrum_grad, mask_logits)
     near_grad, edges = lax.optimization_barrier((near_grad, edges))
     mask_grad, weight_grad, loss = last_steps(

time: 67 us -> 65.4 us (0.976)
  starting transfers between devices: 30.5 us -> 29.5 us
    ppermute x7 -> x6, starting transfers between devices: 14.3 us -> 6.42 us  [from_group(): return lax.ppermute(x, 'src', [(i, i ^ d) for i in range(GROUPS)])]
    ppermute x0 -> x1, starting transfers between devices: none -> 6.38 us  [from_group_nearby(): return lax.ppermute(x, ('src', 'tile'), pairs)]
    ppermute x7 -> x6, waiting for transfers between devices: 7.14 us -> 6.4 us  [from_group(): return lax.ppermute(x, 'src', [(i, i ^ d) for i in range(GROUPS)])]
  transfers between devices with their start and end apart: 10 -> 10, of which waited for: 5 -> 6; matrix products, arithmetic and copies ran while one was open for 0% -> 0% of each run, Pallas kernels for 3% -> 3%
where the time goes in v8:
time: 65.4 us; the launch traced here: 65.1 us
  starting transfers between devices  29.5 us (45%)
  Pallas kernels  19.2 us (29%)
  waiting for transfers between devices  14.4 us (22%)
  local copies, waits for them, and re-layouts  1.23 us (2%)
  between operations  0.77 us (1%)
    pallas_call x1, Pallas kernels, image(): pl.pallas_call(image_kernel, grid_spec=pltpu.PrefetchScalarGridSpec(num_s...  13 us
    all_to_all x1, starting transfers between devices, on_device(): sums = lax.all_to_all(sums, 'tile', 0, 0, tiled=True)  11.3 us
    all_to_all x1, waiting for transfers between devices, on_device(): sums = lax.all_to_all(sums, 'tile', 0, 0, tiled=True)  7.61 us
    ppermute x6, starting transfers between devices, from_group(): return lax.ppermute(x, 'src', [(i, i ^ d) for i in range(GROUPS)])  6.42 us
    ppermute x6, waiting for transfers between devices, from_group(): return lax.ppermute(x, 'src', [(i, i ^ d) for i in range(GROUPS)])  6.4 us
    ppermute x1, starting transfers between devices, from_group_nearby(): return lax.ppermute(x, ('src', 'tile'), pairs)  6.38 us
    ppermute x2, starting transfers between devices, from_tile_beside(): return lax.ppermute(x, ('src', 'tile'), pairs)  5.39 us
    pallas_call x1, Pallas kernels, edge_spectrum(): pl.pallas_call(edge_kernel, in_specs=[pl.BlockSpec(memory_space=pltpu.SME...  1.87 us
  transfers between devices with their start and end apart: 10, of which 6 were waited for; matrix products, arithmetic and copies ran while one was open for 0% of the time, Pallas kernels for 3%

profile of v8, /device:TPU:2, one launch (start us, length us, event | category | flops | bytes accessed | tf_op | source)
XLA Modules:
  0.0 65.1 jit_solution(13350925862563120456)
XLA Ops:
  0.6 0.0 copy-start.3
  0.7 1.9 %edge_spectrum.1 = (bf16[64,128]{1,0:T(8,128)(2,1)}, f32[3,16]{1,0:T(4,128)}) custom-call(s32[1]{0:T(128)} %bitcast.group_ref, f32[512,512]{1,0:T(8,128)} %logits_ref.5, bf16[512,128]{1,0:T(8,128)(2,1)} %constant.16.clone.table_ref, f32[1,16]{1,0:T(1,128)} %bitcast.6, s32[2,16]{1,0:T(2,128)} %bitcast.5), custom_call_target="tpu_custom_call" | custom-call | tf_op jit(solution)/shard_map/edge_spectrum/pallas_call | solution.py:95
  2.5 3.5 %collective-permute-start.1 = (bf16[64,128]{1,0:T(8,128)(2,1)}, bf16[64,128]{1,0:T(8,128)(2,1)S(1)}, u32[]{:S(2)}, u32[]{:S(2)}) collective-permute-start(bf16[64,128]{1,0:T(8,128)(2,1)} %get-tuple-element.21), channel_id=1, source_target_pairs={{0,1},{1,2},{2,3},{3,4},{4,5},{5,6},{6,7},{7,8},{8,9},{9,10},{10,1... | collective-permute-start | bytes 49160 | tf_op jit(solution)/shard_map/ppermute | solution.py:399
  6.1 6.4 %collective-permute-start.2 = (f32[3,16]{1,0:T(4,128)S(1)}, f32[3,16]{1,0:T(4,128)S(1)}, u32[]{:S(2)}, u32[]{:S(2)}) collective-permute-start(f32[3,16]{1,0:T(4,128)S(1)} %copy-done.7), channel_id=1, source_target_pairs={{0,136},{1,137},{2,138},{3,139},{4,140},{5,141},{6,142},{7,143},{8... | collective-permute-start | bytes 584 | tf_op jit(solution)/shard_map/ppermute | solution.py:417
  12.5 1.2 %copy-done.2 = bf16[3712,128]{1,0:T(8,128)(2,1)S(1)} copy-done((bf16[3712,128]{1,0:T(8,128)(2,1)S(1)}, bf16[3712,128]{1,0:T(8,128)(2,1)}, u32[]{:S(2)}) %copy-start.2) | copy-done | bytes 950296
  13.6 0.6 column_spectrum.1
  14.2 0.4 collective-permute-done.1.near_ref
  14.7 2.3 %collective-permute-start.4 = (bf16[64,128]{1,0:T(8,128)(2,1)S(1)}, bf16[64,128]{1,0:T(8,128)(2,1)S(1)}, u32[]{:S(2)}, u32[]{:S(2)}) collective-permute-start(bf16[64,128]{1,0:T(8,128)(2,1)S(1)} %collective-permute-done.1.near_ref), channel_id=1, source_target_pairs={{0,64},{64,0},{128,192},{192,128},{1,65},{65,1},{129,193},{193,129... | collective-permute-start | bytes 49160 | tf_op jit(solution)/shard_map/ppermute | solution.py:403
  17.0 0.5 collective-permute-start.3
  17.5 0.7 %collective-permute-done.scalars_1 = f32[3,16]{1,0:T(4,128)S(1)} collective-permute-done((f32[3,16]{1,0:T(4,128)S(1)}, f32[3,16]{1,0:T(4,128)S(1)}, u32[]{:S(2)}, u32[]{:S(2)}) %collective-permute-start) | collective-permute-done | bytes 224 | tf_op jit(solution)/shard_map/ppermute | solution.py:403
  18.1 0.2 collective-permute-done.3.scalars_3
  18.3 13.0 %image.1 = f32[72,128]{1,0:T(8,128)S(1)} custom-call(s32[1]{0:T(128)} %bitcast.group_ref, f32[3,16]{1,0:T(4,128)S(1)} %copy-done.7, f32[3,16]{1,0:T(4,128)S(1)} %collective-permute-done.scalars_1, f32[3,16]{1,0:T(4,128)S(1)} %collective-permute-done.2.scalars_2, f32[3,16]{1,0:T(4,128)S(1)} %collective-permute-done.3.scalars_3, ...), custom_call_target="tpu_custom_call" | custom-call | tf_op jit(solution)/shard_map/image/pallas_call | solution.py:259
  31.3 0.0 copy-start.4
  31.3 0.4 collective-permute-start.5
  31.8 0.9 %collective-permute-done.5 = f32[72,128]{1,0:T(8,128)S(1)} collective-permute-done((f32[72,128]{1,0:T(8,128)S(1)}, f32[72,128]{1,0:T(8,128)S(1)}, u32[]{:S(2)}, u32[]{:S(2)}) %collective-permute-start.5) | collective-permute-done | bytes 36896 | tf_op jit(solution)/shard_map/ppermute | solution.py:403
  32.6 3.2 %collective-permute-start.6 = (f32[72,128]{1,0:T(8,128)S(1)}, f32[72,128]{1,0:T(8,128)S(1)}, u32[]{:S(2)}, u32[]{:S(2)}) collective-permute-start(f32[72,128]{1,0:T(8,128)S(1)} %add.3.chip_ref), channel_id=1, source_target_pairs={{0,128},{64,192},{128,0},{192,64},{1,129},{65,193},{129,1},{193,65... | collective-permute-start | bytes 110600 | tf_op jit(solution)/shard_map/ppermute | solution.py:403
  35.8 4.7 %collective-permute-done.6.far_ref = f32[72,128]{1,0:T(8,128)S(1)} collective-permute-done((f32[72,128]{1,0:T(8,128)S(1)}, f32[72,128]{1,0:T(8,128)S(1)}, u32[]{:S(2)}, u32[]{:S(2)}) %collective-permute-start.6) | collective-permute-done | bytes 36896 | tf_op jit(solution)/shard_map/ppermute | solution.py:403
  40.5 0.6 total.1
  41.1 1.9 %collective-permute-start.7 = (f32[64,128]{1,0:T(8,128)S(1)}, f32[64,128]{1,0:T(8,128)S(1)}, u32[]{:S(2)}, u32[]{:S(2)}) collective-permute-start(f32[64,128]{1,0:T(8,128)S(1)} %get-tuple-element.27.grad_ref), channel_id=1, source_target_pairs={{0,1},{1,2},{2,3},{3,4},{4,5},{5,6},{6,7},{7,8},{8,9},{9,10},{10,1... | collective-permute-start | bytes 98312 | tf_op jit(solution)/shard_map/ppermute | solution.py:399
  43.0 11.3 %all-to-all-start = ((f32[64,1,128]{2,1,0:T(1,128)}), f32[64,1,128]{2,1,0:T(1,128)S(1)}, u32[]{:S(2)}, u32[]{:S(2)}) async-start(f32[64,1,128]{2,1,0:T(1,128)} %get-tuple-element.32), calls=%async_computation | async-start | bytes 65536 | tf_op jit(solution)/shard_map/all_to_all | solution.py:433
  54.4 0.0 copy-start.6
  54.4 1.5 %owned_gradient.1 = (f32[512,512]{1,0:T(8,128)}, f32[128,512]{1,0:T(8,128)S(1)}, f32[128,512]{1,0:T(8,128)S(1)}) custom-call(f32[64,128]{1,0:T(8,128)S(1)} %get-tuple-element.27.grad_ref, f32[512,512]{1,0:T(8,128)S(1)} %copy-done, bf16[512,128]{1,0:T(8,128)(2,1)S(1)} %copy-done.5, bf16[128,512]{1,0:T(8,128)(2,1)S(1)} %copy-done.4), custom_call_target="tpu_custom_call" | custom-call | tf_op jit(solution)/shard_map/owned_gradient/pallas_call | solution.py:334
  55.9 7.6 %all-to-all-done.sums_ref = f32[64,1,128]{2,1,0:T(1,128)S(1)} async-done(((f32[64,1,128]{2,1,0:T(1,128)}), f32[64,1,128]{2,1,0:T(1,128)S(1)}, u32[]{:S(2)}, u32[]{:S(2)}) %all-to-all-start) | async-done | bytes 32800 | tf_op jit(solution)/shard_map/all_to_all | solution.py:433
  63.5 1.6 %last_steps.1 = (f32[512,512]{1,0:T(8,128)}, f32[1,16]{1,0:T(1,128)}, f32[1,1]{1,0:T(1,128)}) custom-call(s32[1]{0:T(128)} %bitcast.group_ref, f32[64,128]{1,0:T(8,128)S(1)} %collective-permute-done.7.near_ref, f32[64,128]{1,0:T(8,128)S(1)} %collective-permute-done.8.other_ref, ...), custom_call_target="tpu_custom_call", output_to_operand_aliasing={{0}: (9, {})} | custom-call | tf_op jit(solution)/shard_map/last_steps/pallas_call | solution.py:375
  (19 shorter events, 0.0 us)
Async XLA Ops:
  0.6 11.8 %copy-start = (f32[512,512]{1,0:T(8,128)S(1)}, f32[512,512]{1,0:T(8,128)}, u32[]{:S(2)}) copy-start(f32[512,512]{1,0:T(8,128)} %logits_ref.5) | copy-start | bytes 3145732
  0.6 11.8 %copy-start.3 = (bf16[512,128]{1,0:T(8,128)(2,1)S(1)}, bf16[512,128]{1,0:T(8,128)(2,1)}, u32[]{:S(2)}) copy-start(bf16[512,128]{1,0:T(8,128)(2,1)} %constant.16.clone.table_ref) | copy-start | bytes 393220
  2.5 3.5 %copy-start.7 = (f32[3,16]{1,0:T(4,128)S(1)}, f32[3,16]{1,0:T(4,128)}, u32[]{:S(2)}) copy-start(f32[3,16]{1,0:T(4,128)} %get-tuple-element.20.own_scalars.packed_ref) | copy-start | bytes 580
  2.5 12.1 %collective-permute-start.1 = (bf16[64,128]{1,0:T(8,128)(2,1)}, bf16[64,128]{1,0:T(8,128)(2,1)S(1)}, u32[]{:S(2)}, u32[]{:S(2)}) collective-permute-start(bf16[64,128]{1,0:T(8,128)(2,1)} %get-tuple-element.21), channel_id=1, source_target_pairs={{0,1},{1,2},{2,3},{3,4},{4,5},{5,6},{6,7},{7,8},{8,9},{9,10},{10,1... | collective-permute-start | bytes 49160 | tf_op jit(solution)/shard_map/ppermute | solution.py:399
  6.0 12.2 %copy-start.1 = (s32[512,512]{1,0:T(8,128)S(1)}, s32[512,512]{1,0:T(8,128)}, u32[]{:S(2)}) copy-start(s32[512,512]{1,0:T(8,128)} %target_ref.1) | copy-start | bytes 3145732
  6.1 8.2 %collective-permute-start.2 = (f32[3,16]{1,0:T(4,128)S(1)}, f32[3,16]{1,0:T(4,128)S(1)}, u32[]{:S(2)}, u32[]{:S(2)}) collective-permute-start(f32[3,16]{1,0:T(4,128)S(1)} %copy-done.7), channel_id=1, source_target_pairs={{0,136},{1,137},{2,138},{3,139},{4,140},{5,141},{6,142},{7,143},{8... | collective-permute-start | bytes 584 | tf_op jit(solution)/shard_map/ppermute | solution.py:417
  12.5 1.2 %copy-start.2 = (bf16[3712,128]{1,0:T(8,128)(2,1)S(1)}, bf16[3712,128]{1,0:T(8,128)(2,1)}, u32[]{:S(2)}) copy-start(bf16[3712,128]{1,0:T(8,128)(2,1)} %constant.17.clone.image_table_ref) | copy-start | bytes 2850820
  14.7 3.6 %collective-permute-start.4 = (bf16[64,128]{1,0:T(8,128)(2,1)S(1)}, bf16[64,128]{1,0:T(8,128)(2,1)S(1)}, u32[]{:S(2)}, u32[]{:S(2)}) collective-permute-start(bf16[64,128]{1,0:T(8,128)(2,1)S(1)} %collective-permute-done.1.near_ref), channel_id=1, source_target_pairs={{0,64},{64,0},{128,192},{192,128},{1,65},{65,1},{129,193},{193,129... | collective-permute-start | bytes 49160 | tf_op jit(solution)/shard_map/ppermute | solution.py:403
  17.0 1.2 %collective-permute-start = (f32[3,16]{1,0:T(4,128)S(1)}, f32[3,16]{1,0:T(4,128)S(1)}, u32[]{:S(2)}, u32[]{:S(2)}) collective-permute-start(f32[3,16]{1,0:T(4,128)S(1)} %copy-done.7), channel_id=1, source_target_pairs={{0,64},{64,0},{128,192},{192,128},{1,65},{65,1},{129,193},{193,129... | collective-permute-start | bytes 584 | tf_op jit(solution)/shard_map/ppermute | solution.py:403
  17.0 1.3 %collective-permute-start.3 = (f32[3,16]{1,0:T(4,128)S(1)}, f32[3,16]{1,0:T(4,128)S(1)}, u32[]{:S(2)}, u32[]{:S(2)}) collective-permute-start(f32[3,16]{1,0:T(4,128)S(1)} %collective-permute-done.2.scalars_2), channel_id=1, source_target_pairs={{0,64},{64,0},{128,192},{192,128},{1,65},{65,1},{129,193},{193,129... | collective-permute-start | bytes 584 | tf_op jit(solution)/shard_map/ppermute | solution.py:403
  18.3 36.1 %copy-start.5 = (bf16[512,128]{1,0:T(8,128)(2,1)S(1)}, bf16[512,128]{1,0:T(8,128)(2,1)}, u32[]{:S(2)}) copy-start(bf16[512,128]{1,0:T(8,128)(2,1)} %constant.18.clone.row_ref) | copy-start | bytes 393220
  31.3 23.1 %copy-start.4 = (bf16[128,512]{1,0:T(8,128)(2,1)S(1)}, bf16[128,512]{1,0:T(8,128)(2,1)}, u32[]{:S(2)}) copy-start(bf16[128,512]{1,0:T(8,128)(2,1)} %constant.19.clone.column_ref) | copy-start | bytes 393220
  31.3 1.3 %collective-permute-start.5 = (f32[72,128]{1,0:T(8,128)S(1)}, f32[72,128]{1,0:T(8,128)S(1)}, u32[]{:S(2)}, u32[]{:S(2)}) collective-permute-start(f32[72,128]{1,0:T(8,128)S(1)} %image.1), channel_id=1, source_target_pairs={{0,64},{64,0},{128,192},{192,128},{1,65},{65,1},{129,193},{193,129... | collective-permute-start | bytes 110600 | tf_op jit(solution)/shard_map/ppermute | solution.py:403
  32.6 7.9 %collective-permute-start.6 = (f32[72,128]{1,0:T(8,128)S(1)}, f32[72,128]{1,0:T(8,128)S(1)}, u32[]{:S(2)}, u32[]{:S(2)}) collective-permute-start(f32[72,128]{1,0:T(8,128)S(1)} %add.3.chip_ref), channel_id=1, source_target_pairs={{0,128},{64,192},{128,0},{192,64},{1,129},{65,193},{129,1},{193,65... | collective-permute-start | bytes 110600 | tf_op jit(solution)/shard_map/ppermute | solution.py:403
  41.1 14.8 %collective-permute-start.7 = (f32[64,128]{1,0:T(8,128)S(1)}, f32[64,128]{1,0:T(8,128)S(1)}, u32[]{:S(2)}, u32[]{:S(2)}) collective-permute-start(f32[64,128]{1,0:T(8,128)S(1)} %get-tuple-element.27.grad_ref), channel_id=1, source_target_pairs={{0,1},{1,2},{2,3},{3,4},{4,5},{5,6},{6,7},{7,8},{8,9},{9,10},{10,1... | collective-permute-start | bytes 98312 | tf_op jit(solution)/shard_map/ppermute | solution.py:399
  43.0 20.5 %all-to-all-start = ((f32[64,1,128]{2,1,0:T(1,128)}), f32[64,1,128]{2,1,0:T(1,128)S(1)}, u32[]{:S(2)}, u32[]{:S(2)}) async-start(f32[64,1,128]{2,1,0:T(1,128)} %get-tuple-element.32), calls=%async_computation | async-start | bytes 65536 | tf_op jit(solution)/shard_map/all_to_all | solution.py:433
  54.4 9.1 %copy-start.6 = (bf16[128,128]{1,0:T(8,128)(2,1)S(1)}, bf16[128,128]{1,0:T(8,128)(2,1)}, u32[]{:S(2)}) copy-start(bf16[128,128]{1,0:T(8,128)(2,1)} %constant.20.clone.row_ref) | copy-start | bytes 98308
  55.9 7.6 %collective-permute-start.8 = (f32[64,128]{1,0:T(8,128)S(1)}, f32[64,128]{1,0:T(8,128)S(1)}, u32[]{:S(2)}, u32[]{:S(2)}) collective-permute-start(f32[64,128]{1,0:T(8,128)S(1)} %collective-permute-done.7.near_ref), channel_id=1, source_target_pairs={{0,64},{64,0},{128,192},{192,128},{1,65},{65,1},{129,193},{193,129... | collective-permute-start | bytes 98312 | tf_op jit(solution)/shard_map/ppermute | solution.py:403
